TPU v7x, 1024 devices: a whole 8x8x8 slice. The times are simulated.
1024 devices in a mesh: section: 32 (over y, z_hi, core), blk: 8 (over x), head: 4 (over z_lo).
Axes of the slice: x: 8, y: 8, z: 8 (z_hi: 2, z_lo: 4; z = z_hi * 4 + z_lo), core: 2. Of those that a mesh axis runs over, the one named last changes fastest.
Arguments:
- queries: bfloat16 [32, 2048, 2048], P('section', ('blk', 'head')), may hold values from -24 to 24
- keys_values: bfloat16 [32, 2048, 1024], P('section', ('blk', 'head')), may hold values from -8 to 8
- segment_ids: int32 [32, 2048], P('section', ('blk', 'head')), may hold values from 0 to 3, never falling along the last dimension, each value on 1 to 1536 neighbouring positions
Outputs:
- attended: bfloat16 [32, 2048, 2048], P('section', ('blk', 'head'))
All inputs are finite; a program needn't handle non-finite values.
Results may differ from a plain program's by a relative error of at most 0.004.
Values may be sent and summed in bfloat16 or wider, within the bound.
No kernel may reach another device: no remote copies, remote signals or barrier semaphores. Data moves between devices by JAX's collectives and lax.ppermute only.
A program may use at most 32 MiB of HBM per device.

v0:
```python
import functools
import math

import jax
import jax.numpy as jnp
from jax import lax
from jax.experimental import pallas as pl
from jax.experimental.pallas import tpu as pltpu
from jax.sharding import PartitionSpec as P

HEAD_SIZE = 128
NEG_FILL = -1e30
LONGEST_SEGMENT = 1536
LABELS = 4
LABEL_ROWS = 8
NO_LABEL = 9.0


def prepare_kernel(place_ref, kv_ref, label_ref, q_ref, pair_ref, *rest, heads):
    q_refs, label_rows = rest[:-1], rest[-1]
    tokens = kv_ref.shape[0]
    kv_width = kv_ref.shape[1] // heads
    q_width = q_ref.shape[1] // heads
    label_rows[...] = jnp.full(label_rows.shape, NO_LABEL, jnp.float32)
    label_rows[0:1, 0:tokens] = label_ref[...].astype(jnp.float32)
    for which in range(heads):
        pair_ref[which, 0:tokens, :] = kv_ref[:, which * kv_width : (which + 1) * kv_width]
        pair_ref[which, tokens : tokens + LABEL_ROWS, :] = label_rows[...].astype(jnp.bfloat16)
    own = place_ref[1]
    for turn in range(heads):
        start = pl.multiple_of(lax.rem(own + turn, heads) * q_width, q_width)
        q_refs[turn][...] = q_ref[:, pl.ds(start, q_width)]


def attend_kernel(place_ref, *refs, heads, back, scale):
    q_refs = refs[:heads]
    pair_refs = refs[heads : heads + back + 1]
    out_refs = refs[heads + back + 1 : 2 * heads + back + 1]
    top_ref, total_ref, sum_ref = refs[2 * heads + back + 1 :]
    tokens = q_refs[0].shape[0]
    grouped = q_refs[0].shape[1] // HEAD_SIZE
    rows = tokens * heads
    block_index, own = place_ref[0], place_ref[1]
    first = block_index * rows
    base = jnp.maximum(block_index - back, 0) * rows

    counts = [jnp.zeros((LABEL_ROWS, HEAD_SIZE), jnp.float32) for _ in range(LABELS)]
    for distance in range(back + 1):
        valid = (block_index >= distance).astype(jnp.float32)
        for piece in range(heads):
            found = pair_refs[distance][piece, tokens : tokens + LABEL_ROWS, 0:HEAD_SIZE]
            found = found.astype(jnp.float32)
            for label in range(1, LABELS):
                counts[label] += jnp.where(found < label, valid, 0.0)
    begins = [base + jnp.sum(counts[label]).astype(jnp.int32) for label in range(1, LABELS)]

    def begin_of(position):
        found = jnp.full_like(position, base)
        for begin in begins:
            found = jnp.maximum(found, jnp.where(begin <= position, begin, base))
        return found

    earliest = base
    for begin in begins:
        earliest = jnp.maximum(earliest, jnp.where(begin <= first, begin, base))

    def keys_of(distance):
        return pair_refs[distance][:, 0:tokens, 0:HEAD_SIZE].reshape(rows, HEAD_SIZE)

    def values_of(distance):
        return pair_refs[distance][:, 0:tokens, HEAD_SIZE : 2 * HEAD_SIZE].reshape(rows, HEAD_SIZE)

    def queries_of(turn):
        return jnp.concatenate(
            [q_refs[turn][:, j * HEAD_SIZE : (j + 1) * HEAD_SIZE] for j in range(grouped)], axis=0
        )

    def positions_of(turn):
        chunk = lax.rem(own - turn + heads, heads)
        row = lax.broadcasted_iota(jnp.int32, (tokens, 1), 0)
        place = first + chunk * tokens + row
        return jnp.concatenate([place] * grouped, axis=0)

    def scores_of(turn, distance):
        scores = lax.dot_general(
            queries_of(turn),
            keys_of(distance),
            (((1,), (1,)), ((), ())),
            preferred_element_type=jnp.float32,
        )
        place = positions_of(turn)
        key_place = (block_index - distance) * rows + lax.broadcasted_iota(jnp.int32, (1, rows), 1)
        allowed = key_place >= begin_of(place)
        if distance == 0:
            allowed = allowed & (key_place <= place)
        return jnp.where(allowed, scores, NEG_FILL)

    def mixed_of(weights, distance):
        return jnp.dot(
            weights.astype(jnp.bfloat16), values_of(distance), preferred_element_type=jnp.float32
        )

    for turn in range(heads):
        scores = scores_of(turn, 0)
        top = jnp.max(scores, axis=1, keepdims=True)
        weights = jnp.exp2((scores - top) * scale)
        top_ref[turn] = top
        total_ref[turn] = jnp.sum(weights, axis=1, keepdims=True)
        sum_ref[turn] = mixed_of(weights, 0)

    for distance in range(1, back + 1):
        last = (block_index - distance) * rows + rows - 1

        @pl.when((block_index >= distance) & (last >= earliest))
        def _(distance=distance):
            for turn in range(heads):
                scores = scores_of(turn, distance)
                old = top_ref[turn]
                top = jnp.maximum(old, jnp.max(scores, axis=1, keepdims=True))
                weights = jnp.exp2((scores - top) * scale)
                factor = jnp.exp2((old - top) * scale)
                top_ref[turn] = top
                total_ref[turn] = total_ref[turn] * factor + jnp.sum(weights, axis=1, keepdims=True)
                sum_ref[turn] = sum_ref[turn] * factor + mixed_of(weights, distance)

    for turn in range(heads):
        normed = (sum_ref[turn] / total_ref[turn]).astype(jnp.bfloat16)
        for j in range(grouped):
            out_refs[turn][:, j * HEAD_SIZE : (j + 1) * HEAD_SIZE] = normed[
                j * tokens : (j + 1) * tokens
            ]


def assemble_kernel(place_ref, *refs, heads):
    pieces, out_ref = refs[:heads], refs[heads]
    width = pieces[0].shape[1]
    own = place_ref[1]
    for turn in range(heads):
        start = pl.multiple_of(lax.rem(own + turn, heads) * width, width)
        out_ref[:, pl.ds(start, width)] = pieces[turn][...]


def whole(count):
    return [pl.BlockSpec(memory_space=pltpu.VMEM)] * count


def place_spec():
    return pl.BlockSpec(memory_space=pltpu.SMEM)


def per_device(queries, keys_values, segment_ids):
    sections = lax.axis_size("section")
    blocks = lax.axis_size("blk")
    heads = lax.axis_size("head")
    tokens = queries.shape[1]
    rows = tokens * heads
    kv_width = keys_values.shape[2] // heads
    q_width = queries.shape[2] // heads
    back = min(blocks - 1, -(-LONGEST_SEGMENT // rows))
    place = jnp.stack([lax.axis_index("blk"), lax.axis_index("head")]).astype(jnp.int32)

    pair_shape = (heads, tokens + LABEL_ROWS, kv_width)
    prepared = pl.pallas_call(
        functools.partial(prepare_kernel, heads=heads),
        out_shape=[jax.ShapeDtypeStruct(pair_shape, jnp.bfloat16)]
        + [jax.ShapeDtypeStruct((tokens, q_width), jnp.bfloat16)] * heads,
        in_specs=[place_spec()] + whole(3),
        out_specs=whole(1 + heads),
        scratch_shapes=[pltpu.VMEM((LABEL_ROWS, kv_width), jnp.float32)],
        name="prepare",
    )(place, keys_values[0], segment_ids, queries[0])
    pairs, turned = prepared[0], prepared[1:]

    own_pairs = lax.all_to_all(pairs, "head", split_axis=0, concat_axis=0, tiled=True)
    earlier = [
        lax.ppermute(own_pairs, "blk", [(i, i + d) for i in range(blocks - d)])
        for d in range(1, back + 1)
    ]
    block_queries = [turned[0]] + [
        lax.ppermute(turned[t], "head", [(i, (i + t) % heads) for i in range(heads)])
        for t in range(1, heads)
    ]

    scale = math.log2(math.e) / math.sqrt(HEAD_SIZE)
    grouped = q_width // HEAD_SIZE
    attended = pl.pallas_call(
        functools.partial(attend_kernel, heads=heads, back=back, scale=scale),
        out_shape=[jax.ShapeDtypeStruct((tokens, q_width), jnp.bfloat16)] * heads,
        in_specs=[place_spec()] + whole(heads + 1 + back),
        out_specs=whole(heads),
        scratch_shapes=[
            pltpu.VMEM((heads, grouped * tokens, 1), jnp.float32),
            pltpu.VMEM((heads, grouped * tokens, 1), jnp.float32),
            pltpu.VMEM((heads, grouped * tokens, HEAD_SIZE), jnp.float32),
        ],
        compiler_params=pltpu.CompilerParams(vmem_limit_bytes=32 << 20),
        name="attend",
    )(place, *block_queries, own_pairs, *earlier)

    def index(section, block, head):
        return ((section % sections) * blocks + block) * heads + head % heads

    received = [
        lax.ppermute(
            attended[t],
            ("section", "blk", "head"),
            [
                (index(s, b, h), index(s + 1, b, h - t))
                for s in range(sections)
                for b in range(blocks)
                for h in range(heads)
            ],
        )
        for t in range(heads)
    ]
    result = pl.pallas_call(
        functools.partial(assemble_kernel, heads=heads),
        out_shape=jax.ShapeDtypeStruct(queries.shape[1:], jnp.bfloat16),
        in_specs=[place_spec()] + whole(heads),
        out_specs=pl.BlockSpec(memory_space=pltpu.VMEM),
        name="assemble",
    )(place, *received)
    return result[None]


def solution(mesh):
    return jax.shard_map(
        per_device,
        mesh=mesh,
        in_specs=(
            P("section", ("blk", "head"), None),
            P("section", ("blk", "head"), None),
            P("section", ("blk", "head")),
        ),
        out_specs=P("section", ("blk", "head"), None),
        check_vma=False,
    )
```

profile of v0, /device:TPU:200, one launch (start us, length us, event | category | flops | bytes accessed | tf_op | source)
XLA Modules:
  0.0 100.0 jit_solution(13353358080010685583)
XLA Ops:
  0.0 0.6 pad_add_fusion.place_ref
  0.6 1.8 %prepare.1 = (bf16[4,72,256]{2,1,0:T(8,128)(2,1)}, bf16[64,512]{1,0:T(8,128)(2,1)}, bf16[64,512]{1,0:T(8,128)(2,1)}, bf16[64,512]{1,0:T(8,128)(2,1)}, bf16[64,512]{1,0:T(8,128)(2,1)}) custom-call(s32[2]{0:T(128)} %pad_add_fusion.place_ref, bf16[64,1024]{1,0:T(8,128)(2,1)} %bitcast.6, s32[1,64]{1,0:T(1,128)} %label_ref.1, bf16[64,2048]{1,0:T(8,128)(2,1)} %bitcast.5), custom_call_target="tpu_custom_call" | custom-call | tf_op jit(solution)/shard_map/prepare/pallas_call | solution.py:163
  2.4 14.2 %all_to_all.5.refs_4_ = bf16[4,72,256]{2,1,0:T(8,128)(2,1)S(1)} all-to-all(bf16[4,72,256]{2,1,0:T(8,128)(2,1)} %get-tuple-element.18), channel_id=1, replica_groups=mesh['section'=32,'blk'=8,'head'=4] {'head'}, dimensions={0} | all-to-all | bytes 294912 | tf_op jit(solution)/shard_map/all_to_all | solution.py:174
  16.6 0.7 collective-permute-start.8
  17.2 2.4 %collective-permute-start = (bf16[64,512]{1,0:T(8,128)(2,1)S(1)}, bf16[64,512]{1,0:T(8,128)(2,1)S(1)}, u32[]{:S(2)}, u32[]{:S(2)}) collective-permute-start(bf16[64,512]{1,0:T(8,128)(2,1)S(1)} %copy-done.8), channel_id=1, source_target_pairs={{0,1},{1,2},{2,3},{3,0},{4,5},{5,6},{6,7},{7,4},{8,9},{9,10},{10,1... | collective-permute-start | bytes 196616 | tf_op jit(solution)/shard_map/ppermute | solution.py:180
  19.7 5.1 %collective-permute-start.1 = (bf16[64,512]{1,0:T(8,128)(2,1)S(1)}, bf16[64,512]{1,0:T(8,128)(2,1)S(1)}, u32[]{:S(2)}, u32[]{:S(2)}) collective-permute-start(bf16[64,512]{1,0:T(8,128)(2,1)S(1)} %copy-done.7), channel_id=1, source_target_pairs={{0,2},{1,3},{2,0},{3,1},{4,6},{5,7},{6,4},{7,5},{8,10},{9,11},{10,... | collective-permute-start | bytes 196616 | tf_op jit(solution)/shard_map/ppermute | solution.py:180
  24.8 1.9 %collective-permute-start.2 = (bf16[64,512]{1,0:T(8,128)(2,1)S(1)}, bf16[64,512]{1,0:T(8,128)(2,1)S(1)}, u32[]{:S(2)}, u32[]{:S(2)}) collective-permute-start(bf16[64,512]{1,0:T(8,128)(2,1)S(1)} %copy-done.6), channel_id=1, source_target_pairs={{0,3},{1,0},{2,1},{3,2},{4,7},{5,4},{6,5},{7,6},{8,11},{9,8},{10,9... | collective-permute-start | bytes 196616 | tf_op jit(solution)/shard_map/ppermute | solution.py:180
  26.8 0.7 collective-permute-start.7
  27.4 0.0 collective-permute-done.refs_1_
  27.5 1.3 %collective-permute-start.6 = (bf16[4,72,256]{2,1,0:T(8,128)(2,1)S(1)}, bf16[4,72,256]{2,1,0:T(8,128)(2,1)S(1)}, u32[]{:S(2)}, u32[]{:S(2)}) collective-permute-start(bf16[4,72,256]{2,1,0:T(8,128)(2,1)S(1)} %all_to_all.5.refs_4_), channel_id=1, source_target_pairs={{0,16},{4,20},{8,24},{12,28},{1,17},{5,21},{9,25},{13,29},{2,18},{... | collective-permute-start | bytes 442376 | tf_op jit(solution)/shard_map/ppermute | solution.py:176
  28.8 0.0 collective-permute-done.1.refs_2_
  28.8 3.8 %collective-permute-start.5 = (bf16[4,72,256]{2,1,0:T(8,128)(2,1)S(1)}, bf16[4,72,256]{2,1,0:T(8,128)(2,1)S(1)}, u32[]{:S(2)}, u32[]{:S(2)}) collective-permute-start(bf16[4,72,256]{2,1,0:T(8,128)(2,1)S(1)} %all_to_all.5.refs_4_), channel_id=1, source_target_pairs={{0,12},{4,16},{8,20},{12,24},{16,28},{1,13},{5,17},{9,21},{13,25},... | collective-permute-start | bytes 442376 | tf_op jit(solution)/shard_map/ppermute | solution.py:176
  32.6 0.0 collective-permute-done.2.refs_3_
  32.6 1.9 %collective-permute-start.4 = (bf16[4,72,256]{2,1,0:T(8,128)(2,1)S(1)}, bf16[4,72,256]{2,1,0:T(8,128)(2,1)S(1)}, u32[]{:S(2)}, u32[]{:S(2)}) collective-permute-start(bf16[4,72,256]{2,1,0:T(8,128)(2,1)S(1)} %all_to_all.5.refs_4_), channel_id=1, source_target_pairs={{0,8},{4,12},{8,16},{12,20},{16,24},{20,28},{1,9},{5,13},{9,17},{1... | collective-permute-start | bytes 442376 | tf_op jit(solution)/shard_map/ppermute | solution.py:176
  34.5 0.0 collective-permute-done.8.refs_10_
  34.5 2.1 %collective-permute-start.3 = (bf16[4,72,256]{2,1,0:T(8,128)(2,1)S(1)}, bf16[4,72,256]{2,1,0:T(8,128)(2,1)S(1)}, u32[]{:S(2)}, u32[]{:S(2)}) collective-permute-start(bf16[4,72,256]{2,1,0:T(8,128)(2,1)S(1)} %all_to_all.5.refs_4_), channel_id=1, source_target_pairs={{0,4},{4,8},{8,12},{12,16},{16,20},{20,24},{24,28},{1,5},{5,9},{9,... | collective-permute-start | bytes 442376 | tf_op jit(solution)/shard_map/ppermute | solution.py:176
  36.7 0.0 collective-permute-done.7.refs_9_
  36.7 3.1 %collective-permute-done.6.refs_8_ = bf16[4,72,256]{2,1,0:T(8,128)(2,1)S(1)} collective-permute-done((bf16[4,72,256]{2,1,0:T(8,128)(2,1)S(1)}, bf16[4,72,256]{2,1,0:T(8,128)(2,1)S(1)}, u32[]{:S(2)}, u32[]{:S(2)}) %collective-permute-start.6) | collective-permute-done | bytes 147488 | tf_op jit(solution)/shard_map/ppermute | solution.py:176
  39.7 8.5 %collective-permute-done.5.refs_7_ = bf16[4,72,256]{2,1,0:T(8,128)(2,1)S(1)} collective-permute-done((bf16[4,72,256]{2,1,0:T(8,128)(2,1)S(1)}, bf16[4,72,256]{2,1,0:T(8,128)(2,1)S(1)}, u32[]{:S(2)}, u32[]{:S(2)}) %collective-permute-start.5) | collective-permute-done | bytes 147488 | tf_op jit(solution)/shard_map/ppermute | solution.py:176
  48.2 7.9 %collective-permute-done.4.refs_6_ = bf16[4,72,256]{2,1,0:T(8,128)(2,1)S(1)} collective-permute-done((bf16[4,72,256]{2,1,0:T(8,128)(2,1)S(1)}, bf16[4,72,256]{2,1,0:T(8,128)(2,1)S(1)}, u32[]{:S(2)}, u32[]{:S(2)}) %collective-permute-start.4) | collective-permute-done | bytes 147488 | tf_op jit(solution)/shard_map/ppermute | solution.py:176
  56.1 2.5 %collective-permute-done.3.refs_5_ = bf16[4,72,256]{2,1,0:T(8,128)(2,1)S(1)} collective-permute-done((bf16[4,72,256]{2,1,0:T(8,128)(2,1)S(1)}, bf16[4,72,256]{2,1,0:T(8,128)(2,1)S(1)}, u32[]{:S(2)}, u32[]{:S(2)}) %collective-permute-start.3) | collective-permute-done | bytes 147488 | tf_op jit(solution)/shard_map/ppermute | solution.py:176
  58.6 6.6 %attend.1 = (bf16[64,512]{1,0:T(8,128)(2,1)S(1)}, bf16[64,512]{1,0:T(8,128)(2,1)S(1)}, bf16[64,512]{1,0:T(8,128)(2,1)S(1)}, bf16[64,512]{1,0:T(8,128)(2,1)S(1)}) custom-call(s32[2]{0:T(128)S(1)} %copy-done.1, bf16[64,512]{1,0:T(8,128)(2,1)S(1)} %copy-done, bf16[64,512]{1,0:T(8,128)(2,1)S(1)} %collective-permute-done.refs_1_, ...), custom_call_target="tpu_custom_call" | custom-call | tf_op jit(solution)/shard_map/attend/pallas_call | solution.py:186
  65.2 6.7 %collective-permute-start.9 = (bf16[64,512]{1,0:T(8,128)(2,1)S(1)}, bf16[64,512]{1,0:T(8,128)(2,1)S(1)}, u32[]{:S(2)}, u32[]{:S(2)}) collective-permute-start(bf16[64,512]{1,0:T(8,128)(2,1)S(1)} %get-tuple-element.19), channel_id=1, source_target_pairs={{0,32},{1,33},{2,34},{3,35},{4,36},{5,37},{6,38},{7,39},{8,40},{9,... | collective-permute-start | bytes 196616 | tf_op jit(solution)/shard_map/ppermute | solution.py:204
  71.9 10.7 %collective-permute-start.10 = (bf16[64,512]{1,0:T(8,128)(2,1)S(1)}, bf16[64,512]{1,0:T(8,128)(2,1)S(1)}, u32[]{:S(2)}, u32[]{:S(2)}) collective-permute-start(bf16[64,512]{1,0:T(8,128)(2,1)S(1)} %get-tuple-element.20), channel_id=1, source_target_pairs={{0,35},{1,32},{2,33},{3,34},{4,39},{5,36},{6,37},{7,38},{8,43},{9,... | collective-permute-start | bytes 196616 | tf_op jit(solution)/shard_map/ppermute | solution.py:204
  82.7 4.4 %collective-permute-start.11 = (bf16[64,512]{1,0:T(8,128)(2,1)S(1)}, bf16[64,512]{1,0:T(8,128)(2,1)S(1)}, u32[]{:S(2)}, u32[]{:S(2)}) collective-permute-start(bf16[64,512]{1,0:T(8,128)(2,1)S(1)} %get-tuple-element.21), channel_id=1, source_target_pairs={{0,34},{1,35},{2,32},{3,33},{4,38},{5,39},{6,36},{7,37},{8,42},{9,... | collective-permute-start | bytes 196616 | tf_op jit(solution)/shard_map/ppermute | solution.py:204
  87.0 1.9 %collective-permute-start.12 = (bf16[64,512]{1,0:T(8,128)(2,1)S(1)}, bf16[64,512]{1,0:T(8,128)(2,1)S(1)}, u32[]{:S(2)}, u32[]{:S(2)}) collective-permute-start(bf16[64,512]{1,0:T(8,128)(2,1)S(1)} %get-tuple-element.22), channel_id=1, source_target_pairs={{0,33},{1,34},{2,35},{3,32},{4,37},{5,38},{6,39},{7,36},{8,41},{9,... | collective-permute-start | bytes 196616 | tf_op jit(solution)/shard_map/ppermute | solution.py:204
  89.0 0.0 collective-permute-done.9.refs_0_
  89.0 0.0 collective-permute-done.10.refs_1_
  89.0 4.0 %collective-permute-done.11.refs_2_ = bf16[64,512]{1,0:T(8,128)(2,1)S(1)} collective-permute-done((bf16[64,512]{1,0:T(8,128)(2,1)S(1)}, bf16[64,512]{1,0:T(8,128)(2,1)S(1)}, u32[]{:S(2)}, u32[]{:S(2)}) %collective-permute-start.11) | collective-permute-done | bytes 65568 | tf_op jit(solution)/shard_map/ppermute | solution.py:204
  93.0 4.8 %collective-permute-done.12.refs_3_ = bf16[64,512]{1,0:T(8,128)(2,1)S(1)} collective-permute-done((bf16[64,512]{1,0:T(8,128)(2,1)S(1)}, bf16[64,512]{1,0:T(8,128)(2,1)S(1)}, u32[]{:S(2)}, u32[]{:S(2)}) %collective-permute-start.12) | collective-permute-done | bytes 65568 | tf_op jit(solution)/shard_map/ppermute | solution.py:204
  97.8 0.6 copy-done.5
  98.4 1.7 %assemble.1 = bf16[64,2048]{1,0:T(8,128)(2,1)} custom-call(s32[2]{0:T(128)} %pad_add_fusion.place_ref, bf16[64,512]{1,0:T(8,128)(2,1)} %copy-done.2, bf16[64,512]{1,0:T(8,128)(2,1)} %copy-done.3, bf16[64,512]{1,0:T(8,128)(2,1)} %copy-done.4, bf16[64,512]{1,0:T(8,128)(2,1)} %copy-done.5), custom_call_target="tpu_custom_call" | custom-call | tf_op jit(solution)/shard_map/assemble/pallas_call | solution.py:216
  (17 shorter events, 0.0 us)
Async XLA Ops:
  2.4 14.9 %copy-start.8 = (bf16[64,512]{1,0:T(8,128)(2,1)S(1)}, bf16[64,512]{1,0:T(8,128)(2,1)}, u32[]{:S(2)}) copy-start(bf16[64,512]{1,0:T(8,128)(2,1)} %get-tuple-element.15) | copy-start | bytes 196612
  2.4 17.3 %copy-start.7 = (bf16[64,512]{1,0:T(8,128)(2,1)S(1)}, bf16[64,512]{1,0:T(8,128)(2,1)}, u32[]{:S(2)}) copy-start(bf16[64,512]{1,0:T(8,128)(2,1)} %get-tuple-element.16) | copy-start | bytes 196612
  2.4 22.4 %copy-start.6 = (bf16[64,512]{1,0:T(8,128)(2,1)S(1)}, bf16[64,512]{1,0:T(8,128)(2,1)}, u32[]{:S(2)}) copy-start(bf16[64,512]{1,0:T(8,128)(2,1)} %get-tuple-element.17) | copy-start | bytes 196612
  2.4 56.2 %copy-start = (bf16[64,512]{1,0:T(8,128)(2,1)S(1)}, bf16[64,512]{1,0:T(8,128)(2,1)}, u32[]{:S(2)}) copy-start(bf16[64,512]{1,0:T(8,128)(2,1)} %get-tuple-element.14.refs_0_) | copy-start | bytes 196612
  16.6 18.0 %collective-permute-start.8 = (bf16[4,72,256]{2,1,0:T(8,128)(2,1)S(1)}, bf16[4,72,256]{2,1,0:T(8,128)(2,1)S(1)}, u32[]{:S(2)}, u32[]{:S(2)}) collective-permute-start(bf16[4,72,256]{2,1,0:T(8,128)(2,1)S(1)} %all_to_all.5.refs_4_), channel_id=1, source_target_pairs={{0,24},{4,28},{1,25},{5,29},{2,26},{6,30},{3,27},{7,31},{32,56},{3... | collective-permute-start | bytes 442376 | tf_op jit(solution)/shard_map/ppermute | solution.py:176
  17.2 10.2 %collective-permute-start = (bf16[64,512]{1,0:T(8,128)(2,1)S(1)}, bf16[64,512]{1,0:T(8,128)(2,1)S(1)}, u32[]{:S(2)}, u32[]{:S(2)}) collective-permute-start(bf16[64,512]{1,0:T(8,128)(2,1)S(1)} %copy-done.8), channel_id=1, source_target_pairs={{0,1},{1,2},{2,3},{3,0},{4,5},{5,6},{6,7},{7,4},{8,9},{9,10},{10,1... | collective-permute-start | bytes 196616 | tf_op jit(solution)/shard_map/ppermute | solution.py:180
  19.7 9.1 %collective-permute-start.1 = (bf16[64,512]{1,0:T(8,128)(2,1)S(1)}, bf16[64,512]{1,0:T(8,128)(2,1)S(1)}, u32[]{:S(2)}, u32[]{:S(2)}) collective-permute-start(bf16[64,512]{1,0:T(8,128)(2,1)S(1)} %copy-done.7), channel_id=1, source_target_pairs={{0,2},{1,3},{2,0},{3,1},{4,6},{5,7},{6,4},{7,5},{8,10},{9,11},{10,... | collective-permute-start | bytes 196616 | tf_op jit(solution)/shard_map/ppermute | solution.py:180
  24.8 33.8 %copy-start.1 = (s32[2]{0:T(128)S(1)}, s32[2]{0:T(128)}, u32[]{:S(2)}) copy-start(s32[2]{0:T(128)} %pad_add_fusion.place_ref) | copy-start | bytes 28
  24.8 7.7 %collective-permute-start.2 = (bf16[64,512]{1,0:T(8,128)(2,1)S(1)}, bf16[64,512]{1,0:T(8,128)(2,1)S(1)}, u32[]{:S(2)}, u32[]{:S(2)}) collective-permute-start(bf16[64,512]{1,0:T(8,128)(2,1)S(1)} %copy-done.6), channel_id=1, source_target_pairs={{0,3},{1,0},{2,1},{3,2},{4,7},{5,4},{6,5},{7,6},{8,11},{9,8},{10,9... | collective-permute-start | bytes 196616 | tf_op jit(solution)/shard_map/ppermute | solution.py:180
  26.8 9.9 %collective-permute-start.7 = (bf16[4,72,256]{2,1,0:T(8,128)(2,1)S(1)}, bf16[4,72,256]{2,1,0:T(8,128)(2,1)S(1)}, u32[]{:S(2)}, u32[]{:S(2)}) collective-permute-start(bf16[4,72,256]{2,1,0:T(8,128)(2,1)S(1)} %all_to_all.5.refs_4_), channel_id=1, source_target_pairs={{0,20},{4,24},{8,28},{1,21},{5,25},{9,29},{2,22},{6,26},{10,30},{3... | collective-permute-start | bytes 442376 | tf_op jit(solution)/shard_map/ppermute | solution.py:176
  27.5 12.3 %collective-permute-start.6 = (bf16[4,72,256]{2,1,0:T(8,128)(2,1)S(1)}, bf16[4,72,256]{2,1,0:T(8,128)(2,1)S(1)}, u32[]{:S(2)}, u32[]{:S(2)}) collective-permute-start(bf16[4,72,256]{2,1,0:T(8,128)(2,1)S(1)} %all_to_all.5.refs_4_), channel_id=1, source_target_pairs={{0,16},{4,20},{8,24},{12,28},{1,17},{5,21},{9,25},{13,29},{2,18},{... | collective-permute-start | bytes 442376 | tf_op jit(solution)/shard_map/ppermute | solution.py:176
  28.8 19.5 %collective-permute-start.5 = (bf16[4,72,256]{2,1,0:T(8,128)(2,1)S(1)}, bf16[4,72,256]{2,1,0:T(8,128)(2,1)S(1)}, u32[]{:S(2)}, u32[]{:S(2)}) collective-permute-start(bf16[4,72,256]{2,1,0:T(8,128)(2,1)S(1)} %all_to_all.5.refs_4_), channel_id=1, source_target_pairs={{0,12},{4,16},{8,20},{12,24},{16,28},{1,13},{5,17},{9,21},{13,25},... | collective-permute-start | bytes 442376 | tf_op jit(solution)/shard_map/ppermute | solution.py:176
  32.6 23.5 %collective-permute-start.4 = (bf16[4,72,256]{2,1,0:T(8,128)(2,1)S(1)}, bf16[4,72,256]{2,1,0:T(8,128)(2,1)S(1)}, u32[]{:S(2)}, u32[]{:S(2)}) collective-permute-start(bf16[4,72,256]{2,1,0:T(8,128)(2,1)S(1)} %all_to_all.5.refs_4_), channel_id=1, source_target_pairs={{0,8},{4,12},{8,16},{12,20},{16,24},{20,28},{1,9},{5,13},{9,17},{1... | collective-permute-start | bytes 442376 | tf_op jit(solution)/shard_map/ppermute | solution.py:176
  34.5 24.1 %collective-permute-start.3 = (bf16[4,72,256]{2,1,0:T(8,128)(2,1)S(1)}, bf16[4,72,256]{2,1,0:T(8,128)(2,1)S(1)}, u32[]{:S(2)}, u32[]{:S(2)}) collective-permute-start(bf16[4,72,256]{2,1,0:T(8,128)(2,1)S(1)} %all_to_all.5.refs_4_), channel_id=1, source_target_pairs={{0,4},{4,8},{8,12},{12,16},{16,20},{20,24},{24,28},{1,5},{5,9},{9,... | collective-permute-start | bytes 442376 | tf_op jit(solution)/shard_map/ppermute | solution.py:176
  65.2 23.8 %collective-permute-start.9 = (bf16[64,512]{1,0:T(8,128)(2,1)S(1)}, bf16[64,512]{1,0:T(8,128)(2,1)S(1)}, u32[]{:S(2)}, u32[]{:S(2)}) collective-permute-start(bf16[64,512]{1,0:T(8,128)(2,1)S(1)} %get-tuple-element.19), channel_id=1, source_target_pairs={{0,32},{1,33},{2,34},{3,35},{4,36},{5,37},{6,38},{7,39},{8,40},{9,... | collective-permute-start | bytes 196616 | tf_op jit(solution)/shard_map/ppermute | solution.py:204
  71.9 17.1 %collective-permute-start.10 = (bf16[64,512]{1,0:T(8,128)(2,1)S(1)}, bf16[64,512]{1,0:T(8,128)(2,1)S(1)}, u32[]{:S(2)}, u32[]{:S(2)}) collective-permute-start(bf16[64,512]{1,0:T(8,128)(2,1)S(1)} %get-tuple-element.20), channel_id=1, source_target_pairs={{0,35},{1,32},{2,33},{3,34},{4,39},{5,36},{6,37},{7,38},{8,43},{9,... | collective-permute-start | bytes 196616 | tf_op jit(solution)/shard_map/ppermute | solution.py:204
  82.7 10.3 %collective-permute-start.11 = (bf16[64,512]{1,0:T(8,128)(2,1)S(1)}, bf16[64,512]{1,0:T(8,128)(2,1)S(1)}, u32[]{:S(2)}, u32[]{:S(2)}) collective-permute-start(bf16[64,512]{1,0:T(8,128)(2,1)S(1)} %get-tuple-element.21), channel_id=1, source_target_pairs={{0,34},{1,35},{2,32},{3,33},{4,38},{5,39},{6,36},{7,37},{8,42},{9,... | collective-permute-start | bytes 196616 | tf_op jit(solution)/shard_map/ppermute | solution.py:204
  87.0 10.7 %collective-permute-start.12 = (bf16[64,512]{1,0:T(8,128)(2,1)S(1)}, bf16[64,512]{1,0:T(8,128)(2,1)S(1)}, u32[]{:S(2)}, u32[]{:S(2)}) collective-permute-start(bf16[64,512]{1,0:T(8,128)(2,1)S(1)} %get-tuple-element.22), channel_id=1, source_target_pairs={{0,33},{1,34},{2,35},{3,32},{4,37},{5,38},{6,39},{7,36},{8,41},{9,... | collective-permute-start | bytes 196616 | tf_op jit(solution)/shard_map/ppermute | solution.py:204
  89.0 8.8 %copy-start.2 = (bf16[64,512]{1,0:T(8,128)(2,1)}, bf16[64,512]{1,0:T(8,128)(2,1)S(1)}, u32[]{:S(2)}) copy-start(bf16[64,512]{1,0:T(8,128)(2,1)S(1)} %collective-permute-done.9.refs_0_) | copy-start | bytes 196612
  89.0 8.7 %copy-start.3 = (bf16[64,512]{1,0:T(8,128)(2,1)}, bf16[64,512]{1,0:T(8,128)(2,1)S(1)}, u32[]{:S(2)}) copy-start(bf16[64,512]{1,0:T(8,128)(2,1)S(1)} %collective-permute-done.10.refs_1_) | copy-start | bytes 196612
  93.0 4.8 %copy-start.4 = (bf16[64,512]{1,0:T(8,128)(2,1)}, bf16[64,512]{1,0:T(8,128)(2,1)S(1)}, u32[]{:S(2)}) copy-start(bf16[64,512]{1,0:T(8,128)(2,1)S(1)} %collective-permute-done.11.refs_2_) | copy-start | bytes 196612
  97.7 0.6 copy-start.5
where the time goes:
time: 101 us; the launch traced here: 100 us
  starting transfers between devices  43.7 us (43%)
  waiting for transfers between devices  30.6 us (30%)
  blocking collectives  14.2 us (14%)
  Pallas kernels  10 us (10%)
    ppermute x4, starting transfers between devices, per_device(): lax.ppermute(attended[t], ('section', 'blk', 'head'), [(index(s, b, h), i...  23.8 us
    ppermute x6, waiting for transfers between devices, per_device(): lax.ppermute(own_pairs, 'blk', [(i, i + d) for i in range(blocks - d)])  21.9 us
    all_to_all x1, blocking collectives, per_device(): lax.all_to_all(pairs, 'head', split_axis=0, concat_axis=0, tiled=True)  14.2 us
    ppermute x6, starting transfers between devices, per_device(): lax.ppermute(own_pairs, 'blk', [(i, i + d) for i in range(blocks - d)])  10.5 us
    ppermute x3, starting transfers between devices, per_device(): lax.ppermute(turned[t], 'head', [(i, (i + t) % heads) for i in range(head...  9.47 us
    ppermute x4, waiting for transfers between devices, per_device(): lax.ppermute(attended[t], ('section', 'blk', 'head'), [(index(s, b, h), i...  8.74 us
    pallas_call x1, Pallas kernels, per_device(): pl.pallas_call(functools.partial(attend_kernel, heads=heads, back=back, s...  6.58 us
  transfers between devices with their start and end apart: 13, of which 6 were waited for; matrix products, arithmetic and copies ran while one was open for 0% of the time, Pallas kernels for 0%

commit v1 on v0

v1 whole, which is shorter than its diff:
```python
import functools
import math

import jax
import jax.numpy as jnp
from jax import lax
from jax.experimental import pallas as pl
from jax.experimental.pallas import tpu as pltpu
from jax.sharding import PartitionSpec as P

HEAD_SIZE = 128
NEG_FILL = -1e30
LONGEST_SEGMENT = 1536
LABELS = 4
LABEL_ROWS = 8
NO_LABEL = 9.0
NEAR = 4


def prepare_kernel(kv_ref, label_ref, q_ref, out_ref, label_rows, *, heads):
    tokens = kv_ref.shape[0]
    width = kv_ref.shape[1] // heads
    q_width = q_ref.shape[1] // heads
    label_rows[...] = jnp.full(label_rows.shape, NO_LABEL, jnp.float32)
    label_rows[0:1, 0:tokens] = label_ref[...].astype(jnp.float32)
    for which in range(heads):
        out_ref[which, 0:tokens, :] = kv_ref[:, which * width : (which + 1) * width]
        for part in range(q_width // width):
            start = which * q_width + part * width
            out_ref[which, (1 + part) * tokens : (2 + part) * tokens, :] = q_ref[
                :, start : start + width
            ]
        out_ref[which, out_ref.shape[1] - LABEL_ROWS :, :] = label_rows[...].astype(jnp.bfloat16)


def pack_kernel(given_ref, out_ref, label_rows, *, tokens):
    heads = given_ref.shape[0]
    rows = heads * tokens
    keys = given_ref[:, 0:tokens, 0:HEAD_SIZE].reshape(rows, HEAD_SIZE)
    values = given_ref[:, 0:tokens, HEAD_SIZE : 2 * HEAD_SIZE].reshape(rows, HEAD_SIZE)
    out_ref[0:HEAD_SIZE, :] = values.T
    for part in range(rows // HEAD_SIZE):
        out_ref[HEAD_SIZE : 2 * HEAD_SIZE, part * HEAD_SIZE : (part + 1) * HEAD_SIZE] = keys[
            part * HEAD_SIZE : (part + 1) * HEAD_SIZE
        ]
    label_rows[...] = jnp.zeros(label_rows.shape, jnp.float32)
    found = given_ref[:, given_ref.shape[1] - LABEL_ROWS :, :].astype(jnp.float32)
    for label in range(1, LABELS):
        below = jnp.sum(jnp.where(found < label, 1.0, 0.0), axis=0)
        label_rows[label : label + 1, :] = jnp.sum(below, axis=0, keepdims=True)
    out_ref[2 * HEAD_SIZE :, :] = label_rows[...].astype(jnp.bfloat16)


def count_labels(pair_refs, distances, block_index):
    count = jnp.zeros((LABEL_ROWS, 2 * HEAD_SIZE), jnp.float32)
    for distance, ref in zip(distances, pair_refs, strict=True):
        valid = jnp.where(block_index >= distance, 1.0, 0.0)
        count += ref[2 * HEAD_SIZE :, :].astype(jnp.float32) * valid
    return [jnp.sum(count[label : label + 1]).astype(jnp.int32) for label in range(1, LABELS)]


def begin_of(position, begins, base):
    found = jnp.full_like(position, base)
    for begin in begins:
        found = jnp.maximum(found, jnp.where(begin <= position, begin, base))
    return found


def scalar_begin(position, begins, base):
    found = base
    for begin in begins:
        found = jnp.maximum(found, jnp.where(begin <= position, begin, base))
    return found


def keys_of(ref):
    held = ref[HEAD_SIZE : 2 * HEAD_SIZE, :]
    parts = held.shape[1] // HEAD_SIZE
    return jnp.concatenate(
        [held[:, part * HEAD_SIZE : (part + 1) * HEAD_SIZE] for part in range(parts)], axis=0
    )


def values_of(ref):
    return ref[0:HEAD_SIZE, :]


def queries_of(given_ref, chunk, tokens, grouped):
    parts = given_ref.shape[2] // HEAD_SIZE
    pieces = []
    for j in range(grouped):
        row, column = (1 + j // parts) * tokens, (j % parts) * HEAD_SIZE
        pieces.append(given_ref[chunk, row : row + tokens, column : column + HEAD_SIZE])
    return jnp.concatenate(pieces, axis=0)


def positions_of(first, chunk, tokens, grouped):
    lane = lax.broadcasted_iota(jnp.int32, (1, grouped * tokens), 1)
    return first + chunk * tokens + lax.rem(lane, tokens)


def scores_of(keys, queries, key_first, place, begin, causal):
    scores = lax.dot_general(
        keys, queries, (((1,), (1,)), ((), ())), preferred_element_type=jnp.float32
    )
    key_place = key_first + lax.broadcasted_iota(jnp.int32, (scores.shape[0], 1), 0)
    allowed = key_place >= begin
    if causal:
        allowed = allowed & (key_place <= place)
    return jnp.where(allowed, scores, NEG_FILL)


def fold(state, keys, values, queries, key_first, place, begin, causal, scale):
    scores = scores_of(keys, queries, key_first, place, begin, causal)
    top = jnp.max(scores, axis=0, keepdims=True)
    if state is not None:
        old, total, mixed = state
        top = jnp.maximum(old, top)
    weights = jnp.exp2((scores - top) * scale)
    added = jnp.sum(weights, axis=0, keepdims=True)
    moved = jnp.dot(values, weights.astype(jnp.bfloat16), preferred_element_type=jnp.float32)
    if state is None:
        return top, added, moved
    factor = jnp.exp2((old - top) * scale)
    return top, total * factor + added, mixed * factor + moved


def near_kernel(given_ref, *refs, tokens, grouped, near, scale):
    pair_refs = refs[:near]
    count_ref, top_ref, total_ref, mixed_ref = refs[near:]
    heads = given_ref.shape[0]
    rows = tokens * heads
    block_index, own = lax.axis_index("blk"), lax.axis_index("head")
    first = block_index * rows
    base = jnp.maximum(block_index - (near - 1), 0) * rows
    counts = count_labels(pair_refs, range(near), block_index)
    for which, count in enumerate(counts):
        count_ref[which] = count
    begins = [base + count for count in counts]
    earliest = scalar_begin(first, begins, base)

    def chunk_of(turn):
        return lax.rem(own - turn + heads, heads)

    def step(turn, distance, state, keys, values):
        chunk = chunk_of(turn)
        place = positions_of(first, chunk, tokens, grouped)
        return fold(
            state,
            keys,
            values,
            queries_of(given_ref, chunk, tokens, grouped),
            (block_index - distance) * rows,
            place,
            begin_of(place, begins, base),
            distance == 0,
            scale,
        )

    def put(turn, state):
        top_ref[turn], total_ref[turn], mixed_ref[turn] = state

    keys, values = keys_of(pair_refs[0]), values_of(pair_refs[0])
    for turn in range(heads):
        put(turn, step(turn, 0, None, keys, values))
    for distance in range(1, near):
        last = (block_index - distance) * rows + rows - 1

        @pl.when((block_index >= distance) & (last >= earliest))
        def _(distance=distance):
            keys = keys_of(pair_refs[distance])
            values = values_of(pair_refs[distance])
            for turn in range(heads):
                state = top_ref[turn], total_ref[turn], mixed_ref[turn]
                put(turn, step(turn, distance, state, keys, values))


def far_kernel(
    count_ref,
    given_ref,
    top_ref,
    total_ref,
    mixed_ref,
    *refs,
    turn,
    tokens,
    grouped,
    near,
    back,
    scale,
):
    pair_refs = refs[: back + 1 - near]
    out_ref, new_total, new_mixed, new_top = refs[back + 1 - near :]
    heads = given_ref.shape[0]
    rows = tokens * heads
    block_index, own = lax.axis_index("blk"), lax.axis_index("head")
    first = block_index * rows
    base = jnp.maximum(block_index - back, 0) * rows
    new_top[...] = top_ref[turn]
    new_total[...] = total_ref[turn]
    new_mixed[...] = mixed_ref[turn]

    @pl.when(block_index >= near)
    def _():
        counts = count_labels(pair_refs, range(near, back + 1), block_index)
        begins = [base + count + count_ref[which] for which, count in enumerate(counts)]
        earliest = scalar_begin(first, begins, base)
        chunk = lax.rem(own - turn + heads, heads)
        place = positions_of(first, chunk, tokens, grouped)
        begin = begin_of(place, begins, base)
        for distance in range(near, back + 1):
            last = (block_index - distance) * rows + rows - 1

            @pl.when((block_index >= distance) & (last >= earliest))
            def _(distance=distance):
                ref = pair_refs[distance - near]
                new_top[...], new_total[...], new_mixed[...] = fold(
                    (new_top[...], new_total[...], new_mixed[...]),
                    keys_of(ref),
                    values_of(ref),
                    queries_of(given_ref, chunk, tokens, grouped),
                    (block_index - distance) * rows,
                    place,
                    begin,
                    False,
                    scale,
                )

    normed = (new_mixed[...] / new_total[...]).T.astype(jnp.bfloat16)
    for j in range(grouped):
        out_ref[:, j * HEAD_SIZE : (j + 1) * HEAD_SIZE] = normed[j * tokens : (j + 1) * tokens]


def assemble_kernel(*refs, heads):
    pieces, out_ref, semaphores = refs[:heads], refs[heads], refs[heads + 1]
    width = pieces[0].shape[1]
    own = lax.axis_index("head")
    copies = []
    for turn in range(heads):
        start = pl.multiple_of(lax.rem(own + turn, heads) * width, width)
        copies.append(
            pltpu.make_async_copy(
                pieces[turn], out_ref.at[:, pl.ds(start, width)], semaphores.at[turn]
            )
        )
        copies[-1].start()
    for copy in copies:
        copy.wait()


def vmem(count):
    return [pl.BlockSpec(memory_space=pltpu.VMEM)] * count


def cost(tiles, rows, width):
    return pl.CostEstimate(
        flops=4 * tiles * rows * rows * width,
        bytes_accessed=tiles * rows * width * 4,
        transcendentals=tiles * rows * rows,
    )


def per_device(queries, keys_values, segment_ids):
    sections = lax.axis_size("section")
    blocks = lax.axis_size("blk")
    heads = lax.axis_size("head")
    tokens = queries.shape[1]
    rows = tokens * heads
    kv_width = keys_values.shape[2] // heads
    q_width = queries.shape[2] // heads
    grouped = q_width // HEAD_SIZE
    back = min(blocks - 1, -(-LONGEST_SEGMENT // rows))
    near = min(NEAR, back)
    scale = math.log2(math.e) / math.sqrt(HEAD_SIZE)

    parts = 1 + q_width // kv_width
    prepared = pl.pallas_call(
        functools.partial(prepare_kernel, heads=heads),
        out_shape=jax.ShapeDtypeStruct(
            (heads, parts * tokens + LABEL_ROWS, kv_width), jnp.bfloat16
        ),
        in_specs=vmem(3),
        out_specs=vmem(1)[0],
        scratch_shapes=[pltpu.VMEM((LABEL_ROWS, kv_width), jnp.float32)],
        compiler_params=pltpu.CompilerParams(vmem_limit_bytes=4 << 20),
        name="prepare",
    )(keys_values[0], segment_ids, queries[0])
    given = lax.all_to_all(prepared, "head", split_axis=0, concat_axis=0, tiled=True)
    own_pairs = pl.pallas_call(
        functools.partial(pack_kernel, tokens=tokens),
        out_shape=jax.ShapeDtypeStruct((2 * HEAD_SIZE + LABEL_ROWS, rows), jnp.bfloat16),
        in_specs=vmem(1),
        out_specs=vmem(1)[0],
        scratch_shapes=[pltpu.VMEM((LABEL_ROWS, kv_width), jnp.float32)],
        compiler_params=pltpu.CompilerParams(vmem_limit_bytes=4 << 20),
        name="pack",
    )(given)
    earlier = [
        lax.ppermute(own_pairs, "blk", [(i, i + d) for i in range(blocks - d)])
        for d in range(1, back + 1)
    ]

    lanes = grouped * tokens
    state = [
        jax.ShapeDtypeStruct((heads, 1, lanes), jnp.float32),
        jax.ShapeDtypeStruct((heads, 1, lanes), jnp.float32),
        jax.ShapeDtypeStruct((heads, HEAD_SIZE, lanes), jnp.float32),
    ]
    counts, *state = pl.pallas_call(
        functools.partial(near_kernel, tokens=tokens, grouped=grouped, near=near, scale=scale),
        out_shape=[jax.ShapeDtypeStruct((LABELS - 1,), jnp.int32)] + state,
        in_specs=vmem(1 + near),
        out_specs=[pl.BlockSpec(memory_space=pltpu.SMEM)] + vmem(3),
        compiler_params=pltpu.CompilerParams(vmem_limit_bytes=16 << 20),
        cost_estimate=cost(near * heads, rows, HEAD_SIZE),
        name="attend_near",
    )(given, own_pairs, *earlier[: near - 1])

    def index(section, block, head):
        return ((section % sections) * blocks + block) * heads + head % heads

    received = []
    for turn in range(heads):
        attended = pl.pallas_call(
            functools.partial(
                far_kernel,
                turn=turn,
                tokens=tokens,
                grouped=grouped,
                near=near,
                back=back,
                scale=scale,
            ),
            out_shape=jax.ShapeDtypeStruct((tokens, q_width), jnp.bfloat16),
            in_specs=[pl.BlockSpec(memory_space=pltpu.SMEM)] + vmem(4 + back + 1 - near),
            out_specs=vmem(1)[0],
            scratch_shapes=[
                pltpu.VMEM((1, lanes), jnp.float32),
                pltpu.VMEM((HEAD_SIZE, lanes), jnp.float32),
                pltpu.VMEM((1, lanes), jnp.float32),
            ],
            compiler_params=pltpu.CompilerParams(vmem_limit_bytes=16 << 20),
            cost_estimate=cost(back + 1 - near, rows, HEAD_SIZE),
            name="attend_far",
        )(counts, given, *state, *earlier[near - 1 :])
        route = [
            (index(s, b, h), index(s + 1, b, h - turn))
            for s in range(sections)
            for b in range(blocks)
            for h in range(heads)
        ]
        received.append(lax.ppermute(attended, ("section", "blk", "head"), route))
    result = pl.pallas_call(
        functools.partial(assemble_kernel, heads=heads),
        out_shape=jax.ShapeDtypeStruct(queries.shape[1:], jnp.bfloat16),
        in_specs=vmem(heads),
        out_specs=pl.BlockSpec(memory_space=pl.ANY),
        scratch_shapes=[pltpu.SemaphoreType.DMA((heads,))],
        compiler_params=pltpu.CompilerParams(vmem_limit_bytes=4 << 20),
        name="assemble",
    )(*received)
    return result[None]


def solution(mesh):
    return jax.shard_map(
        per_device,
        mesh=mesh,
        in_specs=(
            P("section", ("blk", "head"), None),
            P("section", ("blk", "head"), None),
            P("section", ("blk", "head")),
        ),
        out_specs=P("section", ("blk", "head"), None),
        check_vma=False,
    )
```

time: 101 us -> 97.5 us (0.965)
  the two profiles are of different devices: /device:TPU:200 before, /device:TPU:76 now
where the time goes in v1:
time: 97.5 us; the launch traced here: 97 us
  waiting for transfers between devices  30.8 us (32%)
  starting transfers between devices  26.8 us (27%)
  blocking collectives  21.8 us (22%)
  Pallas kernels  14.9 us (15%)
  local copies, waits for them, and re-layouts  2.51 us (3%)
    all_to_all x1, blocking collectives, per_device(): lax.all_to_all(prepared, 'head', split_axis=0, concat_axis=0, tiled=True)  21.8 us
    ppermute x6, waiting for transfers between devices, per_device(): lax.ppermute(own_pairs, 'blk', [(i, i + d) for i in range(blocks - d)])  21.1 us
    ppermute x4, starting transfers between devices, per_device(): received.append(lax.ppermute(attended, ('section', 'blk', 'head'), route))  17.9 us
    ppermute x4, waiting for transfers between devices, per_device(): received.append(lax.ppermute(attended, ('section', 'blk', 'head'), route))  9.66 us
    ppermute x6, starting transfers between devices, per_device(): lax.ppermute(own_pairs, 'blk', [(i, i + d) for i in range(blocks - d)])  8.95 us
    pallas_call x4, Pallas kernels, per_device(): pl.pallas_call(functools.partial(far_kernel, turn=turn, tokens=tokens, gr...  8.35 us
    pallas_call x1, Pallas kernels, per_device(): pl.pallas_call(functools.partial(near_kernel, tokens=tokens, grouped=grou...  5.74 us
    unnamed x6, local copies, waits for them, and re-layouts  2.51 us
  transfers between devices with their start and end apart: 10, of which 5 were waited for; matrix products, arithmetic and copies ran while one was open for 0% of the time, Pallas kernels for 12%

profile of v1, /device:TPU:76, one launch (start us, length us, event | category | flops | bytes accessed | tf_op | source)
XLA Modules:
  0.0 97.0 jit_solution(1879925042847375219)
XLA Ops:
  0.0 0.0 copy-start.2
  0.0 0.7 copy-done.2
  0.7 0.9 copy-done
  1.6 0.9 copy-done.1
  2.5 21.8 %all_to_all.5.given_ref = bf16[4,200,256]{2,1,0:T(8,128)(2,1)S(1)} all-to-all(bf16[4,200,256]{2,1,0:T(8,128)(2,1)S(1)} %prepare.1), channel_id=1, replica_groups=mesh['section'=32,'blk'=8,'head'=4] {'head'}, dimensions={0} | all-to-all | bytes 819200 | tf_op jit(solution)/shard_map/all_to_all | solution.py:288
  24.4 0.1 pack.1.refs_0_
  24.4 2.5 %collective-permute-start = (bf16[264,256]{1,0:T(8,128)(2,1)S(1)}, bf16[264,256]{1,0:T(8,128)(2,1)S(1)}, u32[]{:S(2)}, u32[]{:S(2)}) collective-permute-start(bf16[264,256]{1,0:T(8,128)(2,1)S(1)} %pack.1.refs_0_), channel_id=1, source_target_pairs={{0,4},{4,8},{8,12},{12,16},{16,20},{20,24},{24,28},{1,5},{5,9},{9,... | collective-permute-start | bytes 405512 | tf_op jit(solution)/shard_map/ppermute | solution.py:299
  26.9 1.3 %collective-permute-start.1 = (bf16[264,256]{1,0:T(8,128)(2,1)S(1)}, bf16[264,256]{1,0:T(8,128)(2,1)S(1)}, u32[]{:S(2)}, u32[]{:S(2)}) collective-permute-start(bf16[264,256]{1,0:T(8,128)(2,1)S(1)} %pack.1.refs_0_), channel_id=1, source_target_pairs={{0,8},{4,12},{8,16},{12,20},{16,24},{20,28},{1,9},{5,13},{9,17},{1... | collective-permute-start | bytes 405512 | tf_op jit(solution)/shard_map/ppermute | solution.py:299
  28.2 1.3 %collective-permute-start.2 = (bf16[264,256]{1,0:T(8,128)(2,1)S(1)}, bf16[264,256]{1,0:T(8,128)(2,1)S(1)}, u32[]{:S(2)}, u32[]{:S(2)}) collective-permute-start(bf16[264,256]{1,0:T(8,128)(2,1)S(1)} %pack.1.refs_0_), channel_id=1, source_target_pairs={{0,12},{4,16},{8,20},{12,24},{16,28},{1,13},{5,17},{9,21},{13,25},... | collective-permute-start | bytes 405512 | tf_op jit(solution)/shard_map/ppermute | solution.py:299
  29.5 1.3 %collective-permute-start.3 = (bf16[264,256]{1,0:T(8,128)(2,1)S(1)}, bf16[264,256]{1,0:T(8,128)(2,1)S(1)}, u32[]{:S(2)}, u32[]{:S(2)}) collective-permute-start(bf16[264,256]{1,0:T(8,128)(2,1)S(1)} %pack.1.refs_0_), channel_id=1, source_target_pairs={{0,16},{4,20},{8,24},{12,28},{1,17},{5,21},{9,25},{13,29},{2,18},{... | collective-permute-start | bytes 405512 | tf_op jit(solution)/shard_map/ppermute | solution.py:299
  30.8 1.3 %collective-permute-start.4 = (bf16[264,256]{1,0:T(8,128)(2,1)S(1)}, bf16[264,256]{1,0:T(8,128)(2,1)S(1)}, u32[]{:S(2)}, u32[]{:S(2)}) collective-permute-start(bf16[264,256]{1,0:T(8,128)(2,1)S(1)} %pack.1.refs_0_), channel_id=1, source_target_pairs={{0,20},{4,24},{8,28},{1,21},{5,25},{9,29},{2,22},{6,26},{10,30},{3... | collective-permute-start | bytes 405512 | tf_op jit(solution)/shard_map/ppermute | solution.py:299
  32.1 2.0 %collective-permute-done.refs_1_ = bf16[264,256]{1,0:T(8,128)(2,1)S(1)} collective-permute-done((bf16[264,256]{1,0:T(8,128)(2,1)S(1)}, bf16[264,256]{1,0:T(8,128)(2,1)S(1)}, u32[]{:S(2)}, u32[]{:S(2)}) %collective-permute-start) | collective-permute-done | bytes 135200 | tf_op jit(solution)/shard_map/ppermute | solution.py:299
  34.1 1.3 %collective-permute-start.5 = (bf16[264,256]{1,0:T(8,128)(2,1)S(1)}, bf16[264,256]{1,0:T(8,128)(2,1)S(1)}, u32[]{:S(2)}, u32[]{:S(2)}) collective-permute-start(bf16[264,256]{1,0:T(8,128)(2,1)S(1)} %pack.1.refs_0_), channel_id=1, source_target_pairs={{0,24},{4,28},{1,25},{5,29},{2,26},{6,30},{3,27},{7,31},{32,56},{3... | collective-permute-start | bytes 405512 | tf_op jit(solution)/shard_map/ppermute | solution.py:299
  35.4 2.5 %collective-permute-done.1.refs_2_ = bf16[264,256]{1,0:T(8,128)(2,1)S(1)} collective-permute-done((bf16[264,256]{1,0:T(8,128)(2,1)S(1)}, bf16[264,256]{1,0:T(8,128)(2,1)S(1)}, u32[]{:S(2)}, u32[]{:S(2)}) %collective-permute-start.1) | collective-permute-done | bytes 135200 | tf_op jit(solution)/shard_map/ppermute | solution.py:299
  37.9 16.7 %collective-permute-done.2.refs_3_ = bf16[264,256]{1,0:T(8,128)(2,1)S(1)} collective-permute-done((bf16[264,256]{1,0:T(8,128)(2,1)S(1)}, bf16[264,256]{1,0:T(8,128)(2,1)S(1)}, u32[]{:S(2)}, u32[]{:S(2)}) %collective-permute-start.2) | collective-permute-done | bytes 135200 | tf_op jit(solution)/shard_map/ppermute | solution.py:299
  54.6 5.7 %attend_near.1 = (s32[3]{0:T(128)S(1)}, f32[4,1,256]{2,1,0:T(1,128)S(1)}, f32[4,1,256]{2,1,0:T(1,128)S(1)}, f32[4,128,256]{2,1,0:T(8,128)S(1)}) custom-call(bf16[4,200,256]{2,1,0:T(8,128)(2,1)S(1)} %all_to_all.5.given_ref, bf16[264,256]{1,0:T(8,128)(2,1)S(1)} %pack.1.refs_0_, bf16[264,256]{1,0:T(8,128)(2,1)S(1)} %collective-permute-done.refs_1_, ...), custom_call_target="tpu_custom_call" | custom-call | flops 536870912 | bytes 2097152 | tf_op jit(solution)/shard_map/attend_near/pallas_call | solution.py:309
  60.3 0.0 collective-permute-done.3.refs_0_
  60.3 0.0 collective-permute-done.4.refs_1_
  60.3 0.0 collective-permute-done.5.refs_2_
  60.3 2.1 %attend_far.7 = bf16[64,512]{1,0:T(8,128)(2,1)S(1)} custom-call(s32[3]{0:T(128)S(1)} %get-tuple-element.9.count_ref, bf16[4,200,256]{2,1,0:T(8,128)(2,1)S(1)} %all_to_all.5.given_ref, f32[4,1,256]{2,1,0:T(1,128)S(1)} %get-tuple-element.10.top_ref, f32[4,1,256]{2,1,0:T(1,128)S(1)} %get-tuple-element.11.total_ref, ...), custom_call_target="tpu_custom_call" | custom-call | flops 100663296 | bytes 393216 | tf_op jit(solution)/shard_map/attend_far/pallas_call | solution.py:324
  62.4 1.9 %collective-permute-start.9 = (bf16[64,512]{1,0:T(8,128)(2,1)S(1)}, bf16[64,512]{1,0:T(8,128)(2,1)S(1)}, u32[]{:S(2)}, u32[]{:S(2)}) collective-permute-start(bf16[64,512]{1,0:T(8,128)(2,1)S(1)} %attend_far.7), channel_id=1, source_target_pairs={{0,33},{1,34},{2,35},{3,32},{4,37},{5,38},{6,39},{7,36},{8,41},{9,... | collective-permute-start | bytes 196616 | tf_op jit(solution)/shard_map/ppermute | solution.py:352
  64.4 2.1 %attend_far.6 = bf16[64,512]{1,0:T(8,128)(2,1)S(1)} custom-call(s32[3]{0:T(128)S(1)} %get-tuple-element.9.count_ref, bf16[4,200,256]{2,1,0:T(8,128)(2,1)S(1)} %all_to_all.5.given_ref, f32[4,1,256]{2,1,0:T(1,128)S(1)} %get-tuple-element.10.top_ref, f32[4,1,256]{2,1,0:T(1,128)S(1)} %get-tuple-element.11.total_ref, ...), custom_call_target="tpu_custom_call" | custom-call | flops 100663296 | bytes 393216 | tf_op jit(solution)/shard_map/attend_far/pallas_call | solution.py:324
  66.5 9.6 %collective-permute-start.8 = (bf16[64,512]{1,0:T(8,128)(2,1)S(1)}, bf16[64,512]{1,0:T(8,128)(2,1)S(1)}, u32[]{:S(2)}, u32[]{:S(2)}) collective-permute-start(bf16[64,512]{1,0:T(8,128)(2,1)S(1)} %attend_far.6), channel_id=1, source_target_pairs={{0,34},{1,35},{2,32},{3,33},{4,38},{5,39},{6,36},{7,37},{8,42},{9,... | collective-permute-start | bytes 196616 | tf_op jit(solution)/shard_map/ppermute | solution.py:352
  76.1 2.1 %attend_far.5 = bf16[64,512]{1,0:T(8,128)(2,1)S(1)} custom-call(s32[3]{0:T(128)S(1)} %get-tuple-element.9.count_ref, bf16[4,200,256]{2,1,0:T(8,128)(2,1)S(1)} %all_to_all.5.given_ref, f32[4,1,256]{2,1,0:T(1,128)S(1)} %get-tuple-element.10.top_ref, f32[4,1,256]{2,1,0:T(1,128)S(1)} %get-tuple-element.11.total_ref, ...), custom_call_target="tpu_custom_call" | custom-call | flops 100663296 | bytes 393216 | tf_op jit(solution)/shard_map/attend_far/pallas_call | solution.py:324
  78.2 4.5 %collective-permute-start.7 = (bf16[64,512]{1,0:T(8,128)(2,1)S(1)}, bf16[64,512]{1,0:T(8,128)(2,1)S(1)}, u32[]{:S(2)}, u32[]{:S(2)}) collective-permute-start(bf16[64,512]{1,0:T(8,128)(2,1)S(1)} %attend_far.5), channel_id=1, source_target_pairs={{0,35},{1,32},{2,33},{3,34},{4,39},{5,36},{6,37},{7,38},{8,43},{9,... | collective-permute-start | bytes 196616 | tf_op jit(solution)/shard_map/ppermute | solution.py:352
  82.6 2.1 %attend_far.4 = bf16[64,512]{1,0:T(8,128)(2,1)S(1)} custom-call(s32[3]{0:T(128)S(1)} %get-tuple-element.9.count_ref, bf16[4,200,256]{2,1,0:T(8,128)(2,1)S(1)} %all_to_all.5.given_ref, f32[4,1,256]{2,1,0:T(1,128)S(1)} %get-tuple-element.10.top_ref, f32[4,1,256]{2,1,0:T(1,128)S(1)} %get-tuple-element.11.total_ref, ...), custom_call_target="tpu_custom_call" | custom-call | flops 100663296 | bytes 393216 | tf_op jit(solution)/shard_map/attend_far/pallas_call | solution.py:324
  84.7 1.9 %collective-permute-start.6 = (bf16[64,512]{1,0:T(8,128)(2,1)S(1)}, bf16[64,512]{1,0:T(8,128)(2,1)S(1)}, u32[]{:S(2)}, u32[]{:S(2)}) collective-permute-start(bf16[64,512]{1,0:T(8,128)(2,1)S(1)} %attend_far.4), channel_id=1, source_target_pairs={{0,32},{1,33},{2,34},{3,35},{4,36},{5,37},{6,38},{7,39},{8,40},{9,... | collective-permute-start | bytes 196616 | tf_op jit(solution)/shard_map/ppermute | solution.py:352
  86.6 0.0 collective-permute-done.9.refs_3_
  86.7 0.0 collective-permute-done.8.refs_2_
  86.7 2.2 %collective-permute-done.7.refs_1_ = bf16[64,512]{1,0:T(8,128)(2,1)S(1)} collective-permute-done((bf16[64,512]{1,0:T(8,128)(2,1)S(1)}, bf16[64,512]{1,0:T(8,128)(2,1)S(1)}, u32[]{:S(2)}, u32[]{:S(2)}) %collective-permute-start.7) | collective-permute-done | bytes 65568 | tf_op jit(solution)/shard_map/ppermute | solution.py:352
  88.9 7.5 %collective-permute-done.6.refs_0_ = bf16[64,512]{1,0:T(8,128)(2,1)S(1)} collective-permute-done((bf16[64,512]{1,0:T(8,128)(2,1)S(1)}, bf16[64,512]{1,0:T(8,128)(2,1)S(1)}, u32[]{:S(2)}, u32[]{:S(2)}) %collective-permute-start.6) | collective-permute-done | bytes 65568 | tf_op jit(solution)/shard_map/ppermute | solution.py:352
  96.3 0.7 assemble.1
  (3 shorter events, 0.0 us)
Async XLA Ops:
  0.0 0.7 copy-start.2
  0.7 0.9 copy-start
  1.6 0.9 copy-start.1
  24.4 9.7 %collective-permute-start = (bf16[264,256]{1,0:T(8,128)(2,1)S(1)}, bf16[264,256]{1,0:T(8,128)(2,1)S(1)}, u32[]{:S(2)}, u32[]{:S(2)}) collective-permute-start(bf16[264,256]{1,0:T(8,128)(2,1)S(1)} %pack.1.refs_0_), channel_id=1, source_target_pairs={{0,4},{4,8},{8,12},{12,16},{16,20},{20,24},{24,28},{1,5},{5,9},{9,... | collective-permute-start | bytes 405512 | tf_op jit(solution)/shard_map/ppermute | solution.py:299
  26.9 10.9 %collective-permute-start.1 = (bf16[264,256]{1,0:T(8,128)(2,1)S(1)}, bf16[264,256]{1,0:T(8,128)(2,1)S(1)}, u32[]{:S(2)}, u32[]{:S(2)}) collective-permute-start(bf16[264,256]{1,0:T(8,128)(2,1)S(1)} %pack.1.refs_0_), channel_id=1, source_target_pairs={{0,8},{4,12},{8,16},{12,20},{16,24},{20,28},{1,9},{5,13},{9,17},{1... | collective-permute-start | bytes 405512 | tf_op jit(solution)/shard_map/ppermute | solution.py:299
  28.2 26.3 %collective-permute-start.2 = (bf16[264,256]{1,0:T(8,128)(2,1)S(1)}, bf16[264,256]{1,0:T(8,128)(2,1)S(1)}, u32[]{:S(2)}, u32[]{:S(2)}) collective-permute-start(bf16[264,256]{1,0:T(8,128)(2,1)S(1)} %pack.1.refs_0_), channel_id=1, source_target_pairs={{0,12},{4,16},{8,20},{12,24},{16,28},{1,13},{5,17},{9,21},{13,25},... | collective-permute-start | bytes 405512 | tf_op jit(solution)/shard_map/ppermute | solution.py:299
  29.5 30.8 %collective-permute-start.3 = (bf16[264,256]{1,0:T(8,128)(2,1)S(1)}, bf16[264,256]{1,0:T(8,128)(2,1)S(1)}, u32[]{:S(2)}, u32[]{:S(2)}) collective-permute-start(bf16[264,256]{1,0:T(8,128)(2,1)S(1)} %pack.1.refs_0_), channel_id=1, source_target_pairs={{0,16},{4,20},{8,24},{12,28},{1,17},{5,21},{9,25},{13,29},{2,18},{... | collective-permute-start | bytes 405512 | tf_op jit(solution)/shard_map/ppermute | solution.py:299
  30.8 29.5 %collective-permute-start.4 = (bf16[264,256]{1,0:T(8,128)(2,1)S(1)}, bf16[264,256]{1,0:T(8,128)(2,1)S(1)}, u32[]{:S(2)}, u32[]{:S(2)}) collective-permute-start(bf16[264,256]{1,0:T(8,128)(2,1)S(1)} %pack.1.refs_0_), channel_id=1, source_target_pairs={{0,20},{4,24},{8,28},{1,21},{5,25},{9,29},{2,22},{6,26},{10,30},{3... | collective-permute-start | bytes 405512 | tf_op jit(solution)/shard_map/ppermute | solution.py:299
  34.1 26.2 %collective-permute-start.5 = (bf16[264,256]{1,0:T(8,128)(2,1)S(1)}, bf16[264,256]{1,0:T(8,128)(2,1)S(1)}, u32[]{:S(2)}, u32[]{:S(2)}) collective-permute-start(bf16[264,256]{1,0:T(8,128)(2,1)S(1)} %pack.1.refs_0_), channel_id=1, source_target_pairs={{0,24},{4,28},{1,25},{5,29},{2,26},{6,30},{3,27},{7,31},{32,56},{3... | collective-permute-start | bytes 405512 | tf_op jit(solution)/shard_map/ppermute | solution.py:299
  62.4 24.2 %collective-permute-start.9 = (bf16[64,512]{1,0:T(8,128)(2,1)S(1)}, bf16[64,512]{1,0:T(8,128)(2,1)S(1)}, u32[]{:S(2)}, u32[]{:S(2)}) collective-permute-start(bf16[64,512]{1,0:T(8,128)(2,1)S(1)} %attend_far.7), channel_id=1, source_target_pairs={{0,33},{1,34},{2,35},{3,32},{4,37},{5,38},{6,39},{7,36},{8,41},{9,... | collective-permute-start | bytes 196616 | tf_op jit(solution)/shard_map/ppermute | solution.py:352
  66.5 20.2 %collective-permute-start.8 = (bf16[64,512]{1,0:T(8,128)(2,1)S(1)}, bf16[64,512]{1,0:T(8,128)(2,1)S(1)}, u32[]{:S(2)}, u32[]{:S(2)}) collective-permute-start(bf16[64,512]{1,0:T(8,128)(2,1)S(1)} %attend_far.6), channel_id=1, source_target_pairs={{0,34},{1,35},{2,32},{3,33},{4,38},{5,39},{6,36},{7,37},{8,42},{9,... | collective-permute-start | bytes 196616 | tf_op jit(solution)/shard_map/ppermute | solution.py:352
  78.2 10.7 %collective-permute-start.7 = (bf16[64,512]{1,0:T(8,128)(2,1)S(1)}, bf16[64,512]{1,0:T(8,128)(2,1)S(1)}, u32[]{:S(2)}, u32[]{:S(2)}) collective-permute-start(bf16[64,512]{1,0:T(8,128)(2,1)S(1)} %attend_far.5), channel_id=1, source_target_pairs={{0,35},{1,32},{2,33},{3,34},{4,39},{5,36},{6,37},{7,38},{8,43},{9,... | collective-permute-start | bytes 196616 | tf_op jit(solution)/shard_map/ppermute | solution.py:352
  84.7 11.6 %collective-permute-start.6 = (bf16[64,512]{1,0:T(8,128)(2,1)S(1)}, bf16[64,512]{1,0:T(8,128)(2,1)S(1)}, u32[]{:S(2)}, u32[]{:S(2)}) collective-permute-start(bf16[64,512]{1,0:T(8,128)(2,1)S(1)} %attend_far.4), channel_id=1, source_target_pairs={{0,32},{1,33},{2,34},{3,35},{4,36},{5,37},{6,38},{7,39},{8,40},{9,... | collective-permute-start | bytes 196616 | tf_op jit(solution)/shard_map/ppermute | solution.py:352

commit v2 on v1

v2 whole, which is shorter than its diff:
```python
import functools
import math

import jax
import jax.numpy as jnp
from jax import lax
from jax.experimental import pallas as pl
from jax.experimental.pallas import tpu as pltpu
from jax.sharding import PartitionSpec as P

HEAD_SIZE = 128
NEG_FILL = -1e30
LONGEST_SEGMENT = 1536
LABELS = 4
LABEL_ROWS = 8
NO_LABEL = 9.0
NEAR = 3
PREPARE_VMEM = 56 << 20
SEND_ORDER = (2, 3, 1, 0)


def prepare_kernel(
    kv_ref, label_ref, q_ref, out_ref, own_labels, label_rows, packed_rows, semaphores, *, heads
):
    tokens = kv_ref.shape[0]
    width = kv_ref.shape[1] // heads
    q_parts = q_ref.shape[1] // heads // width
    copies = []

    def start(source, target):
        copies.append(pltpu.make_async_copy(source, target, semaphores.at[len(copies)]))
        copies[-1].start()

    start(label_ref, own_labels)
    for which in range(heads):
        start(
            kv_ref.at[:, pl.ds(which * width, width)],
            out_ref.at[which, pl.ds(0, tokens), :],
        )
        for part in range(q_parts):
            start(
                q_ref.at[:, pl.ds((which * q_parts + part) * width, width)],
                out_ref.at[which, pl.ds((1 + part) * tokens, tokens), :],
            )
    copies[0].wait()
    label_rows[...] = jnp.full(label_rows.shape, NO_LABEL, jnp.float32)
    label_rows[0:1, 0:tokens] = own_labels[...].astype(jnp.float32)
    packed_rows[...] = label_rows[...].astype(jnp.bfloat16)
    for which in range(heads):
        start(packed_rows, out_ref.at[which, pl.ds(out_ref.shape[1] - LABEL_ROWS, LABEL_ROWS), :])
    for copy in copies[1:]:
        copy.wait()


def pack_kernel(given_ref, out_ref, label_rows, *, tokens):
    heads = given_ref.shape[0]
    rows = heads * tokens
    keys = given_ref[:, 0:tokens, 0:HEAD_SIZE].reshape(rows, HEAD_SIZE)
    values = given_ref[:, 0:tokens, HEAD_SIZE : 2 * HEAD_SIZE].reshape(rows, HEAD_SIZE)
    out_ref[0:HEAD_SIZE, :] = values.T
    for part in range(rows // HEAD_SIZE):
        out_ref[HEAD_SIZE : 2 * HEAD_SIZE, part * HEAD_SIZE : (part + 1) * HEAD_SIZE] = keys[
            part * HEAD_SIZE : (part + 1) * HEAD_SIZE
        ]
    label_rows[...] = jnp.zeros(label_rows.shape, jnp.float32)
    found = given_ref[:, given_ref.shape[1] - LABEL_ROWS :, :].astype(jnp.float32)
    for label in range(1, LABELS):
        below = jnp.sum(jnp.where(found < label, 1.0, 0.0), axis=0)
        label_rows[label : label + 1, :] = jnp.sum(below, axis=0, keepdims=True)
    out_ref[2 * HEAD_SIZE :, :] = label_rows[...].astype(jnp.bfloat16)


def count_labels(pair_refs, distances, block_index):
    count = jnp.zeros((LABEL_ROWS, 2 * HEAD_SIZE), jnp.float32)
    for distance, ref in zip(distances, pair_refs, strict=True):
        valid = jnp.where(block_index >= distance, 1.0, 0.0)
        count += ref[2 * HEAD_SIZE :, :].astype(jnp.float32) * valid
    return [jnp.sum(count[label : label + 1]).astype(jnp.int32) for label in range(1, LABELS)]


def begin_of(position, begins, base):
    found = jnp.full_like(position, base)
    for begin in begins:
        found = jnp.maximum(found, jnp.where(begin <= position, begin, base))
    return found


def keys_of(ref):
    held = ref[HEAD_SIZE : 2 * HEAD_SIZE, :]
    parts = held.shape[1] // HEAD_SIZE
    return jnp.concatenate(
        [held[:, part * HEAD_SIZE : (part + 1) * HEAD_SIZE] for part in range(parts)], axis=0
    )


def values_of(ref):
    return ref[0:HEAD_SIZE, :]


def queries_of(given_ref, chunk, tokens, grouped):
    parts = given_ref.shape[2] // HEAD_SIZE
    pieces = []
    for j in range(grouped):
        row, column = (1 + j // parts) * tokens, (j % parts) * HEAD_SIZE
        pieces.append(given_ref[chunk, row : row + tokens, column : column + HEAD_SIZE])
    return jnp.concatenate(pieces, axis=0)


def positions_of(first, chunk, tokens, grouped):
    lane = lax.broadcasted_iota(jnp.int32, (1, grouped * tokens), 1)
    return first + chunk * tokens + lax.rem(lane, tokens)


def fold(state, pair_refs, queries, key_first, place, begin, scale):
    keys = jnp.concatenate([keys_of(ref) for ref in pair_refs], axis=0)
    values = jnp.concatenate([values_of(ref) for ref in pair_refs], axis=1)
    scores = lax.dot_general(
        keys, queries, (((1,), (1,)), ((), ())), preferred_element_type=jnp.float32
    )
    key = lax.broadcasted_iota(jnp.int32, scores.shape, 0)
    allowed = key >= begin - key_first
    if place is not None:
        allowed = allowed & (key <= place - key_first)
    scores = jnp.where(allowed, scores, NEG_FILL)
    top = jnp.max(scores, axis=0, keepdims=True)
    if state is not None:
        old, total, mixed = state
        top = jnp.maximum(old, top)
    weights = jnp.exp2((scores - top) * scale)
    added = jnp.sum(weights, axis=0, keepdims=True)
    moved = jnp.dot(values, weights.astype(jnp.bfloat16), preferred_element_type=jnp.float32)
    if state is None:
        return top, added, moved
    factor = jnp.exp2((old - top) * scale)
    return top, total * factor + added, mixed * factor + moved


def near_kernel(given_ref, *refs, tokens, grouped, near, scale):
    pair_refs = refs[:near]
    count_ref, top_ref, total_ref, mixed_ref = refs[near:]
    heads = given_ref.shape[0]
    rows = tokens * heads
    block_index, own = lax.axis_index("blk"), lax.axis_index("head")
    first = block_index * rows
    base = jnp.maximum(block_index - (near - 1), 0) * rows
    counts = count_labels(pair_refs, range(near), block_index)
    for which, count in enumerate(counts):
        count_ref[which] = count
    begins = [base + count for count in counts]
    for turn in range(heads):
        chunk = lax.rem(own - turn + heads, heads)
        place = positions_of(first, chunk, tokens, grouped)
        top_ref[turn], total_ref[turn], mixed_ref[turn] = fold(
            None,
            pair_refs[::-1],
            queries_of(given_ref, chunk, tokens, grouped),
            first - (near - 1) * rows,
            place,
            begin_of(place, begins, base),
            scale,
        )


def far_kernel(count_ref, given_ref, top_ref, total_ref, mixed_ref, *refs, tokens, grouped, near, back, scale):
    pair_refs = refs[: back + 1 - near]
    heads = given_ref.shape[0]
    out_refs = refs[back + 1 - near : back + 1 - near + heads]
    new_total, new_mixed = refs[back + 1 - near + heads :]
    rows = tokens * heads
    block_index, own = lax.axis_index("blk"), lax.axis_index("head")
    first = block_index * rows
    base = jnp.maximum(block_index - back, 0) * rows

    @pl.when(block_index < near)
    def _():
        new_total[...] = total_ref[...]
        new_mixed[...] = mixed_ref[...]

    @pl.when(block_index >= near)
    def _():
        counts = count_labels(pair_refs, range(near, back + 1), block_index)
        begins = [base + count + count_ref[which] for which, count in enumerate(counts)]
        for turn in range(heads):
            chunk = lax.rem(own - turn + heads, heads)
            place = positions_of(first, chunk, tokens, grouped)
            _, new_total[turn], new_mixed[turn] = fold(
                (top_ref[turn], total_ref[turn], mixed_ref[turn]),
                pair_refs[::-1],
                queries_of(given_ref, chunk, tokens, grouped),
                first - back * rows,
                None,
                begin_of(place, begins, base),
                scale,
            )

    for turn in range(heads):
        normed = (new_mixed[turn] * (1.0 / new_total[turn])).astype(jnp.bfloat16).T
        for j in range(grouped):
            out_refs[turn][:, j * HEAD_SIZE : (j + 1) * HEAD_SIZE] = normed[
                j * tokens : (j + 1) * tokens
            ]


def assemble_kernel(*refs, heads):
    pieces, out_ref, semaphores = refs[:heads], refs[heads], refs[heads + 1]
    width = pieces[0].shape[1]
    own = lax.axis_index("head")
    copies = []
    for turn in range(heads):
        start = pl.multiple_of(lax.rem(own + turn, heads) * width, width)
        copies.append(
            pltpu.make_async_copy(
                pieces[turn], out_ref.at[:, pl.ds(start, width)], semaphores.at[turn]
            )
        )
        copies[-1].start()
    for copy in copies:
        copy.wait()


def vmem(count):
    return [pl.BlockSpec(memory_space=pltpu.VMEM)] * count


def cost(tiles, rows, width):
    return pl.CostEstimate(
        flops=4 * tiles * rows * rows * width,
        bytes_accessed=tiles * rows * width * 4,
        transcendentals=tiles * rows * rows,
    )


def call_near(given, pairs, tokens, grouped, near, scale):
    heads, lanes = given.shape[0], grouped * tokens
    state = [
        jax.ShapeDtypeStruct((heads, 1, lanes), jnp.float32),
        jax.ShapeDtypeStruct((heads, 1, lanes), jnp.float32),
        jax.ShapeDtypeStruct((heads, HEAD_SIZE, lanes), jnp.float32),
    ]
    counts, *state = pl.pallas_call(
        functools.partial(near_kernel, tokens=tokens, grouped=grouped, near=near, scale=scale),
        out_shape=[jax.ShapeDtypeStruct((LABELS - 1,), jnp.int32)] + state,
        in_specs=vmem(1 + near),
        out_specs=[pl.BlockSpec(memory_space=pltpu.SMEM)] + vmem(3),
        compiler_params=pltpu.CompilerParams(vmem_limit_bytes=16 << 20),
        cost_estimate=cost(near * heads, heads * tokens, HEAD_SIZE),
        name="attend_near",
    )(given, *pairs)
    return counts, state


def call_far(counts, given, state, pairs, tokens, grouped, near, back, scale):
    heads, lanes = given.shape[0], grouped * tokens
    return pl.pallas_call(
        functools.partial(
            far_kernel, tokens=tokens, grouped=grouped, near=near, back=back, scale=scale
        ),
        out_shape=[jax.ShapeDtypeStruct((tokens, grouped * HEAD_SIZE), jnp.bfloat16)] * heads,
        in_specs=[pl.BlockSpec(memory_space=pltpu.SMEM)] + vmem(4 + back + 1 - near),
        out_specs=vmem(heads),
        scratch_shapes=[
            pltpu.VMEM((heads, 1, lanes), jnp.float32),
            pltpu.VMEM((heads, HEAD_SIZE, lanes), jnp.float32),
        ],
        compiler_params=pltpu.CompilerParams(vmem_limit_bytes=16 << 20),
        cost_estimate=cost((back + 1 - near) * heads, heads * tokens, HEAD_SIZE),
        name="attend_far",
    )(counts, given, *state, *pairs)


def per_device(queries, keys_values, segment_ids):
    sections = lax.axis_size("section")
    blocks = lax.axis_size("blk")
    heads = lax.axis_size("head")
    tokens = queries.shape[1]
    rows = tokens * heads
    kv_width = keys_values.shape[2] // heads
    q_width = queries.shape[2] // heads
    grouped = q_width // HEAD_SIZE
    back = min(blocks - 1, -(-LONGEST_SEGMENT // rows))
    near = min(NEAR, back)
    scale = math.log2(math.e) / math.sqrt(HEAD_SIZE)

    parts = 1 + q_width // kv_width
    prepared = pl.pallas_call(
        functools.partial(prepare_kernel, heads=heads),
        out_shape=jax.ShapeDtypeStruct(
            (heads, parts * tokens + LABEL_ROWS, kv_width), jnp.bfloat16
        ),
        in_specs=[pl.BlockSpec(memory_space=pltpu.HBM)] * 3,
        out_specs=pl.BlockSpec(memory_space=pltpu.HBM),
        scratch_shapes=[
            pltpu.VMEM((1, tokens), jnp.int32),
            pltpu.VMEM((LABEL_ROWS, kv_width), jnp.float32),
            pltpu.VMEM((LABEL_ROWS, kv_width), jnp.bfloat16),
            pltpu.SemaphoreType.DMA((1 + heads * (parts + 1),)),
        ],
        compiler_params=pltpu.CompilerParams(vmem_limit_bytes=PREPARE_VMEM),
        name="prepare",
    )(keys_values[0], segment_ids, queries[0])
    given = lax.all_to_all(prepared, "head", split_axis=0, concat_axis=0, tiled=True)
    own_pairs = pl.pallas_call(
        functools.partial(pack_kernel, tokens=tokens),
        out_shape=jax.ShapeDtypeStruct((2 * HEAD_SIZE + LABEL_ROWS, rows), jnp.bfloat16),
        in_specs=vmem(1),
        out_specs=vmem(1)[0],
        scratch_shapes=[pltpu.VMEM((LABEL_ROWS, kv_width), jnp.float32)],
        compiler_params=pltpu.CompilerParams(vmem_limit_bytes=4 << 20),
        name="pack",
    )(given)
    earlier = [
        lax.ppermute(own_pairs, "blk", [(i, i + d) for i in range(blocks - d)])
        for d in range(1, back + 1)
    ]

    counts, state = call_near(given, [own_pairs, *earlier[: near - 1]], tokens, grouped, near, scale)

    def index(section, block, head):
        return ((section % sections) * blocks + block) * heads + head % heads

    attended = call_far(
        counts, given, state, earlier[near - 1 :], tokens, grouped, near, back, scale
    )
    received = [None] * heads
    for turn in SEND_ORDER:
        route = [
            (index(s, b, h), index(s + 1, b, h - turn))
            for s in range(sections)
            for b in range(blocks)
            for h in range(heads)
        ]
        received[turn] = lax.ppermute(attended[turn], ("section", "blk", "head"), route)
    result = pl.pallas_call(
        functools.partial(assemble_kernel, heads=heads),
        out_shape=jax.ShapeDtypeStruct(queries.shape[1:], jnp.bfloat16),
        in_specs=vmem(heads),
        out_specs=pl.BlockSpec(memory_space=pl.ANY),
        scratch_shapes=[pltpu.SemaphoreType.DMA((heads,))],
        compiler_params=pltpu.CompilerParams(vmem_limit_bytes=4 << 20),
        name="assemble",
    )(*received)
    return result[None]


def solution(mesh):
    return jax.shard_map(
        per_device,
        mesh=mesh,
        in_specs=(
            P("section", ("blk", "head"), None),
            P("section", ("blk", "head"), None),
            P("section", ("blk", "head")),
        ),
        out_specs=P("section", ("blk", "head"), None),
        check_vma=False,
    )
```

time: 97.5 us -> 99.1 us (1.016)
  the two profiles are of different devices: /device:TPU:76 before, /device:TPU:12 now
where the time goes in v2:
time: 99.1 us; the launch traced here: 98.7 us
  waiting for transfers between devices  28.7 us (29%)
  starting transfers between devices  28 us (28%)
  blocking collectives  22 us (22%)
  Pallas kernels  19.8 us (20%)
    all_to_all x1, blocking collectives, per_device(): lax.all_to_all(prepared, 'head', split_axis=0, concat_axis=0, tiled=True)  22 us
    ppermute x6, waiting for transfers between devices, per_device(): lax.ppermute(own_pairs, 'blk', [(i, i + d) for i in range(blocks - d)])  21.8 us
    ppermute x4, starting transfers between devices, per_device(): lax.ppermute(attended[turn], ('section', 'blk', 'head'), route)  19.1 us
    pallas_call x1, Pallas kernels, per_device(): pl.pallas_call(functools.partial(prepare_kernel, heads=heads), out_shape=...  13.2 us
    ppermute x6, starting transfers between devices, per_device(): lax.ppermute(own_pairs, 'blk', [(i, i + d) for i in range(blocks - d)])  8.95 us
    ppermute x4, waiting for transfers between devices, per_device(): lax.ppermute(attended[turn], ('section', 'blk', 'head'), route)  6.97 us
    pallas_call x1, Pallas kernels, call_far(): pl.pallas_call(functools.partial(far_kernel, tokens=tokens, grouped=group...  3.52 us
    pallas_call x1, Pallas kernels, call_near(): pl.pallas_call(functools.partial(near_kernel, tokens=tokens, grouped=grou...  2.31 us
  transfers between devices with their start and end apart: 10, of which 7 were waited for; matrix products, arithmetic and copies ran while one was open for 0% of the time, Pallas kernels for 2%

profile of v2, /device:TPU:12, one launch (start us, length us, event | category | flops | bytes accessed | tf_op | source)
XLA Modules:
  0.0 98.7 jit_solution(5932816406437129924)
XLA Ops:
  0.0 13.2 %prepare.1 = bf16[4,200,256]{2,1,0:T(8,128)(2,1)} custom-call(bf16[64,1024]{1,0:T(8,128)(2,1)} %bitcast.4, s32[1,64]{1,0:T(1,128)} %label_ref.1, bf16[64,2048]{1,0:T(8,128)(2,1)} %bitcast.3), custom_call_target="tpu_custom_call" | custom-call | tf_op jit(solution)/shard_map/prepare/pallas_call | solution.py:285
  13.2 22.0 %all_to_all.5.given_ref = bf16[4,200,256]{2,1,0:T(8,128)(2,1)S(1)} all-to-all(bf16[4,200,256]{2,1,0:T(8,128)(2,1)} %prepare.1), channel_id=1, replica_groups=mesh['section'=32,'blk'=8,'head'=4] {'head'}, dimensions={0} | all-to-all | bytes 819200 | tf_op jit(solution)/shard_map/all_to_all | solution.py:301
  35.2 0.1 pack.1.refs_0_
  35.3 2.5 %collective-permute-start = (bf16[264,256]{1,0:T(8,128)(2,1)S(1)}, bf16[264,256]{1,0:T(8,128)(2,1)S(1)}, u32[]{:S(2)}, u32[]{:S(2)}) collective-permute-start(bf16[264,256]{1,0:T(8,128)(2,1)S(1)} %pack.1.refs_0_), channel_id=1, source_target_pairs={{0,4},{4,8},{8,12},{12,16},{16,20},{20,24},{24,28},{1,5},{5,9},{9,... | collective-permute-start | bytes 405512 | tf_op jit(solution)/shard_map/ppermute | solution.py:312
  37.8 1.3 %collective-permute-start.1 = (bf16[264,256]{1,0:T(8,128)(2,1)S(1)}, bf16[264,256]{1,0:T(8,128)(2,1)S(1)}, u32[]{:S(2)}, u32[]{:S(2)}) collective-permute-start(bf16[264,256]{1,0:T(8,128)(2,1)S(1)} %pack.1.refs_0_), channel_id=1, source_target_pairs={{0,8},{4,12},{8,16},{12,20},{16,24},{20,28},{1,9},{5,13},{9,17},{1... | collective-permute-start | bytes 405512 | tf_op jit(solution)/shard_map/ppermute | solution.py:312
  39.1 1.3 %collective-permute-start.2 = (bf16[264,256]{1,0:T(8,128)(2,1)S(1)}, bf16[264,256]{1,0:T(8,128)(2,1)S(1)}, u32[]{:S(2)}, u32[]{:S(2)}) collective-permute-start(bf16[264,256]{1,0:T(8,128)(2,1)S(1)} %pack.1.refs_0_), channel_id=1, source_target_pairs={{0,12},{4,16},{8,20},{12,24},{16,28},{1,13},{5,17},{9,21},{13,25},... | collective-permute-start | bytes 405512 | tf_op jit(solution)/shard_map/ppermute | solution.py:312
  40.4 1.3 %collective-permute-start.3 = (bf16[264,256]{1,0:T(8,128)(2,1)S(1)}, bf16[264,256]{1,0:T(8,128)(2,1)S(1)}, u32[]{:S(2)}, u32[]{:S(2)}) collective-permute-start(bf16[264,256]{1,0:T(8,128)(2,1)S(1)} %pack.1.refs_0_), channel_id=1, source_target_pairs={{0,16},{4,20},{8,24},{12,28},{1,17},{5,21},{9,25},{13,29},{2,18},{... | collective-permute-start | bytes 405512 | tf_op jit(solution)/shard_map/ppermute | solution.py:312
  41.7 1.3 %collective-permute-start.4 = (bf16[264,256]{1,0:T(8,128)(2,1)S(1)}, bf16[264,256]{1,0:T(8,128)(2,1)S(1)}, u32[]{:S(2)}, u32[]{:S(2)}) collective-permute-start(bf16[264,256]{1,0:T(8,128)(2,1)S(1)} %pack.1.refs_0_), channel_id=1, source_target_pairs={{0,20},{4,24},{8,28},{1,21},{5,25},{9,29},{2,22},{6,26},{10,30},{3... | collective-permute-start | bytes 405512 | tf_op jit(solution)/shard_map/ppermute | solution.py:312
  43.0 2.0 %collective-permute-done.refs_1_ = bf16[264,256]{1,0:T(8,128)(2,1)S(1)} collective-permute-done((bf16[264,256]{1,0:T(8,128)(2,1)S(1)}, bf16[264,256]{1,0:T(8,128)(2,1)S(1)}, u32[]{:S(2)}, u32[]{:S(2)}) %collective-permute-start) | collective-permute-done | bytes 135200 | tf_op jit(solution)/shard_map/ppermute | solution.py:312
  45.0 1.3 %collective-permute-start.5 = (bf16[264,256]{1,0:T(8,128)(2,1)S(1)}, bf16[264,256]{1,0:T(8,128)(2,1)S(1)}, u32[]{:S(2)}, u32[]{:S(2)}) collective-permute-start(bf16[264,256]{1,0:T(8,128)(2,1)S(1)} %pack.1.refs_0_), channel_id=1, source_target_pairs={{0,24},{4,28},{1,25},{5,29},{2,26},{6,30},{3,27},{7,31},{32,56},{3... | collective-permute-start | bytes 405512 | tf_op jit(solution)/shard_map/ppermute | solution.py:312
  46.2 2.9 %collective-permute-done.1.refs_2_ = bf16[264,256]{1,0:T(8,128)(2,1)S(1)} collective-permute-done((bf16[264,256]{1,0:T(8,128)(2,1)S(1)}, bf16[264,256]{1,0:T(8,128)(2,1)S(1)}, u32[]{:S(2)}, u32[]{:S(2)}) %collective-permute-start.1) | collective-permute-done | bytes 135200 | tf_op jit(solution)/shard_map/ppermute | solution.py:312
  49.1 2.3 %attend_near.1 = (s32[3]{0:T(128)S(1)}, f32[4,1,256]{2,1,0:T(1,128)S(1)}, f32[4,1,256]{2,1,0:T(1,128)S(1)}, f32[4,128,256]{2,1,0:T(8,128)S(1)}) custom-call(bf16[4,200,256]{2,1,0:T(8,128)(2,1)S(1)} %all_to_all.5.given_ref, bf16[264,256]{1,0:T(8,128)(2,1)S(1)} %pack.1.refs_0_, bf16[264,256]{1,0:T(8,128)(2,1)S(1)} %collective-permute-done.refs_1_, ...), custom_call_target="tpu_custom_call" | custom-call | flops 402653184 | bytes 1572864 | tf_op jit(solution)/shard_map/attend_near/pallas_call | solution.py:240
  51.4 14.0 %collective-permute-done.2.refs_0_ = bf16[264,256]{1,0:T(8,128)(2,1)S(1)} collective-permute-done((bf16[264,256]{1,0:T(8,128)(2,1)S(1)}, bf16[264,256]{1,0:T(8,128)(2,1)S(1)}, u32[]{:S(2)}, u32[]{:S(2)}) %collective-permute-start.2) | collective-permute-done | bytes 135200 | tf_op jit(solution)/shard_map/ppermute | solution.py:312
  65.4 0.0 collective-permute-done.3.refs_1_
  65.4 0.0 collective-permute-done.4.refs_2_
  65.4 3.0 %collective-permute-done.5.refs_3_ = bf16[264,256]{1,0:T(8,128)(2,1)S(1)} collective-permute-done((bf16[264,256]{1,0:T(8,128)(2,1)S(1)}, bf16[264,256]{1,0:T(8,128)(2,1)S(1)}, u32[]{:S(2)}, u32[]{:S(2)}) %collective-permute-start.5) | collective-permute-done | bytes 135200 | tf_op jit(solution)/shard_map/ppermute | solution.py:312
  68.4 3.5 %attend_far.1 = (bf16[64,512]{1,0:T(8,128)(2,1)S(1)}, bf16[64,512]{1,0:T(8,128)(2,1)S(1)}, bf16[64,512]{1,0:T(8,128)(2,1)S(1)}, bf16[64,512]{1,0:T(8,128)(2,1)S(1)}) custom-call(s32[3]{0:T(128)S(1)} %get-tuple-element.13.count_ref, bf16[4,200,256]{2,1,0:T(8,128)(2,1)S(1)} %all_to_all.5.given_ref, f32[4,1,256]{2,1,0:T(1,128)S(1)} %get-tuple-element.14.top_ref, ...), custom_call_target="tpu_custom_call" | custom-call | flops 536870912 | bytes 2097152 | tf_op jit(solution)/shard_map/attend_far/pallas_call | solution.py:254
  71.9 1.9 %collective-permute-start.6 = (bf16[64,512]{1,0:T(8,128)(2,1)S(1)}, bf16[64,512]{1,0:T(8,128)(2,1)S(1)}, u32[]{:S(2)}, u32[]{:S(2)}) collective-permute-start(bf16[64,512]{1,0:T(8,128)(2,1)S(1)} %get-tuple-element.17), channel_id=1, source_target_pairs={{0,32},{1,33},{2,34},{3,35},{4,36},{5,37},{6,38},{7,39},{8,40},{9,... | collective-permute-start | bytes 196616 | tf_op jit(solution)/shard_map/ppermute | solution.py:332
  73.8 13.3 %collective-permute-start.7 = (bf16[64,512]{1,0:T(8,128)(2,1)S(1)}, bf16[64,512]{1,0:T(8,128)(2,1)S(1)}, u32[]{:S(2)}, u32[]{:S(2)}) collective-permute-start(bf16[64,512]{1,0:T(8,128)(2,1)S(1)} %get-tuple-element.18), channel_id=1, source_target_pairs={{0,35},{1,32},{2,33},{3,34},{4,39},{5,36},{6,37},{7,38},{8,43},{9,... | collective-permute-start | bytes 196616 | tf_op jit(solution)/shard_map/ppermute | solution.py:332
  87.1 1.9 %collective-permute-start.8 = (bf16[64,512]{1,0:T(8,128)(2,1)S(1)}, bf16[64,512]{1,0:T(8,128)(2,1)S(1)}, u32[]{:S(2)}, u32[]{:S(2)}) collective-permute-start(bf16[64,512]{1,0:T(8,128)(2,1)S(1)} %get-tuple-element.19), channel_id=1, source_target_pairs={{0,34},{1,35},{2,32},{3,33},{4,38},{5,39},{6,36},{7,37},{8,42},{9,... | collective-permute-start | bytes 196616 | tf_op jit(solution)/shard_map/ppermute | solution.py:332
  89.1 1.9 %collective-permute-start.9 = (bf16[64,512]{1,0:T(8,128)(2,1)S(1)}, bf16[64,512]{1,0:T(8,128)(2,1)S(1)}, u32[]{:S(2)}, u32[]{:S(2)}) collective-permute-start(bf16[64,512]{1,0:T(8,128)(2,1)S(1)} %get-tuple-element.20), channel_id=1, source_target_pairs={{0,33},{1,34},{2,35},{3,32},{4,37},{5,38},{6,39},{7,36},{8,41},{9,... | collective-permute-start | bytes 196616 | tf_op jit(solution)/shard_map/ppermute | solution.py:332
  91.0 0.0 collective-permute-done.6.refs_0_
  91.0 0.2 collective-permute-done.7.refs_1_
  91.2 5.8 %collective-permute-done.8.refs_2_ = bf16[64,512]{1,0:T(8,128)(2,1)S(1)} collective-permute-done((bf16[64,512]{1,0:T(8,128)(2,1)S(1)}, bf16[64,512]{1,0:T(8,128)(2,1)S(1)}, u32[]{:S(2)}, u32[]{:S(2)}) %collective-permute-start.8) | collective-permute-done | bytes 65568 | tf_op jit(solution)/shard_map/ppermute | solution.py:332
  97.0 1.0 %collective-permute-done.9.refs_3_ = bf16[64,512]{1,0:T(8,128)(2,1)S(1)} collective-permute-done((bf16[64,512]{1,0:T(8,128)(2,1)S(1)}, bf16[64,512]{1,0:T(8,128)(2,1)S(1)}, u32[]{:S(2)}, u32[]{:S(2)}) %collective-permute-start.9) | collective-permute-done | bytes 65568 | tf_op jit(solution)/shard_map/ppermute | solution.py:332
  98.0 0.7 assemble.1
Async XLA Ops:
  35.3 9.7 %collective-permute-start = (bf16[264,256]{1,0:T(8,128)(2,1)S(1)}, bf16[264,256]{1,0:T(8,128)(2,1)S(1)}, u32[]{:S(2)}, u32[]{:S(2)}) collective-permute-start(bf16[264,256]{1,0:T(8,128)(2,1)S(1)} %pack.1.refs_0_), channel_id=1, source_target_pairs={{0,4},{4,8},{8,12},{12,16},{16,20},{20,24},{24,28},{1,5},{5,9},{9,... | collective-permute-start | bytes 405512 | tf_op jit(solution)/shard_map/ppermute | solution.py:312
  37.8 11.3 %collective-permute-start.1 = (bf16[264,256]{1,0:T(8,128)(2,1)S(1)}, bf16[264,256]{1,0:T(8,128)(2,1)S(1)}, u32[]{:S(2)}, u32[]{:S(2)}) collective-permute-start(bf16[264,256]{1,0:T(8,128)(2,1)S(1)} %pack.1.refs_0_), channel_id=1, source_target_pairs={{0,8},{4,12},{8,16},{12,20},{16,24},{20,28},{1,9},{5,13},{9,17},{1... | collective-permute-start | bytes 405512 | tf_op jit(solution)/shard_map/ppermute | solution.py:312
  39.1 26.3 %collective-permute-start.2 = (bf16[264,256]{1,0:T(8,128)(2,1)S(1)}, bf16[264,256]{1,0:T(8,128)(2,1)S(1)}, u32[]{:S(2)}, u32[]{:S(2)}) collective-permute-start(bf16[264,256]{1,0:T(8,128)(2,1)S(1)} %pack.1.refs_0_), channel_id=1, source_target_pairs={{0,12},{4,16},{8,20},{12,24},{16,28},{1,13},{5,17},{9,21},{13,25},... | collective-permute-start | bytes 405512 | tf_op jit(solution)/shard_map/ppermute | solution.py:312
  40.4 25.0 %collective-permute-start.3 = (bf16[264,256]{1,0:T(8,128)(2,1)S(1)}, bf16[264,256]{1,0:T(8,128)(2,1)S(1)}, u32[]{:S(2)}, u32[]{:S(2)}) collective-permute-start(bf16[264,256]{1,0:T(8,128)(2,1)S(1)} %pack.1.refs_0_), channel_id=1, source_target_pairs={{0,16},{4,20},{8,24},{12,28},{1,17},{5,21},{9,25},{13,29},{2,18},{... | collective-permute-start | bytes 405512 | tf_op jit(solution)/shard_map/ppermute | solution.py:312
  41.7 23.7 %collective-permute-start.4 = (bf16[264,256]{1,0:T(8,128)(2,1)S(1)}, bf16[264,256]{1,0:T(8,128)(2,1)S(1)}, u32[]{:S(2)}, u32[]{:S(2)}) collective-permute-start(bf16[264,256]{1,0:T(8,128)(2,1)S(1)} %pack.1.refs_0_), channel_id=1, source_target_pairs={{0,20},{4,24},{8,28},{1,21},{5,25},{9,29},{2,22},{6,26},{10,30},{3... | collective-permute-start | bytes 405512 | tf_op jit(solution)/shard_map/ppermute | solution.py:312
  45.0 23.4 %collective-permute-start.5 = (bf16[264,256]{1,0:T(8,128)(2,1)S(1)}, bf16[264,256]{1,0:T(8,128)(2,1)S(1)}, u32[]{:S(2)}, u32[]{:S(2)}) collective-permute-start(bf16[264,256]{1,0:T(8,128)(2,1)S(1)} %pack.1.refs_0_), channel_id=1, source_target_pairs={{0,24},{4,28},{1,25},{5,29},{2,26},{6,30},{3,27},{7,31},{32,56},{3... | collective-permute-start | bytes 405512 | tf_op jit(solution)/shard_map/ppermute | solution.py:312
  71.9 19.1 %collective-permute-start.6 = (bf16[64,512]{1,0:T(8,128)(2,1)S(1)}, bf16[64,512]{1,0:T(8,128)(2,1)S(1)}, u32[]{:S(2)}, u32[]{:S(2)}) collective-permute-start(bf16[64,512]{1,0:T(8,128)(2,1)S(1)} %get-tuple-element.17), channel_id=1, source_target_pairs={{0,32},{1,33},{2,34},{3,35},{4,36},{5,37},{6,38},{7,39},{8,40},{9,... | collective-permute-start | bytes 196616 | tf_op jit(solution)/shard_map/ppermute | solution.py:332
  73.8 17.4 %collective-permute-start.7 = (bf16[64,512]{1,0:T(8,128)(2,1)S(1)}, bf16[64,512]{1,0:T(8,128)(2,1)S(1)}, u32[]{:S(2)}, u32[]{:S(2)}) collective-permute-start(bf16[64,512]{1,0:T(8,128)(2,1)S(1)} %get-tuple-element.18), channel_id=1, source_target_pairs={{0,35},{1,32},{2,33},{3,34},{4,39},{5,36},{6,37},{7,38},{8,43},{9,... | collective-permute-start | bytes 196616 | tf_op jit(solution)/shard_map/ppermute | solution.py:332
  87.1 9.8 %collective-permute-start.8 = (bf16[64,512]{1,0:T(8,128)(2,1)S(1)}, bf16[64,512]{1,0:T(8,128)(2,1)S(1)}, u32[]{:S(2)}, u32[]{:S(2)}) collective-permute-start(bf16[64,512]{1,0:T(8,128)(2,1)S(1)} %get-tuple-element.19), channel_id=1, source_target_pairs={{0,34},{1,35},{2,32},{3,33},{4,38},{5,39},{6,36},{7,37},{8,42},{9,... | collective-permute-start | bytes 196616 | tf_op jit(solution)/shard_map/ppermute | solution.py:332
  89.1 8.9 %collective-permute-start.9 = (bf16[64,512]{1,0:T(8,128)(2,1)S(1)}, bf16[64,512]{1,0:T(8,128)(2,1)S(1)}, u32[]{:S(2)}, u32[]{:S(2)}) collective-permute-start(bf16[64,512]{1,0:T(8,128)(2,1)S(1)} %get-tuple-element.20), channel_id=1, source_target_pairs={{0,33},{1,34},{2,35},{3,32},{4,37},{5,38},{6,39},{7,36},{8,41},{9,... | collective-permute-start | bytes 196616 | tf_op jit(solution)/shard_map/ppermute | solution.py:332

commit v3 on v2

v3 whole, which is shorter than its diff:
```python
import functools
import math

import jax
import jax.numpy as jnp
from jax import lax
from jax.experimental import pallas as pl
from jax.experimental.pallas import tpu as pltpu
from jax.sharding import PartitionSpec as P

HEAD_SIZE = 128
NEG_FILL = -1e30
LONGEST_SEGMENT = 1536
LABELS = 4
LABEL_ROWS = 8
NO_LABEL = 9.0
NEAR = (0, 1, 4, 5, 6)
FAR = (2, 3)
PREPARE_VMEM = 56 << 20
SEND_ORDER = (2, 3, 1, 0)


def prepare_kernel(kv_ref, label_ref, q_ref, out_ref, label_rows, *, heads):
    tokens = kv_ref.shape[0]
    width = kv_ref.shape[1] // heads
    q_width = q_ref.shape[1] // heads
    label_rows[...] = jnp.full(label_rows.shape, NO_LABEL, jnp.float32)
    label_rows[0:1, 0:tokens] = label_ref[...].astype(jnp.float32)
    for which in range(heads):
        out_ref[which, 0:tokens, :] = kv_ref[:, which * width : (which + 1) * width]
        for part in range(q_width // width):
            start = which * q_width + part * width
            out_ref[which, (1 + part) * tokens : (2 + part) * tokens, :] = q_ref[
                :, start : start + width
            ]
        out_ref[which, out_ref.shape[1] - LABEL_ROWS :, :] = label_rows[...].astype(jnp.bfloat16)


def pack_kernel(given_ref, out_ref, label_rows, *, tokens):
    heads = given_ref.shape[0]
    rows = heads * tokens
    keys = given_ref[:, 0:tokens, 0:HEAD_SIZE].reshape(rows, HEAD_SIZE)
    values = given_ref[:, 0:tokens, HEAD_SIZE : 2 * HEAD_SIZE].reshape(rows, HEAD_SIZE)
    out_ref[0:HEAD_SIZE, :] = values.T
    for part in range(rows // HEAD_SIZE):
        out_ref[HEAD_SIZE : 2 * HEAD_SIZE, part * HEAD_SIZE : (part + 1) * HEAD_SIZE] = keys[
            part * HEAD_SIZE : (part + 1) * HEAD_SIZE
        ]
    label_rows[...] = jnp.zeros(label_rows.shape, jnp.float32)
    found = given_ref[:, given_ref.shape[1] - LABEL_ROWS :, :].astype(jnp.float32)
    for label in range(1, LABELS):
        below = jnp.sum(jnp.where(found < label, 1.0, 0.0), axis=0)
        below = jnp.sum(jnp.sum(below, axis=0, keepdims=True), axis=1, keepdims=True)
        label_rows[label : label + 1, :] = jnp.broadcast_to(below, (1, rows))
    out_ref[2 * HEAD_SIZE :, :] = label_rows[...].astype(jnp.bfloat16)


def counts_of(ref):
    held = ref[2 * HEAD_SIZE :, :].astype(jnp.float32)
    return [held[label : label + 1] for label in range(1, LABELS)]


def keys_of(ref):
    held = ref[HEAD_SIZE : 2 * HEAD_SIZE, :]
    parts = held.shape[1] // HEAD_SIZE
    return jnp.concatenate(
        [held[:, part * HEAD_SIZE : (part + 1) * HEAD_SIZE] for part in range(parts)], axis=0
    )


def values_of(ref):
    return ref[0:HEAD_SIZE, :]


def queries_of(given_ref, chunk, tokens, grouped):
    parts = given_ref.shape[2] // HEAD_SIZE
    pieces = []
    for j in range(grouped):
        row, column = (1 + j // parts) * tokens, (j % parts) * HEAD_SIZE
        pieces.append(given_ref[chunk, row : row + tokens, column : column + HEAD_SIZE])
    return jnp.concatenate(pieces, axis=0)


def fold(state, distances, pair_refs, own_ref, given_ref, turn, tokens, grouped, scale):
    heads = given_ref.shape[0]
    rows, lanes = heads * tokens, grouped * tokens
    block_index, own = lax.axis_index("blk"), lax.axis_index("head")
    chunk = lax.rem(own - turn + heads, heads)
    place = chunk * tokens + lax.rem(lax.broadcasted_iota(jnp.int32, (1, lanes), 1), tokens)
    own_counts = counts_of(own_ref)
    keys = jnp.concatenate([keys_of(ref) for ref in pair_refs], axis=0)
    values = jnp.concatenate([values_of(ref) for ref in pair_refs], axis=1)
    scores = lax.dot_general(
        keys,
        queries_of(given_ref, chunk, tokens, grouped),
        (((1,), (1,)), ((), ())),
        preferred_element_type=jnp.float32,
    )
    key = lax.broadcasted_iota(jnp.int32, (rows, lanes), 0)
    masked = []
    for which, distance in enumerate(distances):
        begin = jnp.zeros((1, lanes), jnp.float32)
        for own_count, count in zip(own_counts, counts_of(pair_refs[which]), strict=True):
            inside = place.astype(jnp.float32) >= own_count
            begin = jnp.maximum(begin, jnp.where(inside, count, 0.0))
        begin = jnp.where(block_index >= distance, begin.astype(jnp.int32), rows)
        allowed = key >= begin
        if distance == 0:
            allowed = allowed & (key <= place)
        masked.append(jnp.where(allowed, scores[which * rows : (which + 1) * rows], NEG_FILL))
    scores = jnp.concatenate(masked, axis=0)
    top = jnp.max(scores, axis=0, keepdims=True)
    if state is not None:
        old, total, mixed = state
        top = jnp.maximum(old, top)
    weights = jnp.exp2((scores - top) * scale)
    added = jnp.sum(weights, axis=0, keepdims=True)
    moved = jnp.dot(values, weights.astype(jnp.bfloat16), preferred_element_type=jnp.float32)
    if state is None:
        return top, added, moved
    factor = jnp.exp2((old - top) * scale)
    return top, total * factor + added, mixed * factor + moved


def near_kernel(given_ref, *refs, distances, tokens, grouped, scale):
    pair_refs = refs[: len(distances)]
    top_ref, total_ref, mixed_ref = refs[len(distances) :]
    for turn in range(given_ref.shape[0]):
        top_ref[turn], total_ref[turn], mixed_ref[turn] = fold(
            None, distances, pair_refs, pair_refs[0], given_ref, turn, tokens, grouped, scale
        )


def far_kernel(
    given_ref, own_ref, top_ref, total_ref, mixed_ref, *refs, distances, tokens, grouped, scale
):
    heads = given_ref.shape[0]
    pair_refs = refs[: len(distances)]
    out_refs = refs[len(distances) : len(distances) + heads]
    new_total, new_mixed = refs[len(distances) + heads :]
    block_index = lax.axis_index("blk")

    @pl.when(block_index < min(distances))
    def _():
        new_total[...] = total_ref[...]
        new_mixed[...] = mixed_ref[...]

    @pl.when(block_index >= min(distances))
    def _():
        for turn in range(heads):
            _, new_total[turn], new_mixed[turn] = fold(
                (top_ref[turn], total_ref[turn], mixed_ref[turn]),
                distances,
                pair_refs,
                own_ref,
                given_ref,
                turn,
                tokens,
                grouped,
                scale,
            )

    for turn in range(heads):
        normed = (new_mixed[turn] * (1.0 / new_total[turn])).astype(jnp.bfloat16).T
        for j in range(grouped):
            out_refs[turn][:, j * HEAD_SIZE : (j + 1) * HEAD_SIZE] = normed[
                j * tokens : (j + 1) * tokens
            ]


def assemble_kernel(*refs, heads):
    pieces, out_ref, semaphores = refs[:heads], refs[heads], refs[heads + 1]
    width = pieces[0].shape[1]
    own = lax.axis_index("head")
    copies = []
    for turn in range(heads):
        start = pl.multiple_of(lax.rem(own + turn, heads) * width, width)
        copies.append(
            pltpu.make_async_copy(
                pieces[turn], out_ref.at[:, pl.ds(start, width)], semaphores.at[turn]
            )
        )
        copies[-1].start()
    for copy in copies:
        copy.wait()


def vmem(count):
    return [pl.BlockSpec(memory_space=pltpu.VMEM)] * count


def cost(tiles, rows, width):
    return pl.CostEstimate(
        flops=4 * tiles * rows * rows * width,
        bytes_accessed=tiles * rows * width * 4,
        transcendentals=tiles * rows * rows,
    )


def call_near(given, pairs, distances, tokens, grouped, scale):
    heads, lanes = given.shape[0], grouped * tokens
    return pl.pallas_call(
        functools.partial(
            near_kernel, distances=distances, tokens=tokens, grouped=grouped, scale=scale
        ),
        out_shape=[
            jax.ShapeDtypeStruct((heads, 1, lanes), jnp.float32),
            jax.ShapeDtypeStruct((heads, 1, lanes), jnp.float32),
            jax.ShapeDtypeStruct((heads, HEAD_SIZE, lanes), jnp.float32),
        ],
        in_specs=vmem(1 + len(distances)),
        out_specs=vmem(3),
        compiler_params=pltpu.CompilerParams(vmem_limit_bytes=16 << 20),
        cost_estimate=cost(len(distances) * heads, heads * tokens, HEAD_SIZE),
        name="attend_near",
    )(given, *pairs)


def call_far(given, own_pairs, state, pairs, distances, tokens, grouped, scale):
    heads, lanes = given.shape[0], grouped * tokens
    return pl.pallas_call(
        functools.partial(
            far_kernel, distances=distances, tokens=tokens, grouped=grouped, scale=scale
        ),
        out_shape=[jax.ShapeDtypeStruct((tokens, grouped * HEAD_SIZE), jnp.bfloat16)] * heads,
        in_specs=vmem(5 + len(distances)),
        out_specs=vmem(heads),
        scratch_shapes=[
            pltpu.VMEM((heads, 1, lanes), jnp.float32),
            pltpu.VMEM((heads, HEAD_SIZE, lanes), jnp.float32),
        ],
        compiler_params=pltpu.CompilerParams(vmem_limit_bytes=16 << 20),
        cost_estimate=cost(len(distances) * heads, heads * tokens, HEAD_SIZE),
        name="attend_far",
    )(given, own_pairs, *state, *pairs)


def per_device(queries, keys_values, segment_ids):
    sections = lax.axis_size("section")
    blocks = lax.axis_size("blk")
    heads = lax.axis_size("head")
    tokens = queries.shape[1]
    rows = tokens * heads
    kv_width = keys_values.shape[2] // heads
    q_width = queries.shape[2] // heads
    grouped = q_width // HEAD_SIZE
    back = min(blocks - 1, -(-LONGEST_SEGMENT // rows))
    scale = math.log2(math.e) / math.sqrt(HEAD_SIZE)

    parts = 1 + q_width // kv_width
    prepared = pl.pallas_call(
        functools.partial(prepare_kernel, heads=heads),
        out_shape=jax.ShapeDtypeStruct(
            (heads, parts * tokens + LABEL_ROWS, kv_width), jnp.bfloat16
        ),
        in_specs=vmem(3),
        out_specs=vmem(1)[0],
        scratch_shapes=[pltpu.VMEM((LABEL_ROWS, kv_width), jnp.float32)],
        compiler_params=pltpu.CompilerParams(vmem_limit_bytes=PREPARE_VMEM),
        name="prepare",
    )(keys_values[0], segment_ids, queries[0])
    given = lax.all_to_all(prepared, "head", split_axis=0, concat_axis=0, tiled=True)
    own_pairs = pl.pallas_call(
        functools.partial(pack_kernel, tokens=tokens),
        out_shape=jax.ShapeDtypeStruct((2 * HEAD_SIZE + LABEL_ROWS, rows), jnp.bfloat16),
        in_specs=vmem(1),
        out_specs=vmem(1)[0],
        scratch_shapes=[pltpu.VMEM((LABEL_ROWS, kv_width), jnp.float32)],
        compiler_params=pltpu.CompilerParams(vmem_limit_bytes=4 << 20),
        name="pack",
    )(given)
    pairs = {0: own_pairs}
    for d in [d for d in NEAR + FAR if 0 < d <= back]:
        route = [(i, i + d) for i in range(blocks - d)]
        pairs[d] = lax.ppermute(own_pairs, "blk", route)
    near = tuple(d for d in NEAR if d <= back)
    far = tuple(d for d in pairs if d not in near)
    state = call_near(given, [pairs[d] for d in near], near, tokens, grouped, scale)
    attended = call_far(
        given, own_pairs, state, [pairs[d] for d in far], far, tokens, grouped, scale
    )

    def index(section, block, head):
        return ((section % sections) * blocks + block) * heads + head % heads

    received = [None] * heads
    for turn in SEND_ORDER:
        route = [
            (index(s, b, h), index(s + 1, b, h - turn))
            for s in range(sections)
            for b in range(blocks)
            for h in range(heads)
        ]
        received[turn] = lax.ppermute(attended[turn], ("section", "blk", "head"), route)
    result = pl.pallas_call(
        functools.partial(assemble_kernel, heads=heads),
        out_shape=jax.ShapeDtypeStruct(queries.shape[1:], jnp.bfloat16),
        in_specs=vmem(heads),
        out_specs=pl.BlockSpec(memory_space=pl.ANY),
        scratch_shapes=[pltpu.SemaphoreType.DMA((heads,))],
        compiler_params=pltpu.CompilerParams(vmem_limit_bytes=4 << 20),
        name="assemble",
    )(*received)
    return result[None]


def solution(mesh):
    return jax.shard_map(
        per_device,
        mesh=mesh,
        in_specs=(
            P("section", ("blk", "head"), None),
            P("section", ("blk", "head"), None),
            P("section", ("blk", "head")),
        ),
        out_specs=P("section", ("blk", "head"), None),
        check_vma=False,
    )
```

time: 99.1 us -> 85.5 us (0.86)
  Pallas kernels: 19.8 us -> 7.98 us
  waiting for transfers between devices: 28.7 us -> 27 us
    pallas_call x1, Pallas kernels: 13.2 us -> 1.81 us  [per_device(): pl.pallas_call(functools.partial(prepare_kernel, heads=heads), out_shape=...]
    ppermute x6, waiting for transfers between devices: 21.8 us -> 20 us  [per_device(): pairs[d] = lax.ppermute(own_pairs, 'blk', route)]
  transfers between devices with their start and end apart: 10 -> 10, of which waited for: 7 -> 6; matrix products, arithmetic and copies ran while one was open for 0% -> 0% of each run, Pallas kernels for 2% -> 4%
where the time goes in v3:
time: 85.5 us; the launch traced here: 85.1 us
  starting transfers between devices  28 us (33%)
  waiting for transfers between devices  27 us (32%)
  blocking collectives  22 us (26%)
  Pallas kernels  7.98 us (9%)
    all_to_all x1, blocking collectives, per_device(): lax.all_to_all(prepared, 'head', split_axis=0, concat_axis=0, tiled=True)  22 us
    ppermute x6, waiting for transfers between devices, per_device(): pairs[d] = lax.ppermute(own_pairs, 'blk', route)  20 us
    ppermute x4, starting transfers between devices, per_device(): lax.ppermute(attended[turn], ('section', 'blk', 'head'), route)  19.1 us
    ppermute x6, starting transfers between devices, per_device(): pairs[d] = lax.ppermute(own_pairs, 'blk', route)  8.96 us
    ppermute x4, waiting for transfers between devices, per_device(): lax.ppermute(attended[turn], ('section', 'blk', 'head'), route)  6.97 us
    pallas_call x1, Pallas kernels, call_near(): pl.pallas_call(functools.partial(near_kernel, distances=distances, tokens...  3.42 us
    pallas_call x1, Pallas kernels, call_far(): pl.pallas_call(functools.partial(far_kernel, distances=distances, tokens=...  1.92 us
    pallas_call x1, Pallas kernels, per_device(): pl.pallas_call(functools.partial(prepare_kernel, heads=heads), out_shape=...  1.81 us
  transfers between devices with their start and end apart: 10, of which 6 were waited for; matrix products, arithmetic and copies ran while one was open for 0% of the time, Pallas kernels for 4%

profile of v3, /device:TPU:12, one launch (start us, length us, event | category | flops | bytes accessed | tf_op | source)
XLA Modules:
  0.0 85.1 jit_solution(9618299185766381216)
XLA Ops:
  0.0 1.8 %prepare.1 = bf16[4,200,256]{2,1,0:T(8,128)(2,1)} custom-call(bf16[64,1024]{1,0:T(8,128)(2,1)} %bitcast.4, s32[1,64]{1,0:T(1,128)} %label_ref.1, bf16[64,2048]{1,0:T(8,128)(2,1)} %bitcast.3), custom_call_target="tpu_custom_call" | custom-call | tf_op jit(solution)/shard_map/prepare/pallas_call | solution.py:251
  1.8 22.0 %all_to_all.5.given_ref = bf16[4,200,256]{2,1,0:T(8,128)(2,1)S(1)} all-to-all(bf16[4,200,256]{2,1,0:T(8,128)(2,1)} %prepare.1), channel_id=1, replica_groups=mesh['section'=32,'blk'=8,'head'=4] {'head'}, dimensions={0} | all-to-all | bytes 819200 | tf_op jit(solution)/shard_map/all_to_all | solution.py:262
  23.8 0.1 pack.1.refs_0_.own_ref
  23.9 2.5 %collective-permute-start = (bf16[264,256]{1,0:T(8,128)(2,1)S(1)}, bf16[264,256]{1,0:T(8,128)(2,1)S(1)}, u32[]{:S(2)}, u32[]{:S(2)}) collective-permute-start(bf16[264,256]{1,0:T(8,128)(2,1)S(1)} %pack.1.refs_0_.own_ref), channel_id=1, source_target_pairs={{0,4},{4,8},{8,12},{12,16},{16,20},{20,24},{24,28},{1,5},{5,9},{9,... | collective-permute-start | bytes 405512 | tf_op jit(solution)/shard_map/ppermute | solution.py:275
  26.5 1.3 %collective-permute-start.1 = (bf16[264,256]{1,0:T(8,128)(2,1)S(1)}, bf16[264,256]{1,0:T(8,128)(2,1)S(1)}, u32[]{:S(2)}, u32[]{:S(2)}) collective-permute-start(bf16[264,256]{1,0:T(8,128)(2,1)S(1)} %pack.1.refs_0_.own_ref), channel_id=1, source_target_pairs={{0,16},{4,20},{8,24},{12,28},{1,17},{5,21},{9,25},{13,29},{2,18},{... | collective-permute-start | bytes 405512 | tf_op jit(solution)/shard_map/ppermute | solution.py:275
  27.8 1.3 %collective-permute-start.2 = (bf16[264,256]{1,0:T(8,128)(2,1)S(1)}, bf16[264,256]{1,0:T(8,128)(2,1)S(1)}, u32[]{:S(2)}, u32[]{:S(2)}) collective-permute-start(bf16[264,256]{1,0:T(8,128)(2,1)S(1)} %pack.1.refs_0_.own_ref), channel_id=1, source_target_pairs={{0,20},{4,24},{8,28},{1,21},{5,25},{9,29},{2,22},{6,26},{10,30},{3... | collective-permute-start | bytes 405512 | tf_op jit(solution)/shard_map/ppermute | solution.py:275
  29.1 1.3 %collective-permute-start.3 = (bf16[264,256]{1,0:T(8,128)(2,1)S(1)}, bf16[264,256]{1,0:T(8,128)(2,1)S(1)}, u32[]{:S(2)}, u32[]{:S(2)}) collective-permute-start(bf16[264,256]{1,0:T(8,128)(2,1)S(1)} %pack.1.refs_0_.own_ref), channel_id=1, source_target_pairs={{0,24},{4,28},{1,25},{5,29},{2,26},{6,30},{3,27},{7,31},{32,56},{3... | collective-permute-start | bytes 405512 | tf_op jit(solution)/shard_map/ppermute | solution.py:275
  30.4 1.3 %collective-permute-start.4 = (bf16[264,256]{1,0:T(8,128)(2,1)S(1)}, bf16[264,256]{1,0:T(8,128)(2,1)S(1)}, u32[]{:S(2)}, u32[]{:S(2)}) collective-permute-start(bf16[264,256]{1,0:T(8,128)(2,1)S(1)} %pack.1.refs_0_.own_ref), channel_id=1, source_target_pairs={{0,8},{4,12},{8,16},{12,20},{16,24},{20,28},{1,9},{5,13},{9,17},{1... | collective-permute-start | bytes 405512 | tf_op jit(solution)/shard_map/ppermute | solution.py:275
  31.7 0.0 collective-permute-done.refs_1_
  31.7 1.3 %collective-permute-start.5 = (bf16[264,256]{1,0:T(8,128)(2,1)S(1)}, bf16[264,256]{1,0:T(8,128)(2,1)S(1)}, u32[]{:S(2)}, u32[]{:S(2)}) collective-permute-start(bf16[264,256]{1,0:T(8,128)(2,1)S(1)} %pack.1.refs_0_.own_ref), channel_id=1, source_target_pairs={{0,12},{4,16},{8,20},{12,24},{16,28},{1,13},{5,17},{9,21},{13,25},... | collective-permute-start | bytes 405512 | tf_op jit(solution)/shard_map/ppermute | solution.py:275
  33.0 7.8 %collective-permute-done.1.refs_2_ = bf16[264,256]{1,0:T(8,128)(2,1)S(1)} collective-permute-done((bf16[264,256]{1,0:T(8,128)(2,1)S(1)}, bf16[264,256]{1,0:T(8,128)(2,1)S(1)}, u32[]{:S(2)}, u32[]{:S(2)}) %collective-permute-start.1) | collective-permute-done | bytes 135200 | tf_op jit(solution)/shard_map/ppermute | solution.py:275
  40.8 4.2 %collective-permute-done.2.refs_3_ = bf16[264,256]{1,0:T(8,128)(2,1)S(1)} collective-permute-done((bf16[264,256]{1,0:T(8,128)(2,1)S(1)}, bf16[264,256]{1,0:T(8,128)(2,1)S(1)}, u32[]{:S(2)}, u32[]{:S(2)}) %collective-permute-start.2) | collective-permute-done | bytes 135200 | tf_op jit(solution)/shard_map/ppermute | solution.py:275
  45.0 7.9 %collective-permute-done.3.refs_4_ = bf16[264,256]{1,0:T(8,128)(2,1)S(1)} collective-permute-done((bf16[264,256]{1,0:T(8,128)(2,1)S(1)}, bf16[264,256]{1,0:T(8,128)(2,1)S(1)}, u32[]{:S(2)}, u32[]{:S(2)}) %collective-permute-start.3) | collective-permute-done | bytes 135200 | tf_op jit(solution)/shard_map/ppermute | solution.py:275
  52.9 3.4 %attend_near.1 = (f32[4,1,256]{2,1,0:T(1,128)S(1)}, f32[4,1,256]{2,1,0:T(1,128)S(1)}, f32[4,128,256]{2,1,0:T(8,128)S(1)}) custom-call(bf16[4,200,256]{2,1,0:T(8,128)(2,1)S(1)} %all_to_all.5.given_ref, bf16[264,256]{1,0:T(8,128)(2,1)S(1)} %pack.1.refs_0_.own_ref, bf16[264,256]{1,0:T(8,128)(2,1)S(1)} %collective-permute-done.refs_1_, ...), custom_call_target="tpu_custom_call" | custom-call | flops 671088640 | bytes 2621440 | tf_op jit(solution)/shard_map/attend_near/pallas_call | solution.py:202
  56.4 0.0 collective-permute-done.4.refs_0_
  56.4 0.0 collective-permute-done.5.refs_1_
  56.4 1.9 %attend_far.1 = (bf16[64,512]{1,0:T(8,128)(2,1)S(1)}, bf16[64,512]{1,0:T(8,128)(2,1)S(1)}, bf16[64,512]{1,0:T(8,128)(2,1)S(1)}, bf16[64,512]{1,0:T(8,128)(2,1)S(1)}) custom-call(bf16[4,200,256]{2,1,0:T(8,128)(2,1)S(1)} %all_to_all.5.given_ref, bf16[264,256]{1,0:T(8,128)(2,1)S(1)} %pack.1.refs_0_.own_ref, f32[4,1,256]{2,1,0:T(1,128)S(1)} %get-tuple-element.12.top_ref, ...), custom_call_target="tpu_custom_call" | custom-call | flops 268435456 | bytes 1048576 | tf_op jit(solution)/shard_map/attend_far/pallas_call | solution.py:221
  58.3 1.9 %collective-permute-start.6 = (bf16[64,512]{1,0:T(8,128)(2,1)S(1)}, bf16[64,512]{1,0:T(8,128)(2,1)S(1)}, u32[]{:S(2)}, u32[]{:S(2)}) collective-permute-start(bf16[64,512]{1,0:T(8,128)(2,1)S(1)} %get-tuple-element.15), channel_id=1, source_target_pairs={{0,32},{1,33},{2,34},{3,35},{4,36},{5,37},{6,38},{7,39},{8,40},{9,... | collective-permute-start | bytes 196616 | tf_op jit(solution)/shard_map/ppermute | solution.py:294
  60.2 13.3 %collective-permute-start.7 = (bf16[64,512]{1,0:T(8,128)(2,1)S(1)}, bf16[64,512]{1,0:T(8,128)(2,1)S(1)}, u32[]{:S(2)}, u32[]{:S(2)}) collective-permute-start(bf16[64,512]{1,0:T(8,128)(2,1)S(1)} %get-tuple-element.16), channel_id=1, source_target_pairs={{0,35},{1,32},{2,33},{3,34},{4,39},{5,36},{6,37},{7,38},{8,43},{9,... | collective-permute-start | bytes 196616 | tf_op jit(solution)/shard_map/ppermute | solution.py:294
  73.6 1.9 %collective-permute-start.8 = (bf16[64,512]{1,0:T(8,128)(2,1)S(1)}, bf16[64,512]{1,0:T(8,128)(2,1)S(1)}, u32[]{:S(2)}, u32[]{:S(2)}) collective-permute-start(bf16[64,512]{1,0:T(8,128)(2,1)S(1)} %get-tuple-element.17), channel_id=1, source_target_pairs={{0,34},{1,35},{2,32},{3,33},{4,38},{5,39},{6,36},{7,37},{8,42},{9,... | collective-permute-start | bytes 196616 | tf_op jit(solution)/shard_map/ppermute | solution.py:294
  75.5 1.9 %collective-permute-start.9 = (bf16[64,512]{1,0:T(8,128)(2,1)S(1)}, bf16[64,512]{1,0:T(8,128)(2,1)S(1)}, u32[]{:S(2)}, u32[]{:S(2)}) collective-permute-start(bf16[64,512]{1,0:T(8,128)(2,1)S(1)} %get-tuple-element.18), channel_id=1, source_target_pairs={{0,33},{1,34},{2,35},{3,32},{4,37},{5,38},{6,39},{7,36},{8,41},{9,... | collective-permute-start | bytes 196616 | tf_op jit(solution)/shard_map/ppermute | solution.py:294
  77.4 0.0 collective-permute-done.6.refs_0_
  77.4 0.2 collective-permute-done.7.refs_1_
  77.6 5.8 %collective-permute-done.8.refs_2_ = bf16[64,512]{1,0:T(8,128)(2,1)S(1)} collective-permute-done((bf16[64,512]{1,0:T(8,128)(2,1)S(1)}, bf16[64,512]{1,0:T(8,128)(2,1)S(1)}, u32[]{:S(2)}, u32[]{:S(2)}) %collective-permute-start.8) | collective-permute-done | bytes 65568 | tf_op jit(solution)/shard_map/ppermute | solution.py:294
  83.4 1.0 %collective-permute-done.9.refs_3_ = bf16[64,512]{1,0:T(8,128)(2,1)S(1)} collective-permute-done((bf16[64,512]{1,0:T(8,128)(2,1)S(1)}, bf16[64,512]{1,0:T(8,128)(2,1)S(1)}, u32[]{:S(2)}, u32[]{:S(2)}) %collective-permute-start.9) | collective-permute-done | bytes 65568 | tf_op jit(solution)/shard_map/ppermute | solution.py:294
  84.4 0.7 assemble.1
Async XLA Ops:
  23.9 7.7 %collective-permute-start = (bf16[264,256]{1,0:T(8,128)(2,1)S(1)}, bf16[264,256]{1,0:T(8,128)(2,1)S(1)}, u32[]{:S(2)}, u32[]{:S(2)}) collective-permute-start(bf16[264,256]{1,0:T(8,128)(2,1)S(1)} %pack.1.refs_0_.own_ref), channel_id=1, source_target_pairs={{0,4},{4,8},{8,12},{12,16},{16,20},{20,24},{24,28},{1,5},{5,9},{9,... | collective-permute-start | bytes 405512 | tf_op jit(solution)/shard_map/ppermute | solution.py:275
  26.5 14.4 %collective-permute-start.1 = (bf16[264,256]{1,0:T(8,128)(2,1)S(1)}, bf16[264,256]{1,0:T(8,128)(2,1)S(1)}, u32[]{:S(2)}, u32[]{:S(2)}) collective-permute-start(bf16[264,256]{1,0:T(8,128)(2,1)S(1)} %pack.1.refs_0_.own_ref), channel_id=1, source_target_pairs={{0,16},{4,20},{8,24},{12,28},{1,17},{5,21},{9,25},{13,29},{2,18},{... | collective-permute-start | bytes 405512 | tf_op jit(solution)/shard_map/ppermute | solution.py:275
  27.8 17.3 %collective-permute-start.2 = (bf16[264,256]{1,0:T(8,128)(2,1)S(1)}, bf16[264,256]{1,0:T(8,128)(2,1)S(1)}, u32[]{:S(2)}, u32[]{:S(2)}) collective-permute-start(bf16[264,256]{1,0:T(8,128)(2,1)S(1)} %pack.1.refs_0_.own_ref), channel_id=1, source_target_pairs={{0,20},{4,24},{8,28},{1,21},{5,25},{9,29},{2,22},{6,26},{10,30},{3... | collective-permute-start | bytes 405512 | tf_op jit(solution)/shard_map/ppermute | solution.py:275
  29.1 23.9 %collective-permute-start.3 = (bf16[264,256]{1,0:T(8,128)(2,1)S(1)}, bf16[264,256]{1,0:T(8,128)(2,1)S(1)}, u32[]{:S(2)}, u32[]{:S(2)}) collective-permute-start(bf16[264,256]{1,0:T(8,128)(2,1)S(1)} %pack.1.refs_0_.own_ref), channel_id=1, source_target_pairs={{0,24},{4,28},{1,25},{5,29},{2,26},{6,30},{3,27},{7,31},{32,56},{3... | collective-permute-start | bytes 405512 | tf_op jit(solution)/shard_map/ppermute | solution.py:275
  30.4 26.0 %collective-permute-start.4 = (bf16[264,256]{1,0:T(8,128)(2,1)S(1)}, bf16[264,256]{1,0:T(8,128)(2,1)S(1)}, u32[]{:S(2)}, u32[]{:S(2)}) collective-permute-start(bf16[264,256]{1,0:T(8,128)(2,1)S(1)} %pack.1.refs_0_.own_ref), channel_id=1, source_target_pairs={{0,8},{4,12},{8,16},{12,20},{16,24},{20,28},{1,9},{5,13},{9,17},{1... | collective-permute-start | bytes 405512 | tf_op jit(solution)/shard_map/ppermute | solution.py:275
  31.7 24.7 %collective-permute-start.5 = (bf16[264,256]{1,0:T(8,128)(2,1)S(1)}, bf16[264,256]{1,0:T(8,128)(2,1)S(1)}, u32[]{:S(2)}, u32[]{:S(2)}) collective-permute-start(bf16[264,256]{1,0:T(8,128)(2,1)S(1)} %pack.1.refs_0_.own_ref), channel_id=1, source_target_pairs={{0,12},{4,16},{8,20},{12,24},{16,28},{1,13},{5,17},{9,21},{13,25},... | collective-permute-start | bytes 405512 | tf_op jit(solution)/shard_map/ppermute | solution.py:275
  58.3 19.1 %collective-permute-start.6 = (bf16[64,512]{1,0:T(8,128)(2,1)S(1)}, bf16[64,512]{1,0:T(8,128)(2,1)S(1)}, u32[]{:S(2)}, u32[]{:S(2)}) collective-permute-start(bf16[64,512]{1,0:T(8,128)(2,1)S(1)} %get-tuple-element.15), channel_id=1, source_target_pairs={{0,32},{1,33},{2,34},{3,35},{4,36},{5,37},{6,38},{7,39},{8,40},{9,... | collective-permute-start | bytes 196616 | tf_op jit(solution)/shard_map/ppermute | solution.py:294
  60.2 17.3 %collective-permute-start.7 = (bf16[64,512]{1,0:T(8,128)(2,1)S(1)}, bf16[64,512]{1,0:T(8,128)(2,1)S(1)}, u32[]{:S(2)}, u32[]{:S(2)}) collective-permute-start(bf16[64,512]{1,0:T(8,128)(2,1)S(1)} %get-tuple-element.16), channel_id=1, source_target_pairs={{0,35},{1,32},{2,33},{3,34},{4,39},{5,36},{6,37},{7,38},{8,43},{9,... | collective-permute-start | bytes 196616 | tf_op jit(solution)/shard_map/ppermute | solution.py:294
  73.6 9.8 %collective-permute-start.8 = (bf16[64,512]{1,0:T(8,128)(2,1)S(1)}, bf16[64,512]{1,0:T(8,128)(2,1)S(1)}, u32[]{:S(2)}, u32[]{:S(2)}) collective-permute-start(bf16[64,512]{1,0:T(8,128)(2,1)S(1)} %get-tuple-element.17), channel_id=1, source_target_pairs={{0,34},{1,35},{2,32},{3,33},{4,38},{5,39},{6,36},{7,37},{8,42},{9,... | collective-permute-start | bytes 196616 | tf_op jit(solution)/shard_map/ppermute | solution.py:294
  75.5 8.9 %collective-permute-start.9 = (bf16[64,512]{1,0:T(8,128)(2,1)S(1)}, bf16[64,512]{1,0:T(8,128)(2,1)S(1)}, u32[]{:S(2)}, u32[]{:S(2)}) collective-permute-start(bf16[64,512]{1,0:T(8,128)(2,1)S(1)} %get-tuple-element.18), channel_id=1, source_target_pairs={{0,33},{1,34},{2,35},{3,32},{4,37},{5,38},{6,39},{7,36},{8,41},{9,... | collective-permute-start | bytes 196616 | tf_op jit(solution)/shard_map/ppermute | solution.py:294

commit v4 on v3

--- a/solution.py
+++ b/solution.py
@@ -14,8 +14,9 @@
 LABELS = 4
 LABEL_ROWS = 8
 NO_LABEL = 9.0
-NEAR = (0, 1, 4, 5, 6)
-FAR = (2, 3)
+NEAR = (0, 1, 2, 5, 6)
+FAR = (3, 4)
+SENT = {1: 0, 2: 0, 5: 0, 6: 0, 3: 2, 4: 2}
 PREPARE_VMEM = 56 << 20
 SEND_ORDER = (2, 3, 1, 0)
 
@@ -270,11 +271,12 @@
         name="pack",
     )(given)
     pairs = {0: own_pairs}
-    for d in [d for d in NEAR + FAR if 0 < d <= back]:
-        route = [(i, i + d) for i in range(blocks - d)]
-        pairs[d] = lax.ppermute(own_pairs, "blk", route)
+    for d, held in SENT.items():
+        if d <= back:
+            route = [(i, i + d - held) for i in range(held, blocks - d + held)]
+            pairs[d] = lax.ppermute(pairs[held], "blk", route)
     near = tuple(d for d in NEAR if d <= back)
-    far = tuple(d for d in pairs if d not in near)
+    far = tuple(d for d in FAR if d <= back)
     state = call_near(given, [pairs[d] for d in near], near, tokens, grouped, scale)
     attended = call_far(
         given, own_pairs, state, [pairs[d] for d in far], far, tokens, grouped, scale

time: 85.5 us -> 81.7 us (0.956)
  waiting for transfers between devices: 27 us -> 22.4 us
    ppermute x6, waiting for transfers between devices: 20 us -> 15.5 us  [per_device(): pairs[d] = lax.ppermute(pairs[held], 'blk', route)]
  transfers between devices with their start and end apart: 10 -> 10, of which waited for: 6 -> 5; matrix products, arithmetic and copies ran while one was open for 0% -> 0% of each run, Pallas kernels for 4% -> 4%
where the time goes in v4:
time: 81.7 us; the launch traced here: 81.3 us
  starting transfers between devices  28.7 us (35%)
  waiting for transfers between devices  22.4 us (27%)
  blocking collectives  22 us (27%)
  Pallas kernels  7.98 us (10%)
    all_to_all x1, blocking collectives, per_device(): lax.all_to_all(prepared, 'head', split_axis=0, concat_axis=0, tiled=True)  22 us
    ppermute x4, starting transfers between devices, per_device(): lax.ppermute(attended[turn], ('section', 'blk', 'head'), route)  19.1 us
    ppermute x6, waiting for transfers between devices, per_device(): pairs[d] = lax.ppermute(pairs[held], 'blk', route)  15.5 us
    ppermute x6, starting transfers between devices, per_device(): pairs[d] = lax.ppermute(pairs[held], 'blk', route)  9.61 us
    ppermute x4, waiting for transfers between devices, per_device(): lax.ppermute(attended[turn], ('section', 'blk', 'head'), route)  6.96 us
    pallas_call x1, Pallas kernels, call_near(): pl.pallas_call(functools.partial(near_kernel, distances=distances, tokens...  3.42 us
    pallas_call x1, Pallas kernels, call_far(): pl.pallas_call(functools.partial(far_kernel, distances=distances, tokens=...  1.92 us
    pallas_call x1, Pallas kernels, per_device(): pl.pallas_call(functools.partial(prepare_kernel, heads=heads), out_shape=...  1.81 us
  transfers between devices with their start and end apart: 10, of which 5 were waited for; matrix products, arithmetic and copies ran while one was open for 0% of the time, Pallas kernels for 4%

profile of v4, /device:TPU:12, one launch (start us, length us, event | category | flops | bytes accessed | tf_op | source)
XLA Modules:
  0.0 81.3 jit_solution(14606943745510877774)
XLA Ops:
  0.0 1.8 %prepare.1 = bf16[4,200,256]{2,1,0:T(8,128)(2,1)} custom-call(bf16[64,1024]{1,0:T(8,128)(2,1)} %bitcast.4, s32[1,64]{1,0:T(1,128)} %label_ref.1, bf16[64,2048]{1,0:T(8,128)(2,1)} %bitcast.3), custom_call_target="tpu_custom_call" | custom-call | tf_op jit(solution)/shard_map/prepare/pallas_call | solution.py:252
  1.8 22.0 %all_to_all.5.given_ref = bf16[4,200,256]{2,1,0:T(8,128)(2,1)S(1)} all-to-all(bf16[4,200,256]{2,1,0:T(8,128)(2,1)} %prepare.1), channel_id=1, replica_groups=mesh['section'=32,'blk'=8,'head'=4] {'head'}, dimensions={0} | all-to-all | bytes 819200 | tf_op jit(solution)/shard_map/all_to_all | solution.py:263
  23.8 0.1 pack.1.refs_0_.own_ref
  23.9 1.3 %collective-permute-start.1 = (bf16[264,256]{1,0:T(8,128)(2,1)S(1)}, bf16[264,256]{1,0:T(8,128)(2,1)S(1)}, u32[]{:S(2)}, u32[]{:S(2)}) collective-permute-start(bf16[264,256]{1,0:T(8,128)(2,1)S(1)} %pack.1.refs_0_.own_ref), channel_id=1, source_target_pairs={{0,8},{4,12},{8,16},{12,20},{16,24},{20,28},{1,9},{5,13},{9,17},{1... | collective-permute-start | bytes 405512 | tf_op jit(solution)/shard_map/ppermute | solution.py:277
  25.2 2.5 %collective-permute-start = (bf16[264,256]{1,0:T(8,128)(2,1)S(1)}, bf16[264,256]{1,0:T(8,128)(2,1)S(1)}, u32[]{:S(2)}, u32[]{:S(2)}) collective-permute-start(bf16[264,256]{1,0:T(8,128)(2,1)S(1)} %pack.1.refs_0_.own_ref), channel_id=1, source_target_pairs={{0,4},{4,8},{8,12},{12,16},{16,20},{20,24},{24,28},{1,5},{5,9},{9,... | collective-permute-start | bytes 405512 | tf_op jit(solution)/shard_map/ppermute | solution.py:277
  27.8 1.3 %collective-permute-start.2 = (bf16[264,256]{1,0:T(8,128)(2,1)S(1)}, bf16[264,256]{1,0:T(8,128)(2,1)S(1)}, u32[]{:S(2)}, u32[]{:S(2)}) collective-permute-start(bf16[264,256]{1,0:T(8,128)(2,1)S(1)} %pack.1.refs_0_.own_ref), channel_id=1, source_target_pairs={{0,20},{4,24},{8,28},{1,21},{5,25},{9,29},{2,22},{6,26},{10,30},{3... | collective-permute-start | bytes 405512 | tf_op jit(solution)/shard_map/ppermute | solution.py:277
  29.1 1.3 %collective-permute-start.3 = (bf16[264,256]{1,0:T(8,128)(2,1)S(1)}, bf16[264,256]{1,0:T(8,128)(2,1)S(1)}, u32[]{:S(2)}, u32[]{:S(2)}) collective-permute-start(bf16[264,256]{1,0:T(8,128)(2,1)S(1)} %pack.1.refs_0_.own_ref), channel_id=1, source_target_pairs={{0,24},{4,28},{1,25},{5,29},{2,26},{6,30},{3,27},{7,31},{32,56},{3... | collective-permute-start | bytes 405512 | tf_op jit(solution)/shard_map/ppermute | solution.py:277
  30.4 5.0 %collective-permute-done.1.refs_2_ = bf16[264,256]{1,0:T(8,128)(2,1)S(1)} collective-permute-done((bf16[264,256]{1,0:T(8,128)(2,1)S(1)}, bf16[264,256]{1,0:T(8,128)(2,1)S(1)}, u32[]{:S(2)}, u32[]{:S(2)}) %collective-permute-start.1) | collective-permute-done | bytes 135200 | tf_op jit(solution)/shard_map/ppermute | solution.py:277
  35.3 1.9 %collective-permute-start.4 = (bf16[264,256]{1,0:T(8,128)(2,1)S(1)}, bf16[264,256]{1,0:T(8,128)(2,1)S(1)}, u32[]{:S(2)}, u32[]{:S(2)}) collective-permute-start(bf16[264,256]{1,0:T(8,128)(2,1)S(1)} %collective-permute-done.1.refs_2_), channel_id=1, source_target_pairs={{8,12},{12,16},{16,20},{20,24},{24,28},{9,13},{13,17},{17,21},{21,... | collective-permute-start | bytes 405512 | tf_op jit(solution)/shard_map/ppermute | solution.py:277
  37.3 1.3 %collective-permute-start.5 = (bf16[264,256]{1,0:T(8,128)(2,1)S(1)}, bf16[264,256]{1,0:T(8,128)(2,1)S(1)}, u32[]{:S(2)}, u32[]{:S(2)}) collective-permute-start(bf16[264,256]{1,0:T(8,128)(2,1)S(1)} %collective-permute-done.1.refs_2_), channel_id=1, source_target_pairs={{8,16},{12,20},{16,24},{20,28},{9,17},{13,21},{17,25},{21,29},{10,... | collective-permute-start | bytes 405512 | tf_op jit(solution)/shard_map/ppermute | solution.py:277
  38.6 0.0 collective-permute-done.refs_1_
  38.6 2.9 %collective-permute-done.2.refs_3_ = bf16[264,256]{1,0:T(8,128)(2,1)S(1)} collective-permute-done((bf16[264,256]{1,0:T(8,128)(2,1)S(1)}, bf16[264,256]{1,0:T(8,128)(2,1)S(1)}, u32[]{:S(2)}, u32[]{:S(2)}) %collective-permute-start.2) | collective-permute-done | bytes 135200 | tf_op jit(solution)/shard_map/ppermute | solution.py:277
  41.5 7.6 %collective-permute-done.3.refs_4_ = bf16[264,256]{1,0:T(8,128)(2,1)S(1)} collective-permute-done((bf16[264,256]{1,0:T(8,128)(2,1)S(1)}, bf16[264,256]{1,0:T(8,128)(2,1)S(1)}, u32[]{:S(2)}, u32[]{:S(2)}) %collective-permute-start.3) | collective-permute-done | bytes 135200 | tf_op jit(solution)/shard_map/ppermute | solution.py:277
  49.1 3.4 %attend_near.1 = (f32[4,1,256]{2,1,0:T(1,128)S(1)}, f32[4,1,256]{2,1,0:T(1,128)S(1)}, f32[4,128,256]{2,1,0:T(8,128)S(1)}) custom-call(bf16[4,200,256]{2,1,0:T(8,128)(2,1)S(1)} %all_to_all.5.given_ref, bf16[264,256]{1,0:T(8,128)(2,1)S(1)} %pack.1.refs_0_.own_ref, bf16[264,256]{1,0:T(8,128)(2,1)S(1)} %collective-permute-done.refs_1_, ...), custom_call_target="tpu_custom_call" | custom-call | flops 671088640 | bytes 2621440 | tf_op jit(solution)/shard_map/attend_near/pallas_call | solution.py:203
  52.5 0.0 collective-permute-done.4.refs_0_
  52.5 0.0 collective-permute-done.5.refs_1_
  52.5 1.9 %attend_far.1 = (bf16[64,512]{1,0:T(8,128)(2,1)S(1)}, bf16[64,512]{1,0:T(8,128)(2,1)S(1)}, bf16[64,512]{1,0:T(8,128)(2,1)S(1)}, bf16[64,512]{1,0:T(8,128)(2,1)S(1)}) custom-call(bf16[4,200,256]{2,1,0:T(8,128)(2,1)S(1)} %all_to_all.5.given_ref, bf16[264,256]{1,0:T(8,128)(2,1)S(1)} %pack.1.refs_0_.own_ref, f32[4,1,256]{2,1,0:T(1,128)S(1)} %get-tuple-element.12.top_ref, ...), custom_call_target="tpu_custom_call" | custom-call | flops 268435456 | bytes 1048576 | tf_op jit(solution)/shard_map/attend_far/pallas_call | solution.py:222
  54.4 1.9 %collective-permute-start.6 = (bf16[64,512]{1,0:T(8,128)(2,1)S(1)}, bf16[64,512]{1,0:T(8,128)(2,1)S(1)}, u32[]{:S(2)}, u32[]{:S(2)}) collective-permute-start(bf16[64,512]{1,0:T(8,128)(2,1)S(1)} %get-tuple-element.15), channel_id=1, source_target_pairs={{0,32},{1,33},{2,34},{3,35},{4,36},{5,37},{6,38},{7,39},{8,40},{9,... | collective-permute-start | bytes 196616 | tf_op jit(solution)/shard_map/ppermute | solution.py:296
  56.4 13.3 %collective-permute-start.7 = (bf16[64,512]{1,0:T(8,128)(2,1)S(1)}, bf16[64,512]{1,0:T(8,128)(2,1)S(1)}, u32[]{:S(2)}, u32[]{:S(2)}) collective-permute-start(bf16[64,512]{1,0:T(8,128)(2,1)S(1)} %get-tuple-element.16), channel_id=1, source_target_pairs={{0,35},{1,32},{2,33},{3,34},{4,39},{5,36},{6,37},{7,38},{8,43},{9,... | collective-permute-start | bytes 196616 | tf_op jit(solution)/shard_map/ppermute | solution.py:296
  69.7 1.9 %collective-permute-start.8 = (bf16[64,512]{1,0:T(8,128)(2,1)S(1)}, bf16[64,512]{1,0:T(8,128)(2,1)S(1)}, u32[]{:S(2)}, u32[]{:S(2)}) collective-permute-start(bf16[64,512]{1,0:T(8,128)(2,1)S(1)} %get-tuple-element.17), channel_id=1, source_target_pairs={{0,34},{1,35},{2,32},{3,33},{4,38},{5,39},{6,36},{7,37},{8,42},{9,... | collective-permute-start | bytes 196616 | tf_op jit(solution)/shard_map/ppermute | solution.py:296
  71.6 1.9 %collective-permute-start.9 = (bf16[64,512]{1,0:T(8,128)(2,1)S(1)}, bf16[64,512]{1,0:T(8,128)(2,1)S(1)}, u32[]{:S(2)}, u32[]{:S(2)}) collective-permute-start(bf16[64,512]{1,0:T(8,128)(2,1)S(1)} %get-tuple-element.18), channel_id=1, source_target_pairs={{0,33},{1,34},{2,35},{3,32},{4,37},{5,38},{6,39},{7,36},{8,41},{9,... | collective-permute-start | bytes 196616 | tf_op jit(solution)/shard_map/ppermute | solution.py:296
  73.6 0.0 collective-permute-done.6.refs_0_
  73.6 0.0 collective-permute-done.7.refs_1_
  73.6 5.9 %collective-permute-done.8.refs_2_ = bf16[64,512]{1,0:T(8,128)(2,1)S(1)} collective-permute-done((bf16[64,512]{1,0:T(8,128)(2,1)S(1)}, bf16[64,512]{1,0:T(8,128)(2,1)S(1)}, u32[]{:S(2)}, u32[]{:S(2)}) %collective-permute-start.8) | collective-permute-done | bytes 65568 | tf_op jit(solution)/shard_map/ppermute | solution.py:296
  79.5 1.0 %collective-permute-done.9.refs_3_ = bf16[64,512]{1,0:T(8,128)(2,1)S(1)} collective-permute-done((bf16[64,512]{1,0:T(8,128)(2,1)S(1)}, bf16[64,512]{1,0:T(8,128)(2,1)S(1)}, u32[]{:S(2)}, u32[]{:S(2)}) %collective-permute-start.9) | collective-permute-done | bytes 65568 | tf_op jit(solution)/shard_map/ppermute | solution.py:296
  80.5 0.7 assemble.1
Async XLA Ops:
  23.9 11.4 %collective-permute-start.1 = (bf16[264,256]{1,0:T(8,128)(2,1)S(1)}, bf16[264,256]{1,0:T(8,128)(2,1)S(1)}, u32[]{:S(2)}, u32[]{:S(2)}) collective-permute-start(bf16[264,256]{1,0:T(8,128)(2,1)S(1)} %pack.1.refs_0_.own_ref), channel_id=1, source_target_pairs={{0,8},{4,12},{8,16},{12,20},{16,24},{20,28},{1,9},{5,13},{9,17},{1... | collective-permute-start | bytes 405512 | tf_op jit(solution)/shard_map/ppermute | solution.py:277
  25.2 13.3 %collective-permute-start = (bf16[264,256]{1,0:T(8,128)(2,1)S(1)}, bf16[264,256]{1,0:T(8,128)(2,1)S(1)}, u32[]{:S(2)}, u32[]{:S(2)}) collective-permute-start(bf16[264,256]{1,0:T(8,128)(2,1)S(1)} %pack.1.refs_0_.own_ref), channel_id=1, source_target_pairs={{0,4},{4,8},{8,12},{12,16},{16,20},{20,24},{24,28},{1,5},{5,9},{9,... | collective-permute-start | bytes 405512 | tf_op jit(solution)/shard_map/ppermute | solution.py:277
  27.8 13.7 %collective-permute-start.2 = (bf16[264,256]{1,0:T(8,128)(2,1)S(1)}, bf16[264,256]{1,0:T(8,128)(2,1)S(1)}, u32[]{:S(2)}, u32[]{:S(2)}) collective-permute-start(bf16[264,256]{1,0:T(8,128)(2,1)S(1)} %pack.1.refs_0_.own_ref), channel_id=1, source_target_pairs={{0,20},{4,24},{8,28},{1,21},{5,25},{9,29},{2,22},{6,26},{10,30},{3... | collective-permute-start | bytes 405512 | tf_op jit(solution)/shard_map/ppermute | solution.py:277
  29.1 20.0 %collective-permute-start.3 = (bf16[264,256]{1,0:T(8,128)(2,1)S(1)}, bf16[264,256]{1,0:T(8,128)(2,1)S(1)}, u32[]{:S(2)}, u32[]{:S(2)}) collective-permute-start(bf16[264,256]{1,0:T(8,128)(2,1)S(1)} %pack.1.refs_0_.own_ref), channel_id=1, source_target_pairs={{0,24},{4,28},{1,25},{5,29},{2,26},{6,30},{3,27},{7,31},{32,56},{3... | collective-permute-start | bytes 405512 | tf_op jit(solution)/shard_map/ppermute | solution.py:277
  35.3 17.2 %collective-permute-start.4 = (bf16[264,256]{1,0:T(8,128)(2,1)S(1)}, bf16[264,256]{1,0:T(8,128)(2,1)S(1)}, u32[]{:S(2)}, u32[]{:S(2)}) collective-permute-start(bf16[264,256]{1,0:T(8,128)(2,1)S(1)} %collective-permute-done.1.refs_2_), channel_id=1, source_target_pairs={{8,12},{12,16},{16,20},{20,24},{24,28},{9,13},{13,17},{17,21},{21,... | collective-permute-start | bytes 405512 | tf_op jit(solution)/shard_map/ppermute | solution.py:277
  37.3 15.2 %collective-permute-start.5 = (bf16[264,256]{1,0:T(8,128)(2,1)S(1)}, bf16[264,256]{1,0:T(8,128)(2,1)S(1)}, u32[]{:S(2)}, u32[]{:S(2)}) collective-permute-start(bf16[264,256]{1,0:T(8,128)(2,1)S(1)} %collective-permute-done.1.refs_2_), channel_id=1, source_target_pairs={{8,16},{12,20},{16,24},{20,28},{9,17},{13,21},{17,25},{21,29},{10,... | collective-permute-start | bytes 405512 | tf_op jit(solution)/shard_map/ppermute | solution.py:277
  54.4 19.1 %collective-permute-start.6 = (bf16[64,512]{1,0:T(8,128)(2,1)S(1)}, bf16[64,512]{1,0:T(8,128)(2,1)S(1)}, u32[]{:S(2)}, u32[]{:S(2)}) collective-permute-start(bf16[64,512]{1,0:T(8,128)(2,1)S(1)} %get-tuple-element.15), channel_id=1, source_target_pairs={{0,32},{1,33},{2,34},{3,35},{4,36},{5,37},{6,38},{7,39},{8,40},{9,... | collective-permute-start | bytes 196616 | tf_op jit(solution)/shard_map/ppermute | solution.py:296
  56.4 17.2 %collective-permute-start.7 = (bf16[64,512]{1,0:T(8,128)(2,1)S(1)}, bf16[64,512]{1,0:T(8,128)(2,1)S(1)}, u32[]{:S(2)}, u32[]{:S(2)}) collective-permute-start(bf16[64,512]{1,0:T(8,128)(2,1)S(1)} %get-tuple-element.16), channel_id=1, source_target_pairs={{0,35},{1,32},{2,33},{3,34},{4,39},{5,36},{6,37},{7,38},{8,43},{9,... | collective-permute-start | bytes 196616 | tf_op jit(solution)/shard_map/ppermute | solution.py:296
  69.7 9.8 %collective-permute-start.8 = (bf16[64,512]{1,0:T(8,128)(2,1)S(1)}, bf16[64,512]{1,0:T(8,128)(2,1)S(1)}, u32[]{:S(2)}, u32[]{:S(2)}) collective-permute-start(bf16[64,512]{1,0:T(8,128)(2,1)S(1)} %get-tuple-element.17), channel_id=1, source_target_pairs={{0,34},{1,35},{2,32},{3,33},{4,38},{5,39},{6,36},{7,37},{8,42},{9,... | collective-permute-start | bytes 196616 | tf_op jit(solution)/shard_map/ppermute | solution.py:296
  71.6 8.9 %collective-permute-start.9 = (bf16[64,512]{1,0:T(8,128)(2,1)S(1)}, bf16[64,512]{1,0:T(8,128)(2,1)S(1)}, u32[]{:S(2)}, u32[]{:S(2)}) collective-permute-start(bf16[64,512]{1,0:T(8,128)(2,1)S(1)} %get-tuple-element.18), channel_id=1, source_target_pairs={{0,33},{1,34},{2,35},{3,32},{4,37},{5,38},{6,39},{7,36},{8,41},{9,... | collective-permute-start | bytes 196616 | tf_op jit(solution)/shard_map/ppermute | solution.py:296

commit v5 on v4

--- a/solution.py
+++ b/solution.py
@@ -14,27 +14,42 @@
 LABELS = 4
 LABEL_ROWS = 8
 NO_LABEL = 9.0
-NEAR = (0, 1, 2, 5, 6)
-FAR = (3, 4)
+NEAR = (0, 1, 2, 5)
+FAR = (6, 3, 4)
 SENT = {1: 0, 2: 0, 5: 0, 6: 0, 3: 2, 4: 2}
-PREPARE_VMEM = 56 << 20
 SEND_ORDER = (2, 3, 1, 0)
 
 
-def prepare_kernel(kv_ref, label_ref, q_ref, out_ref, label_rows, *, heads):
+def prepare_kernel(
+    kv_ref, label_ref, q_ref, out_ref, own_labels, label_rows, semaphores, *, heads
+):
     tokens = kv_ref.shape[0]
     width = kv_ref.shape[1] // heads
-    q_width = q_ref.shape[1] // heads
+    q_parts = q_ref.shape[1] // heads // width
+    copies = []
+
+    def start(source, target):
+        copies.append(pltpu.make_async_copy(source, target, semaphores.at[len(copies)]))
+        copies[-1].start()
+
+    start(label_ref, own_labels)
+    for which in range(heads):
+        start(
+            kv_ref.at[:, pl.ds(which * width, width)],
+            out_ref.at[which, pl.ds(0, tokens), :],
+        )
+        for part in range(q_parts):
+            start(
+                q_ref.at[:, pl.ds((which * q_parts + part) * width, width)],
+                out_ref.at[which, pl.ds((1 + part) * tokens, tokens), :],
+            )
     label_rows[...] = jnp.full(label_rows.shape, NO_LABEL, jnp.float32)
-    label_rows[0:1, 0:tokens] = label_ref[...].astype(jnp.float32)
+    copies[0].wait()
+    label_rows[0:1, 0:tokens] = own_labels[...].astype(jnp.float32)
     for which in range(heads):
-        out_ref[which, 0:tokens, :] = kv_ref[:, which * width : (which + 1) * width]
-        for part in range(q_width // width):
-            start = which * q_width + part * width
-            out_ref[which, (1 + part) * tokens : (2 + part) * tokens, :] = q_ref[
-                :, start : start + width
-            ]
         out_ref[which, out_ref.shape[1] - LABEL_ROWS :, :] = label_rows[...].astype(jnp.bfloat16)
+    for copy in copies[1:]:
+        copy.wait()
 
 
 def pack_kernel(given_ref, out_ref, label_rows, *, tokens):
@@ -254,12 +269,20 @@
         out_shape=jax.ShapeDtypeStruct(
             (heads, parts * tokens + LABEL_ROWS, kv_width), jnp.bfloat16
         ),
-        in_specs=vmem(3),
+        in_specs=[pl.BlockSpec(memory_space=pltpu.HBM)] * 3,
         out_specs=vmem(1)[0],
-        scratch_shapes=[pltpu.VMEM((LABEL_ROWS, kv_width), jnp.float32)],
-        compiler_params=pltpu.CompilerParams(vmem_limit_bytes=PREPARE_VMEM),
+        scratch_shapes=[
+            pltpu.VMEM((1, tokens), jnp.int32),
+            pltpu.VMEM((LABEL_ROWS, kv_width), jnp.float32),
+            pltpu.SemaphoreType.DMA((1 + heads * parts,)),
+        ],
+        compiler_params=pltpu.CompilerParams(vmem_limit_bytes=4 << 20),
         name="prepare",
-    )(keys_values[0], segment_ids, queries[0])
+    )(
+        pltpu.with_memory_space_constraint(keys_values[0], pltpu.HBM),
+        pltpu.with_memory_space_constraint(segment_ids, pltpu.HBM),
+        pltpu.with_memory_space_constraint(queries[0], pltpu.HBM),
+    )
     given = lax.all_to_all(prepared, "head", split_axis=0, concat_axis=0, tiled=True)
     own_pairs = pl.pallas_call(
         functools.partial(pack_kernel, tokens=tokens),

time: 81.7 us -> 78 us (0.955)
  the two profiles are of different devices: /device:TPU:12 before, /device:TPU:74 now
where the time goes in v5:
time: 78 us; the launch traced here: 77.6 us
  starting transfers between devices  29.4 us (38%)
  blocking collectives  21.8 us (28%)
  waiting for transfers between devices  19.1 us (24%)
  Pallas kernels  7.1 us (9%)
    all_to_all x1, blocking collectives, per_device(): lax.all_to_all(prepared, 'head', split_axis=0, concat_axis=0, tiled=True)  21.8 us
    ppermute x4, starting transfers between devices, per_device(): lax.ppermute(attended[turn], ('section', 'blk', 'head'), route)  19.1 us
    ppermute x6, waiting for transfers between devices, per_device(): pairs[d] = lax.ppermute(pairs[held], 'blk', route)  12.2 us
    ppermute x6, starting transfers between devices, per_device(): pairs[d] = lax.ppermute(pairs[held], 'blk', route)  10.3 us
    ppermute x4, waiting for transfers between devices, per_device(): lax.ppermute(attended[turn], ('section', 'blk', 'head'), route)  6.96 us
    pallas_call x1, Pallas kernels, call_near(): pl.pallas_call(functools.partial(near_kernel, distances=distances, tokens...  2.79 us
    pallas_call x1, Pallas kernels, call_far(): pl.pallas_call(functools.partial(far_kernel, distances=distances, tokens=...  2.41 us
  transfers between devices with their start and end apart: 10, of which 4 were waited for; matrix products, arithmetic and copies ran while one was open for 0% of the time, Pallas kernels for 4%

profile of v5, /device:TPU:74, one launch (start us, length us, event | category | flops | bytes accessed | tf_op | source)
XLA Modules:
  0.0 77.6 jit_solution(15642091133695572221)
XLA Ops:
  0.0 1.1 %prepare.1 = bf16[4,200,256]{2,1,0:T(8,128)(2,1)S(1)} custom-call(bf16[64,1024]{1,0:T(8,128)(2,1)} %bitcast.4, s32[1,64]{1,0:T(1,128)} %label_ref.1, bf16[64,2048]{1,0:T(8,128)(2,1)} %bitcast.3), custom_call_target="tpu_custom_call" | custom-call | tf_op jit(solution)/shard_map/prepare/pallas_call | solution.py:267
  1.1 21.8 %all_to_all.5.given_ref = bf16[4,200,256]{2,1,0:T(8,128)(2,1)S(1)} all-to-all(bf16[4,200,256]{2,1,0:T(8,128)(2,1)S(1)} %prepare.1), channel_id=1, replica_groups=mesh['section'=32,'blk'=8,'head'=4] {'head'}, dimensions={0} | all-to-all | bytes 819200 | tf_op jit(solution)/shard_map/all_to_all | solution.py:286
  22.9 0.1 pack.1.refs_0_.own_ref
  23.0 2.5 %collective-permute-start.1 = (bf16[264,256]{1,0:T(8,128)(2,1)S(1)}, bf16[264,256]{1,0:T(8,128)(2,1)S(1)}, u32[]{:S(2)}, u32[]{:S(2)}) collective-permute-start(bf16[264,256]{1,0:T(8,128)(2,1)S(1)} %pack.1.refs_0_.own_ref), channel_id=1, source_target_pairs={{0,8},{4,12},{8,16},{12,20},{16,24},{20,28},{1,9},{5,13},{9,17},{1... | collective-permute-start | bytes 405512 | tf_op jit(solution)/shard_map/ppermute | solution.py:300
  25.5 1.9 %collective-permute-start = (bf16[264,256]{1,0:T(8,128)(2,1)S(1)}, bf16[264,256]{1,0:T(8,128)(2,1)S(1)}, u32[]{:S(2)}, u32[]{:S(2)}) collective-permute-start(bf16[264,256]{1,0:T(8,128)(2,1)S(1)} %pack.1.refs_0_.own_ref), channel_id=1, source_target_pairs={{0,4},{4,8},{8,12},{12,16},{16,20},{20,24},{24,28},{1,5},{5,9},{9,... | collective-permute-start | bytes 405512 | tf_op jit(solution)/shard_map/ppermute | solution.py:300
  27.5 1.3 %collective-permute-start.2 = (bf16[264,256]{1,0:T(8,128)(2,1)S(1)}, bf16[264,256]{1,0:T(8,128)(2,1)S(1)}, u32[]{:S(2)}, u32[]{:S(2)}) collective-permute-start(bf16[264,256]{1,0:T(8,128)(2,1)S(1)} %pack.1.refs_0_.own_ref), channel_id=1, source_target_pairs={{0,20},{4,24},{8,28},{1,21},{5,25},{9,29},{2,22},{6,26},{10,30},{3... | collective-permute-start | bytes 405512 | tf_op jit(solution)/shard_map/ppermute | solution.py:300
  28.8 0.7 collective-permute-start.3
  29.5 5.5 %collective-permute-done.1.refs_2_ = bf16[264,256]{1,0:T(8,128)(2,1)S(1)} collective-permute-done((bf16[264,256]{1,0:T(8,128)(2,1)S(1)}, bf16[264,256]{1,0:T(8,128)(2,1)S(1)}, u32[]{:S(2)}, u32[]{:S(2)}) %collective-permute-start.1) | collective-permute-done | bytes 135200 | tf_op jit(solution)/shard_map/ppermute | solution.py:300
  35.0 2.0 %collective-permute-start.4 = (bf16[264,256]{1,0:T(8,128)(2,1)S(1)}, bf16[264,256]{1,0:T(8,128)(2,1)S(1)}, u32[]{:S(2)}, u32[]{:S(2)}) collective-permute-start(bf16[264,256]{1,0:T(8,128)(2,1)S(1)} %collective-permute-done.1.refs_2_), channel_id=1, source_target_pairs={{8,12},{12,16},{16,20},{20,24},{24,28},{9,13},{13,17},{17,21},{21,... | collective-permute-start | bytes 405512 | tf_op jit(solution)/shard_map/ppermute | solution.py:300
  37.0 1.9 %collective-permute-start.5 = (bf16[264,256]{1,0:T(8,128)(2,1)S(1)}, bf16[264,256]{1,0:T(8,128)(2,1)S(1)}, u32[]{:S(2)}, u32[]{:S(2)}) collective-permute-start(bf16[264,256]{1,0:T(8,128)(2,1)S(1)} %collective-permute-done.1.refs_2_), channel_id=1, source_target_pairs={{8,16},{12,20},{16,24},{20,28},{9,17},{13,21},{17,25},{21,29},{10,... | collective-permute-start | bytes 405512 | tf_op jit(solution)/shard_map/ppermute | solution.py:300
  38.9 0.0 collective-permute-done.refs_1_
  38.9 6.6 %collective-permute-done.2.refs_3_ = bf16[264,256]{1,0:T(8,128)(2,1)S(1)} collective-permute-done((bf16[264,256]{1,0:T(8,128)(2,1)S(1)}, bf16[264,256]{1,0:T(8,128)(2,1)S(1)}, u32[]{:S(2)}, u32[]{:S(2)}) %collective-permute-start.2) | collective-permute-done | bytes 135200 | tf_op jit(solution)/shard_map/ppermute | solution.py:300
  45.6 2.8 %attend_near.1 = (f32[4,1,256]{2,1,0:T(1,128)S(1)}, f32[4,1,256]{2,1,0:T(1,128)S(1)}, f32[4,128,256]{2,1,0:T(8,128)S(1)}) custom-call(bf16[4,200,256]{2,1,0:T(8,128)(2,1)S(1)} %all_to_all.5.given_ref, bf16[264,256]{1,0:T(8,128)(2,1)S(1)} %pack.1.refs_0_.own_ref, bf16[264,256]{1,0:T(8,128)(2,1)S(1)} %collective-permute-done.refs_1_, ...), custom_call_target="tpu_custom_call" | custom-call | flops 536870912 | bytes 2097152 | tf_op jit(solution)/shard_map/attend_near/pallas_call | solution.py:218
  48.4 0.0 collective-permute-done.3.refs_0_
  48.4 0.0 collective-permute-done.4.refs_1_
  48.4 0.0 collective-permute-done.5.refs_2_
  48.4 2.4 %attend_far.1 = (bf16[64,512]{1,0:T(8,128)(2,1)S(1)}, bf16[64,512]{1,0:T(8,128)(2,1)S(1)}, bf16[64,512]{1,0:T(8,128)(2,1)S(1)}, bf16[64,512]{1,0:T(8,128)(2,1)S(1)}) custom-call(bf16[4,200,256]{2,1,0:T(8,128)(2,1)S(1)} %all_to_all.5.given_ref, bf16[264,256]{1,0:T(8,128)(2,1)S(1)} %pack.1.refs_0_.own_ref, f32[4,1,256]{2,1,0:T(1,128)S(1)} %get-tuple-element.12.top_ref, ...), custom_call_target="tpu_custom_call" | custom-call | flops 402653184 | bytes 1572864 | tf_op jit(solution)/shard_map/attend_far/pallas_call | solution.py:237
  50.8 1.9 %collective-permute-start.6 = (bf16[64,512]{1,0:T(8,128)(2,1)S(1)}, bf16[64,512]{1,0:T(8,128)(2,1)S(1)}, u32[]{:S(2)}, u32[]{:S(2)}) collective-permute-start(bf16[64,512]{1,0:T(8,128)(2,1)S(1)} %get-tuple-element.15), channel_id=1, source_target_pairs={{0,32},{1,33},{2,34},{3,35},{4,36},{5,37},{6,38},{7,39},{8,40},{9,... | collective-permute-start | bytes 196616 | tf_op jit(solution)/shard_map/ppermute | solution.py:319
  52.7 13.3 %collective-permute-start.7 = (bf16[64,512]{1,0:T(8,128)(2,1)S(1)}, bf16[64,512]{1,0:T(8,128)(2,1)S(1)}, u32[]{:S(2)}, u32[]{:S(2)}) collective-permute-start(bf16[64,512]{1,0:T(8,128)(2,1)S(1)} %get-tuple-element.16), channel_id=1, source_target_pairs={{0,35},{1,32},{2,33},{3,34},{4,39},{5,36},{6,37},{7,38},{8,43},{9,... | collective-permute-start | bytes 196616 | tf_op jit(solution)/shard_map/ppermute | solution.py:319
  66.0 1.9 %collective-permute-start.8 = (bf16[64,512]{1,0:T(8,128)(2,1)S(1)}, bf16[64,512]{1,0:T(8,128)(2,1)S(1)}, u32[]{:S(2)}, u32[]{:S(2)}) collective-permute-start(bf16[64,512]{1,0:T(8,128)(2,1)S(1)} %get-tuple-element.17), channel_id=1, source_target_pairs={{0,34},{1,35},{2,32},{3,33},{4,38},{5,39},{6,36},{7,37},{8,42},{9,... | collective-permute-start | bytes 196616 | tf_op jit(solution)/shard_map/ppermute | solution.py:319
  68.0 1.9 %collective-permute-start.9 = (bf16[64,512]{1,0:T(8,128)(2,1)S(1)}, bf16[64,512]{1,0:T(8,128)(2,1)S(1)}, u32[]{:S(2)}, u32[]{:S(2)}) collective-permute-start(bf16[64,512]{1,0:T(8,128)(2,1)S(1)} %get-tuple-element.18), channel_id=1, source_target_pairs={{0,33},{1,34},{2,35},{3,32},{4,37},{5,38},{6,39},{7,36},{8,41},{9,... | collective-permute-start | bytes 196616 | tf_op jit(solution)/shard_map/ppermute | solution.py:319
  69.9 0.0 collective-permute-done.6.refs_0_
  69.9 0.0 collective-permute-done.7.refs_1_
  69.9 5.9 %collective-permute-done.8.refs_2_ = bf16[64,512]{1,0:T(8,128)(2,1)S(1)} collective-permute-done((bf16[64,512]{1,0:T(8,128)(2,1)S(1)}, bf16[64,512]{1,0:T(8,128)(2,1)S(1)}, u32[]{:S(2)}, u32[]{:S(2)}) %collective-permute-start.8) | collective-permute-done | bytes 65568 | tf_op jit(solution)/shard_map/ppermute | solution.py:319
  75.9 1.0 %collective-permute-done.9.refs_3_ = bf16[64,512]{1,0:T(8,128)(2,1)S(1)} collective-permute-done((bf16[64,512]{1,0:T(8,128)(2,1)S(1)}, bf16[64,512]{1,0:T(8,128)(2,1)S(1)}, u32[]{:S(2)}, u32[]{:S(2)}) %collective-permute-start.9) | collective-permute-done | bytes 65568 | tf_op jit(solution)/shard_map/ppermute | solution.py:319
  76.9 0.7 assemble.1
Async XLA Ops:
  23.0 12.0 %collective-permute-start.1 = (bf16[264,256]{1,0:T(8,128)(2,1)S(1)}, bf16[264,256]{1,0:T(8,128)(2,1)S(1)}, u32[]{:S(2)}, u32[]{:S(2)}) collective-permute-start(bf16[264,256]{1,0:T(8,128)(2,1)S(1)} %pack.1.refs_0_.own_ref), channel_id=1, source_target_pairs={{0,8},{4,12},{8,16},{12,20},{16,24},{20,28},{1,9},{5,13},{9,17},{1... | collective-permute-start | bytes 405512 | tf_op jit(solution)/shard_map/ppermute | solution.py:300
  25.5 13.4 %collective-permute-start = (bf16[264,256]{1,0:T(8,128)(2,1)S(1)}, bf16[264,256]{1,0:T(8,128)(2,1)S(1)}, u32[]{:S(2)}, u32[]{:S(2)}) collective-permute-start(bf16[264,256]{1,0:T(8,128)(2,1)S(1)} %pack.1.refs_0_.own_ref), channel_id=1, source_target_pairs={{0,4},{4,8},{8,12},{12,16},{16,20},{20,24},{24,28},{1,5},{5,9},{9,... | collective-permute-start | bytes 405512 | tf_op jit(solution)/shard_map/ppermute | solution.py:300
  27.5 18.1 %collective-permute-start.2 = (bf16[264,256]{1,0:T(8,128)(2,1)S(1)}, bf16[264,256]{1,0:T(8,128)(2,1)S(1)}, u32[]{:S(2)}, u32[]{:S(2)}) collective-permute-start(bf16[264,256]{1,0:T(8,128)(2,1)S(1)} %pack.1.refs_0_.own_ref), channel_id=1, source_target_pairs={{0,20},{4,24},{8,28},{1,21},{5,25},{9,29},{2,22},{6,26},{10,30},{3... | collective-permute-start | bytes 405512 | tf_op jit(solution)/shard_map/ppermute | solution.py:300
  28.8 19.6 %collective-permute-start.3 = (bf16[264,256]{1,0:T(8,128)(2,1)S(1)}, bf16[264,256]{1,0:T(8,128)(2,1)S(1)}, u32[]{:S(2)}, u32[]{:S(2)}) collective-permute-start(bf16[264,256]{1,0:T(8,128)(2,1)S(1)} %pack.1.refs_0_.own_ref), channel_id=1, source_target_pairs={{0,24},{4,28},{1,25},{5,29},{2,26},{6,30},{3,27},{7,31},{32,56},{3... | collective-permute-start | bytes 405512 | tf_op jit(solution)/shard_map/ppermute | solution.py:300
  35.0 13.4 %collective-permute-start.4 = (bf16[264,256]{1,0:T(8,128)(2,1)S(1)}, bf16[264,256]{1,0:T(8,128)(2,1)S(1)}, u32[]{:S(2)}, u32[]{:S(2)}) collective-permute-start(bf16[264,256]{1,0:T(8,128)(2,1)S(1)} %collective-permute-done.1.refs_2_), channel_id=1, source_target_pairs={{8,12},{12,16},{16,20},{20,24},{24,28},{9,13},{13,17},{17,21},{21,... | collective-permute-start | bytes 405512 | tf_op jit(solution)/shard_map/ppermute | solution.py:300
  37.0 11.4 %collective-permute-start.5 = (bf16[264,256]{1,0:T(8,128)(2,1)S(1)}, bf16[264,256]{1,0:T(8,128)(2,1)S(1)}, u32[]{:S(2)}, u32[]{:S(2)}) collective-permute-start(bf16[264,256]{1,0:T(8,128)(2,1)S(1)} %collective-permute-done.1.refs_2_), channel_id=1, source_target_pairs={{8,16},{12,20},{16,24},{20,28},{9,17},{13,21},{17,25},{21,29},{10,... | collective-permute-start | bytes 405512 | tf_op jit(solution)/shard_map/ppermute | solution.py:300
  50.8 19.1 %collective-permute-start.6 = (bf16[64,512]{1,0:T(8,128)(2,1)S(1)}, bf16[64,512]{1,0:T(8,128)(2,1)S(1)}, u32[]{:S(2)}, u32[]{:S(2)}) collective-permute-start(bf16[64,512]{1,0:T(8,128)(2,1)S(1)} %get-tuple-element.15), channel_id=1, source_target_pairs={{0,32},{1,33},{2,34},{3,35},{4,36},{5,37},{6,38},{7,39},{8,40},{9,... | collective-permute-start | bytes 196616 | tf_op jit(solution)/shard_map/ppermute | solution.py:319
  52.7 17.2 %collective-permute-start.7 = (bf16[64,512]{1,0:T(8,128)(2,1)S(1)}, bf16[64,512]{1,0:T(8,128)(2,1)S(1)}, u32[]{:S(2)}, u32[]{:S(2)}) collective-permute-start(bf16[64,512]{1,0:T(8,128)(2,1)S(1)} %get-tuple-element.16), channel_id=1, source_target_pairs={{0,35},{1,32},{2,33},{3,34},{4,39},{5,36},{6,37},{7,38},{8,43},{9,... | collective-permute-start | bytes 196616 | tf_op jit(solution)/shard_map/ppermute | solution.py:319
  66.0 9.8 %collective-permute-start.8 = (bf16[64,512]{1,0:T(8,128)(2,1)S(1)}, bf16[64,512]{1,0:T(8,128)(2,1)S(1)}, u32[]{:S(2)}, u32[]{:S(2)}) collective-permute-start(bf16[64,512]{1,0:T(8,128)(2,1)S(1)} %get-tuple-element.17), channel_id=1, source_target_pairs={{0,34},{1,35},{2,32},{3,33},{4,38},{5,39},{6,36},{7,37},{8,42},{9,... | collective-permute-start | bytes 196616 | tf_op jit(solution)/shard_map/ppermute | solution.py:319
  68.0 8.9 %collective-permute-start.9 = (bf16[64,512]{1,0:T(8,128)(2,1)S(1)}, bf16[64,512]{1,0:T(8,128)(2,1)S(1)}, u32[]{:S(2)}, u32[]{:S(2)}) collective-permute-start(bf16[64,512]{1,0:T(8,128)(2,1)S(1)} %get-tuple-element.18), channel_id=1, source_target_pairs={{0,33},{1,34},{2,35},{3,32},{4,37},{5,38},{6,39},{7,36},{8,41},{9,... | collective-permute-start | bytes 196616 | tf_op jit(solution)/shard_map/ppermute | solution.py:319

commit v6 on v5

--- a/solution.py
+++ b/solution.py
@@ -14,10 +14,9 @@
 LABELS = 4
 LABEL_ROWS = 8
 NO_LABEL = 9.0
-NEAR = (0, 1, 2, 5)
-FAR = (6, 3, 4)
-SENT = {1: 0, 2: 0, 5: 0, 6: 0, 3: 2, 4: 2}
-SEND_ORDER = (2, 3, 1, 0)
+NEAR = (0, 2, 5, 1)
+FAR = (6, 4, 3)
+SENT = {2: 0, 5: 0, 6: 0, 1: 0, 4: 2, 3: 2}
 
 
 def prepare_kernel(
@@ -309,7 +308,7 @@
         return ((section % sections) * blocks + block) * heads + head % heads
 
     received = [None] * heads
-    for turn in SEND_ORDER:
+    for turn in range(heads):
         route = [
             (index(s, b, h), index(s + 1, b, h - turn))
             for s in range(sections)

time: 78 us -> 76 us (0.974)
  the two profiles are of different devices: /device:TPU:74 before, /device:TPU:70 now
where the time goes in v6:
time: 76 us; the launch traced here: 75.5 us
  starting transfers between devices  35.8 us (47%)
  blocking collectives  21.8 us (29%)
  waiting for transfers between devices  10.7 us (14%)
  Pallas kernels  7.08 us (9%)
    all_to_all x1, blocking collectives, per_device(): lax.all_to_all(prepared, 'head', split_axis=0, concat_axis=0, tiled=True)  21.8 us
    ppermute x4, starting transfers between devices, per_device(): lax.ppermute(attended[turn], ('section', 'blk', 'head'), route)  18.5 us
    ppermute x6, starting transfers between devices, per_device(): pairs[d] = lax.ppermute(pairs[held], 'blk', route)  17.3 us
    ppermute x4, waiting for transfers between devices, per_device(): lax.ppermute(attended[turn], ('section', 'blk', 'head'), route)  7.25 us
    ppermute x6, waiting for transfers between devices, per_device(): pairs[d] = lax.ppermute(pairs[held], 'blk', route)  3.49 us
    pallas_call x1, Pallas kernels, call_near(): pl.pallas_call(functools.partial(near_kernel, distances=distances, tokens...  2.79 us
    pallas_call x1, Pallas kernels, call_far(): pl.pallas_call(functools.partial(far_kernel, distances=distances, tokens=...  2.39 us
  transfers between devices with their start and end apart: 10, of which 4 were waited for; matrix products, arithmetic and copies ran while one was open for 0% of the time, Pallas kernels for 4%

profile of v6, /device:TPU:70, one launch (start us, length us, event | category | flops | bytes accessed | tf_op | source)
XLA Modules:
  0.0 75.5 jit_solution(15789540929376237774)
XLA Ops:
  0.0 1.1 %prepare.1 = bf16[4,200,256]{2,1,0:T(8,128)(2,1)S(1)} custom-call(bf16[64,1024]{1,0:T(8,128)(2,1)} %bitcast.4, s32[1,64]{1,0:T(1,128)} %label_ref.1, bf16[64,2048]{1,0:T(8,128)(2,1)} %bitcast.3), custom_call_target="tpu_custom_call" | custom-call | tf_op jit(solution)/shard_map/prepare/pallas_call | solution.py:266
  1.1 21.8 %all_to_all.5.given_ref = bf16[4,200,256]{2,1,0:T(8,128)(2,1)S(1)} all-to-all(bf16[4,200,256]{2,1,0:T(8,128)(2,1)S(1)} %prepare.1), channel_id=1, replica_groups=mesh['section'=32,'blk'=8,'head'=4] {'head'}, dimensions={0} | all-to-all | bytes 819200 | tf_op jit(solution)/shard_map/all_to_all | solution.py:285
  22.9 0.1 pack.1.refs_0_.own_ref
  23.0 4.6 %collective-permute-start = (bf16[264,256]{1,0:T(8,128)(2,1)S(1)}, bf16[264,256]{1,0:T(8,128)(2,1)S(1)}, u32[]{:S(2)}, u32[]{:S(2)}) collective-permute-start(bf16[264,256]{1,0:T(8,128)(2,1)S(1)} %pack.1.refs_0_.own_ref), channel_id=1, source_target_pairs={{0,8},{4,12},{8,16},{12,20},{16,24},{20,28},{1,9},{5,13},{9,17},{1... | collective-permute-start | bytes 405512 | tf_op jit(solution)/shard_map/ppermute | solution.py:299
  27.7 0.7 collective-permute-start.1
  28.3 2.5 %collective-permute-start.2 = (bf16[264,256]{1,0:T(8,128)(2,1)S(1)}, bf16[264,256]{1,0:T(8,128)(2,1)S(1)}, u32[]{:S(2)}, u32[]{:S(2)}) collective-permute-start(bf16[264,256]{1,0:T(8,128)(2,1)S(1)} %pack.1.refs_0_.own_ref), channel_id=1, source_target_pairs={{0,4},{4,8},{8,12},{12,16},{16,20},{20,24},{24,28},{1,5},{5,9},{9,... | collective-permute-start | bytes 405512 | tf_op jit(solution)/shard_map/ppermute | solution.py:299
  30.8 0.7 collective-permute-start.3
  31.5 1.8 %collective-permute-done.refs_1_ = bf16[264,256]{1,0:T(8,128)(2,1)S(1)} collective-permute-done((bf16[264,256]{1,0:T(8,128)(2,1)S(1)}, bf16[264,256]{1,0:T(8,128)(2,1)S(1)}, u32[]{:S(2)}, u32[]{:S(2)}) %collective-permute-start) | collective-permute-done | bytes 135200 | tf_op jit(solution)/shard_map/ppermute | solution.py:299
  33.3 6.4 %collective-permute-start.4 = (bf16[264,256]{1,0:T(8,128)(2,1)S(1)}, bf16[264,256]{1,0:T(8,128)(2,1)S(1)}, u32[]{:S(2)}, u32[]{:S(2)}) collective-permute-start(bf16[264,256]{1,0:T(8,128)(2,1)S(1)} %collective-permute-done.refs_1_), channel_id=1, source_target_pairs={{8,16},{12,20},{16,24},{20,28},{9,17},{13,21},{17,25},{21,29},{10,... | collective-permute-start | bytes 405512 | tf_op jit(solution)/shard_map/ppermute | solution.py:299
  39.7 2.4 %collective-permute-start.5 = (bf16[264,256]{1,0:T(8,128)(2,1)S(1)}, bf16[264,256]{1,0:T(8,128)(2,1)S(1)}, u32[]{:S(2)}, u32[]{:S(2)}) collective-permute-start(bf16[264,256]{1,0:T(8,128)(2,1)S(1)} %collective-permute-done.refs_1_), channel_id=1, source_target_pairs={{8,12},{12,16},{16,20},{20,24},{24,28},{9,13},{13,17},{17,21},{21,... | collective-permute-start | bytes 405512 | tf_op jit(solution)/shard_map/ppermute | solution.py:299
  42.1 0.0 collective-permute-done.1.refs_2_
  42.1 0.0 collective-permute-done.2.refs_3_
  42.1 2.8 %attend_near.1 = (f32[4,1,256]{2,1,0:T(1,128)S(1)}, f32[4,1,256]{2,1,0:T(1,128)S(1)}, f32[4,128,256]{2,1,0:T(8,128)S(1)}) custom-call(bf16[4,200,256]{2,1,0:T(8,128)(2,1)S(1)} %all_to_all.5.given_ref, bf16[264,256]{1,0:T(8,128)(2,1)S(1)} %pack.1.refs_0_.own_ref, bf16[264,256]{1,0:T(8,128)(2,1)S(1)} %collective-permute-done.refs_1_, ...), custom_call_target="tpu_custom_call" | custom-call | flops 536870912 | bytes 2097152 | tf_op jit(solution)/shard_map/attend_near/pallas_call | solution.py:217
  44.9 0.0 collective-permute-done.3.refs_0_
  44.9 0.0 collective-permute-done.4.refs_1_
  44.9 1.7 %collective-permute-done.5.refs_2_ = bf16[264,256]{1,0:T(8,128)(2,1)S(1)} collective-permute-done((bf16[264,256]{1,0:T(8,128)(2,1)S(1)}, bf16[264,256]{1,0:T(8,128)(2,1)S(1)}, u32[]{:S(2)}, u32[]{:S(2)}) %collective-permute-start.5) | collective-permute-done | bytes 135200 | tf_op jit(solution)/shard_map/ppermute | solution.py:299
  46.6 2.4 %attend_far.1 = (bf16[64,512]{1,0:T(8,128)(2,1)S(1)}, bf16[64,512]{1,0:T(8,128)(2,1)S(1)}, bf16[64,512]{1,0:T(8,128)(2,1)S(1)}, bf16[64,512]{1,0:T(8,128)(2,1)S(1)}) custom-call(bf16[4,200,256]{2,1,0:T(8,128)(2,1)S(1)} %all_to_all.5.given_ref, bf16[264,256]{1,0:T(8,128)(2,1)S(1)} %pack.1.refs_0_.own_ref, f32[4,1,256]{2,1,0:T(1,128)S(1)} %get-tuple-element.12.top_ref, ...), custom_call_target="tpu_custom_call" | custom-call | flops 402653184 | bytes 1572864 | tf_op jit(solution)/shard_map/attend_far/pallas_call | solution.py:236
  49.0 1.9 %collective-permute-start.6 = (bf16[64,512]{1,0:T(8,128)(2,1)S(1)}, bf16[64,512]{1,0:T(8,128)(2,1)S(1)}, u32[]{:S(2)}, u32[]{:S(2)}) collective-permute-start(bf16[64,512]{1,0:T(8,128)(2,1)S(1)} %get-tuple-element.15), channel_id=1, source_target_pairs={{0,32},{1,33},{2,34},{3,35},{4,36},{5,37},{6,38},{7,39},{8,40},{9,... | collective-permute-start | bytes 196616 | tf_op jit(solution)/shard_map/ppermute | solution.py:318
  50.9 12.7 %collective-permute-start.7 = (bf16[64,512]{1,0:T(8,128)(2,1)S(1)}, bf16[64,512]{1,0:T(8,128)(2,1)S(1)}, u32[]{:S(2)}, u32[]{:S(2)}) collective-permute-start(bf16[64,512]{1,0:T(8,128)(2,1)S(1)} %get-tuple-element.16), channel_id=1, source_target_pairs={{0,35},{1,32},{2,33},{3,34},{4,39},{5,36},{6,37},{7,38},{8,43},{9,... | collective-permute-start | bytes 196616 | tf_op jit(solution)/shard_map/ppermute | solution.py:318
  63.7 1.9 %collective-permute-start.8 = (bf16[64,512]{1,0:T(8,128)(2,1)S(1)}, bf16[64,512]{1,0:T(8,128)(2,1)S(1)}, u32[]{:S(2)}, u32[]{:S(2)}) collective-permute-start(bf16[64,512]{1,0:T(8,128)(2,1)S(1)} %get-tuple-element.17), channel_id=1, source_target_pairs={{0,34},{1,35},{2,32},{3,33},{4,38},{5,39},{6,36},{7,37},{8,42},{9,... | collective-permute-start | bytes 196616 | tf_op jit(solution)/shard_map/ppermute | solution.py:318
  65.6 1.9 %collective-permute-start.9 = (bf16[64,512]{1,0:T(8,128)(2,1)S(1)}, bf16[64,512]{1,0:T(8,128)(2,1)S(1)}, u32[]{:S(2)}, u32[]{:S(2)}) collective-permute-start(bf16[64,512]{1,0:T(8,128)(2,1)S(1)} %get-tuple-element.18), channel_id=1, source_target_pairs={{0,33},{1,34},{2,35},{3,32},{4,37},{5,38},{6,39},{7,36},{8,41},{9,... | collective-permute-start | bytes 196616 | tf_op jit(solution)/shard_map/ppermute | solution.py:318
  67.6 0.0 collective-permute-done.6.refs_0_
  67.6 0.0 collective-permute-done.7.refs_1_
  67.6 6.0 %collective-permute-done.8.refs_2_ = bf16[64,512]{1,0:T(8,128)(2,1)S(1)} collective-permute-done((bf16[64,512]{1,0:T(8,128)(2,1)S(1)}, bf16[64,512]{1,0:T(8,128)(2,1)S(1)}, u32[]{:S(2)}, u32[]{:S(2)}) %collective-permute-start.8) | collective-permute-done | bytes 65568 | tf_op jit(solution)/shard_map/ppermute | solution.py:318
  73.6 1.2 %collective-permute-done.9.refs_3_ = bf16[64,512]{1,0:T(8,128)(2,1)S(1)} collective-permute-done((bf16[64,512]{1,0:T(8,128)(2,1)S(1)}, bf16[64,512]{1,0:T(8,128)(2,1)S(1)}, u32[]{:S(2)}, u32[]{:S(2)}) %collective-permute-start.9) | collective-permute-done | bytes 65568 | tf_op jit(solution)/shard_map/ppermute | solution.py:318
  74.8 0.7 assemble.1
Async XLA Ops:
  23.0 10.3 %collective-permute-start = (bf16[264,256]{1,0:T(8,128)(2,1)S(1)}, bf16[264,256]{1,0:T(8,128)(2,1)S(1)}, u32[]{:S(2)}, u32[]{:S(2)}) collective-permute-start(bf16[264,256]{1,0:T(8,128)(2,1)S(1)} %pack.1.refs_0_.own_ref), channel_id=1, source_target_pairs={{0,8},{4,12},{8,16},{12,20},{16,24},{20,28},{1,9},{5,13},{9,17},{1... | collective-permute-start | bytes 405512 | tf_op jit(solution)/shard_map/ppermute | solution.py:299
  27.7 14.4 %collective-permute-start.1 = (bf16[264,256]{1,0:T(8,128)(2,1)S(1)}, bf16[264,256]{1,0:T(8,128)(2,1)S(1)}, u32[]{:S(2)}, u32[]{:S(2)}) collective-permute-start(bf16[264,256]{1,0:T(8,128)(2,1)S(1)} %pack.1.refs_0_.own_ref), channel_id=1, source_target_pairs={{0,20},{4,24},{8,28},{1,21},{5,25},{9,29},{2,22},{6,26},{10,30},{3... | collective-permute-start | bytes 405512 | tf_op jit(solution)/shard_map/ppermute | solution.py:299
  28.3 13.8 %collective-permute-start.2 = (bf16[264,256]{1,0:T(8,128)(2,1)S(1)}, bf16[264,256]{1,0:T(8,128)(2,1)S(1)}, u32[]{:S(2)}, u32[]{:S(2)}) collective-permute-start(bf16[264,256]{1,0:T(8,128)(2,1)S(1)} %pack.1.refs_0_.own_ref), channel_id=1, source_target_pairs={{0,4},{4,8},{8,12},{12,16},{16,20},{20,24},{24,28},{1,5},{5,9},{9,... | collective-permute-start | bytes 405512 | tf_op jit(solution)/shard_map/ppermute | solution.py:299
  30.8 14.1 %collective-permute-start.3 = (bf16[264,256]{1,0:T(8,128)(2,1)S(1)}, bf16[264,256]{1,0:T(8,128)(2,1)S(1)}, u32[]{:S(2)}, u32[]{:S(2)}) collective-permute-start(bf16[264,256]{1,0:T(8,128)(2,1)S(1)} %pack.1.refs_0_.own_ref), channel_id=1, source_target_pairs={{0,24},{4,28},{1,25},{5,29},{2,26},{6,30},{3,27},{7,31},{32,56},{3... | collective-permute-start | bytes 405512 | tf_op jit(solution)/shard_map/ppermute | solution.py:299
  33.3 11.6 %collective-permute-start.4 = (bf16[264,256]{1,0:T(8,128)(2,1)S(1)}, bf16[264,256]{1,0:T(8,128)(2,1)S(1)}, u32[]{:S(2)}, u32[]{:S(2)}) collective-permute-start(bf16[264,256]{1,0:T(8,128)(2,1)S(1)} %collective-permute-done.refs_1_), channel_id=1, source_target_pairs={{8,16},{12,20},{16,24},{20,28},{9,17},{13,21},{17,25},{21,29},{10,... | collective-permute-start | bytes 405512 | tf_op jit(solution)/shard_map/ppermute | solution.py:299
  39.7 6.9 %collective-permute-start.5 = (bf16[264,256]{1,0:T(8,128)(2,1)S(1)}, bf16[264,256]{1,0:T(8,128)(2,1)S(1)}, u32[]{:S(2)}, u32[]{:S(2)}) collective-permute-start(bf16[264,256]{1,0:T(8,128)(2,1)S(1)} %collective-permute-done.refs_1_), channel_id=1, source_target_pairs={{8,12},{12,16},{16,20},{20,24},{24,28},{9,13},{13,17},{17,21},{21,... | collective-permute-start | bytes 405512 | tf_op jit(solution)/shard_map/ppermute | solution.py:299
  49.0 18.5 %collective-permute-start.6 = (bf16[64,512]{1,0:T(8,128)(2,1)S(1)}, bf16[64,512]{1,0:T(8,128)(2,1)S(1)}, u32[]{:S(2)}, u32[]{:S(2)}) collective-permute-start(bf16[64,512]{1,0:T(8,128)(2,1)S(1)} %get-tuple-element.15), channel_id=1, source_target_pairs={{0,32},{1,33},{2,34},{3,35},{4,36},{5,37},{6,38},{7,39},{8,40},{9,... | collective-permute-start | bytes 196616 | tf_op jit(solution)/shard_map/ppermute | solution.py:318
  50.9 16.6 %collective-permute-start.7 = (bf16[64,512]{1,0:T(8,128)(2,1)S(1)}, bf16[64,512]{1,0:T(8,128)(2,1)S(1)}, u32[]{:S(2)}, u32[]{:S(2)}) collective-permute-start(bf16[64,512]{1,0:T(8,128)(2,1)S(1)} %get-tuple-element.16), channel_id=1, source_target_pairs={{0,35},{1,32},{2,33},{3,34},{4,39},{5,36},{6,37},{7,38},{8,43},{9,... | collective-permute-start | bytes 196616 | tf_op jit(solution)/shard_map/ppermute | solution.py:318
  63.7 9.9 %collective-permute-start.8 = (bf16[64,512]{1,0:T(8,128)(2,1)S(1)}, bf16[64,512]{1,0:T(8,128)(2,1)S(1)}, u32[]{:S(2)}, u32[]{:S(2)}) collective-permute-start(bf16[64,512]{1,0:T(8,128)(2,1)S(1)} %get-tuple-element.17), channel_id=1, source_target_pairs={{0,34},{1,35},{2,32},{3,33},{4,38},{5,39},{6,36},{7,37},{8,42},{9,... | collective-permute-start | bytes 196616 | tf_op jit(solution)/shard_map/ppermute | solution.py:318
  65.6 9.2 %collective-permute-start.9 = (bf16[64,512]{1,0:T(8,128)(2,1)S(1)}, bf16[64,512]{1,0:T(8,128)(2,1)S(1)}, u32[]{:S(2)}, u32[]{:S(2)}) collective-permute-start(bf16[64,512]{1,0:T(8,128)(2,1)S(1)} %get-tuple-element.18), channel_id=1, source_target_pairs={{0,33},{1,34},{2,35},{3,32},{4,37},{5,38},{6,39},{7,36},{8,41},{9,... | collective-permute-start | bytes 196616 | tf_op jit(solution)/shard_map/ppermute | solution.py:318

commit v7 on v6

--- a/solution.py
+++ b/solution.py
@@ -14,6 +14,7 @@
 LABELS = 4
 LABEL_ROWS = 8
 NO_LABEL = 9.0
+SHIFTS = (0, 1, 3, 2)
 NEAR = (0, 2, 5, 1)
 FAR = (6, 4, 3)
 SENT = {2: 0, 5: 0, 6: 0, 1: 0, 4: 2, 3: 2}
@@ -100,7 +101,7 @@
     heads = given_ref.shape[0]
     rows, lanes = heads * tokens, grouped * tokens
     block_index, own = lax.axis_index("blk"), lax.axis_index("head")
-    chunk = lax.rem(own - turn + heads, heads)
+    chunk = lax.rem(own - SHIFTS[turn] + heads, heads)
     place = chunk * tokens + lax.rem(lax.broadcasted_iota(jnp.int32, (1, lanes), 1), tokens)
     own_counts = counts_of(own_ref)
     keys = jnp.concatenate([keys_of(ref) for ref in pair_refs], axis=0)
@@ -189,7 +190,7 @@
     own = lax.axis_index("head")
     copies = []
     for turn in range(heads):
-        start = pl.multiple_of(lax.rem(own + turn, heads) * width, width)
+        start = pl.multiple_of(lax.rem(own + SHIFTS[turn], heads) * width, width)
         copies.append(
             pltpu.make_async_copy(
                 pieces[turn], out_ref.at[:, pl.ds(start, width)], semaphores.at[turn]
@@ -310,7 +311,7 @@
     received = [None] * heads
     for turn in range(heads):
         route = [
-            (index(s, b, h), index(s + 1, b, h - turn))
+            (index(s, b, h), index(s + 1, b, h - SHIFTS[turn]))
             for s in range(sections)
             for b in range(blocks)
             for h in range(heads)

time: 76 us -> 77.1 us (1.014)
  the two profiles are of different devices: /device:TPU:70 before, /device:TPU:74 now
where the time goes in v7:
time: 77.1 us; the launch traced here: 76.7 us
  starting transfers between devices  29.6 us (38%)
  blocking collectives  21.8 us (28%)
  waiting for transfers between devices  18.1 us (23%)
  Pallas kernels  7.08 us (9%)
    all_to_all x1, blocking collectives, per_device(): lax.all_to_all(prepared, 'head', split_axis=0, concat_axis=0, tiled=True)  21.8 us
    ppermute x4, starting transfers between devices, per_device(): lax.ppermute(attended[turn], ('section', 'blk', 'head'), route)  19.3 us
    ppermute x6, starting transfers between devices, per_device(): pairs[d] = lax.ppermute(pairs[held], 'blk', route)  10.2 us
    ppermute x6, waiting for transfers between devices, per_device(): pairs[d] = lax.ppermute(pairs[held], 'blk', route)  9.57 us
    ppermute x4, waiting for transfers between devices, per_device(): lax.ppermute(attended[turn], ('section', 'blk', 'head'), route)  8.5 us
    pallas_call x1, Pallas kernels, call_near(): pl.pallas_call(functools.partial(near_kernel, distances=distances, tokens...  2.78 us
    pallas_call x1, Pallas kernels, call_far(): pl.pallas_call(functools.partial(far_kernel, distances=distances, tokens=...  2.39 us
  transfers between devices with their start and end apart: 10, of which 5 were waited for; matrix products, arithmetic and copies ran while one was open for 0% of the time, Pallas kernels for 4%

profile of v7, /device:TPU:74, one launch (start us, length us, event | category | flops | bytes accessed | tf_op | source)
XLA Modules:
  0.0 76.7 jit_solution(4626683701383223305)
XLA Ops:
  0.0 1.1 %prepare.1 = bf16[4,200,256]{2,1,0:T(8,128)(2,1)S(1)} custom-call(bf16[64,1024]{1,0:T(8,128)(2,1)} %bitcast.4, s32[1,64]{1,0:T(1,128)} %label_ref.1, bf16[64,2048]{1,0:T(8,128)(2,1)} %bitcast.3), custom_call_target="tpu_custom_call" | custom-call | tf_op jit(solution)/shard_map/prepare/pallas_call | solution.py:267
  1.1 21.8 %all_to_all.5.given_ref = bf16[4,200,256]{2,1,0:T(8,128)(2,1)S(1)} all-to-all(bf16[4,200,256]{2,1,0:T(8,128)(2,1)S(1)} %prepare.1), channel_id=1, replica_groups=mesh['section'=32,'blk'=8,'head'=4] {'head'}, dimensions={0} | all-to-all | bytes 819200 | tf_op jit(solution)/shard_map/all_to_all | solution.py:286
  22.9 0.1 pack.1.refs_0_.own_ref
  23.0 2.5 %collective-permute-start = (bf16[264,256]{1,0:T(8,128)(2,1)S(1)}, bf16[264,256]{1,0:T(8,128)(2,1)S(1)}, u32[]{:S(2)}, u32[]{:S(2)}) collective-permute-start(bf16[264,256]{1,0:T(8,128)(2,1)S(1)} %pack.1.refs_0_.own_ref), channel_id=1, source_target_pairs={{0,8},{4,12},{8,16},{12,20},{16,24},{20,28},{1,9},{5,13},{9,17},{1... | collective-permute-start | bytes 405512 | tf_op jit(solution)/shard_map/ppermute | solution.py:300
  25.5 1.3 %collective-permute-start.1 = (bf16[264,256]{1,0:T(8,128)(2,1)S(1)}, bf16[264,256]{1,0:T(8,128)(2,1)S(1)}, u32[]{:S(2)}, u32[]{:S(2)}) collective-permute-start(bf16[264,256]{1,0:T(8,128)(2,1)S(1)} %pack.1.refs_0_.own_ref), channel_id=1, source_target_pairs={{0,20},{4,24},{8,28},{1,21},{5,25},{9,29},{2,22},{6,26},{10,30},{3... | collective-permute-start | bytes 405512 | tf_op jit(solution)/shard_map/ppermute | solution.py:300
  26.8 1.9 %collective-permute-start.2 = (bf16[264,256]{1,0:T(8,128)(2,1)S(1)}, bf16[264,256]{1,0:T(8,128)(2,1)S(1)}, u32[]{:S(2)}, u32[]{:S(2)}) collective-permute-start(bf16[264,256]{1,0:T(8,128)(2,1)S(1)} %pack.1.refs_0_.own_ref), channel_id=1, source_target_pairs={{0,4},{4,8},{8,12},{12,16},{16,20},{20,24},{24,28},{1,5},{5,9},{9,... | collective-permute-start | bytes 405512 | tf_op jit(solution)/shard_map/ppermute | solution.py:300
  28.8 0.7 collective-permute-start.3
  29.5 5.6 %collective-permute-done.refs_1_ = bf16[264,256]{1,0:T(8,128)(2,1)S(1)} collective-permute-done((bf16[264,256]{1,0:T(8,128)(2,1)S(1)}, bf16[264,256]{1,0:T(8,128)(2,1)S(1)}, u32[]{:S(2)}, u32[]{:S(2)}) %collective-permute-start) | collective-permute-done | bytes 135200 | tf_op jit(solution)/shard_map/ppermute | solution.py:300
  35.1 1.9 %collective-permute-start.4 = (bf16[264,256]{1,0:T(8,128)(2,1)S(1)}, bf16[264,256]{1,0:T(8,128)(2,1)S(1)}, u32[]{:S(2)}, u32[]{:S(2)}) collective-permute-start(bf16[264,256]{1,0:T(8,128)(2,1)S(1)} %collective-permute-done.refs_1_), channel_id=1, source_target_pairs={{8,16},{12,20},{16,24},{20,28},{9,17},{13,21},{17,25},{21,29},{10,... | collective-permute-start | bytes 405512 | tf_op jit(solution)/shard_map/ppermute | solution.py:300
  37.0 1.9 %collective-permute-start.5 = (bf16[264,256]{1,0:T(8,128)(2,1)S(1)}, bf16[264,256]{1,0:T(8,128)(2,1)S(1)}, u32[]{:S(2)}, u32[]{:S(2)}) collective-permute-start(bf16[264,256]{1,0:T(8,128)(2,1)S(1)} %collective-permute-done.refs_1_), channel_id=1, source_target_pairs={{8,12},{12,16},{16,20},{20,24},{24,28},{9,13},{13,17},{17,21},{21,... | collective-permute-start | bytes 405512 | tf_op jit(solution)/shard_map/ppermute | solution.py:300
  38.9 3.6 %collective-permute-done.1.refs_2_ = bf16[264,256]{1,0:T(8,128)(2,1)S(1)} collective-permute-done((bf16[264,256]{1,0:T(8,128)(2,1)S(1)}, bf16[264,256]{1,0:T(8,128)(2,1)S(1)}, u32[]{:S(2)}, u32[]{:S(2)}) %collective-permute-start.1) | collective-permute-done | bytes 135200 | tf_op jit(solution)/shard_map/ppermute | solution.py:300
  42.5 0.0 collective-permute-done.2.refs_3_
  42.5 2.8 %attend_near.1 = (f32[4,1,256]{2,1,0:T(1,128)S(1)}, f32[4,1,256]{2,1,0:T(1,128)S(1)}, f32[4,128,256]{2,1,0:T(8,128)S(1)}) custom-call(bf16[4,200,256]{2,1,0:T(8,128)(2,1)S(1)} %all_to_all.5.given_ref, bf16[264,256]{1,0:T(8,128)(2,1)S(1)} %pack.1.refs_0_.own_ref, bf16[264,256]{1,0:T(8,128)(2,1)S(1)} %collective-permute-done.refs_1_, ...), custom_call_target="tpu_custom_call" | custom-call | flops 536870912 | bytes 2097152 | tf_op jit(solution)/shard_map/attend_near/pallas_call | solution.py:218
  45.3 0.0 collective-permute-done.3.refs_0_
  45.3 0.0 collective-permute-done.4.refs_1_
  45.3 0.4 collective-permute-done.5.refs_2_
  45.7 2.4 %attend_far.1 = (bf16[64,512]{1,0:T(8,128)(2,1)S(1)}, bf16[64,512]{1,0:T(8,128)(2,1)S(1)}, bf16[64,512]{1,0:T(8,128)(2,1)S(1)}, bf16[64,512]{1,0:T(8,128)(2,1)S(1)}) custom-call(bf16[4,200,256]{2,1,0:T(8,128)(2,1)S(1)} %all_to_all.5.given_ref, bf16[264,256]{1,0:T(8,128)(2,1)S(1)} %pack.1.refs_0_.own_ref, f32[4,1,256]{2,1,0:T(1,128)S(1)} %get-tuple-element.12.top_ref, ...), custom_call_target="tpu_custom_call" | custom-call | flops 402653184 | bytes 1572864 | tf_op jit(solution)/shard_map/attend_far/pallas_call | solution.py:237
  48.1 1.9 %collective-permute-start.6 = (bf16[64,512]{1,0:T(8,128)(2,1)S(1)}, bf16[64,512]{1,0:T(8,128)(2,1)S(1)}, u32[]{:S(2)}, u32[]{:S(2)}) collective-permute-start(bf16[64,512]{1,0:T(8,128)(2,1)S(1)} %get-tuple-element.15), channel_id=1, source_target_pairs={{0,32},{1,33},{2,34},{3,35},{4,36},{5,37},{6,38},{7,39},{8,40},{9,... | collective-permute-start | bytes 196616 | tf_op jit(solution)/shard_map/ppermute | solution.py:319
  50.0 13.5 %collective-permute-start.7 = (bf16[64,512]{1,0:T(8,128)(2,1)S(1)}, bf16[64,512]{1,0:T(8,128)(2,1)S(1)}, u32[]{:S(2)}, u32[]{:S(2)}) collective-permute-start(bf16[64,512]{1,0:T(8,128)(2,1)S(1)} %get-tuple-element.16), channel_id=1, source_target_pairs={{0,35},{1,32},{2,33},{3,34},{4,39},{5,36},{6,37},{7,38},{8,43},{9,... | collective-permute-start | bytes 196616 | tf_op jit(solution)/shard_map/ppermute | solution.py:319
  63.6 1.9 %collective-permute-start.8 = (bf16[64,512]{1,0:T(8,128)(2,1)S(1)}, bf16[64,512]{1,0:T(8,128)(2,1)S(1)}, u32[]{:S(2)}, u32[]{:S(2)}) collective-permute-start(bf16[64,512]{1,0:T(8,128)(2,1)S(1)} %get-tuple-element.17), channel_id=1, source_target_pairs={{0,33},{1,34},{2,35},{3,32},{4,37},{5,38},{6,39},{7,36},{8,41},{9,... | collective-permute-start | bytes 196616 | tf_op jit(solution)/shard_map/ppermute | solution.py:319
  65.5 1.9 %collective-permute-start.9 = (bf16[64,512]{1,0:T(8,128)(2,1)S(1)}, bf16[64,512]{1,0:T(8,128)(2,1)S(1)}, u32[]{:S(2)}, u32[]{:S(2)}) collective-permute-start(bf16[64,512]{1,0:T(8,128)(2,1)S(1)} %get-tuple-element.18), channel_id=1, source_target_pairs={{0,34},{1,35},{2,32},{3,33},{4,38},{5,39},{6,36},{7,37},{8,42},{9,... | collective-permute-start | bytes 196616 | tf_op jit(solution)/shard_map/ppermute | solution.py:319
  67.4 0.0 collective-permute-done.6.refs_0_
  67.4 0.0 collective-permute-done.7.refs_1_
  67.4 5.0 %collective-permute-done.8.refs_2_ = bf16[64,512]{1,0:T(8,128)(2,1)S(1)} collective-permute-done((bf16[64,512]{1,0:T(8,128)(2,1)S(1)}, bf16[64,512]{1,0:T(8,128)(2,1)S(1)}, u32[]{:S(2)}, u32[]{:S(2)}) %collective-permute-start.8) | collective-permute-done | bytes 65568 | tf_op jit(solution)/shard_map/ppermute | solution.py:319
  72.5 3.5 %collective-permute-done.9.refs_3_ = bf16[64,512]{1,0:T(8,128)(2,1)S(1)} collective-permute-done((bf16[64,512]{1,0:T(8,128)(2,1)S(1)}, bf16[64,512]{1,0:T(8,128)(2,1)S(1)}, u32[]{:S(2)}, u32[]{:S(2)}) %collective-permute-start.9) | collective-permute-done | bytes 65568 | tf_op jit(solution)/shard_map/ppermute | solution.py:319
  75.9 0.7 assemble.1
Async XLA Ops:
  23.0 12.1 %collective-permute-start = (bf16[264,256]{1,0:T(8,128)(2,1)S(1)}, bf16[264,256]{1,0:T(8,128)(2,1)S(1)}, u32[]{:S(2)}, u32[]{:S(2)}) collective-permute-start(bf16[264,256]{1,0:T(8,128)(2,1)S(1)} %pack.1.refs_0_.own_ref), channel_id=1, source_target_pairs={{0,8},{4,12},{8,16},{12,20},{16,24},{20,28},{1,9},{5,13},{9,17},{1... | collective-permute-start | bytes 405512 | tf_op jit(solution)/shard_map/ppermute | solution.py:300
  25.5 17.0 %collective-permute-start.1 = (bf16[264,256]{1,0:T(8,128)(2,1)S(1)}, bf16[264,256]{1,0:T(8,128)(2,1)S(1)}, u32[]{:S(2)}, u32[]{:S(2)}) collective-permute-start(bf16[264,256]{1,0:T(8,128)(2,1)S(1)} %pack.1.refs_0_.own_ref), channel_id=1, source_target_pairs={{0,20},{4,24},{8,28},{1,21},{5,25},{9,29},{2,22},{6,26},{10,30},{3... | collective-permute-start | bytes 405512 | tf_op jit(solution)/shard_map/ppermute | solution.py:300
  26.8 15.7 %collective-permute-start.2 = (bf16[264,256]{1,0:T(8,128)(2,1)S(1)}, bf16[264,256]{1,0:T(8,128)(2,1)S(1)}, u32[]{:S(2)}, u32[]{:S(2)}) collective-permute-start(bf16[264,256]{1,0:T(8,128)(2,1)S(1)} %pack.1.refs_0_.own_ref), channel_id=1, source_target_pairs={{0,4},{4,8},{8,12},{12,16},{16,20},{20,24},{24,28},{1,5},{5,9},{9,... | collective-permute-start | bytes 405512 | tf_op jit(solution)/shard_map/ppermute | solution.py:300
  28.8 16.5 %collective-permute-start.3 = (bf16[264,256]{1,0:T(8,128)(2,1)S(1)}, bf16[264,256]{1,0:T(8,128)(2,1)S(1)}, u32[]{:S(2)}, u32[]{:S(2)}) collective-permute-start(bf16[264,256]{1,0:T(8,128)(2,1)S(1)} %pack.1.refs_0_.own_ref), channel_id=1, source_target_pairs={{0,24},{4,28},{1,25},{5,29},{2,26},{6,30},{3,27},{7,31},{32,56},{3... | collective-permute-start | bytes 405512 | tf_op jit(solution)/shard_map/ppermute | solution.py:300
  35.1 10.2 %collective-permute-start.4 = (bf16[264,256]{1,0:T(8,128)(2,1)S(1)}, bf16[264,256]{1,0:T(8,128)(2,1)S(1)}, u32[]{:S(2)}, u32[]{:S(2)}) collective-permute-start(bf16[264,256]{1,0:T(8,128)(2,1)S(1)} %collective-permute-done.refs_1_), channel_id=1, source_target_pairs={{8,16},{12,20},{16,24},{20,28},{9,17},{13,21},{17,25},{21,29},{10,... | collective-permute-start | bytes 405512 | tf_op jit(solution)/shard_map/ppermute | solution.py:300
  37.0 8.7 %collective-permute-start.5 = (bf16[264,256]{1,0:T(8,128)(2,1)S(1)}, bf16[264,256]{1,0:T(8,128)(2,1)S(1)}, u32[]{:S(2)}, u32[]{:S(2)}) collective-permute-start(bf16[264,256]{1,0:T(8,128)(2,1)S(1)} %collective-permute-done.refs_1_), channel_id=1, source_target_pairs={{8,12},{12,16},{16,20},{20,24},{24,28},{9,13},{13,17},{17,21},{21,... | collective-permute-start | bytes 405512 | tf_op jit(solution)/shard_map/ppermute | solution.py:300
  48.1 19.3 %collective-permute-start.6 = (bf16[64,512]{1,0:T(8,128)(2,1)S(1)}, bf16[64,512]{1,0:T(8,128)(2,1)S(1)}, u32[]{:S(2)}, u32[]{:S(2)}) collective-permute-start(bf16[64,512]{1,0:T(8,128)(2,1)S(1)} %get-tuple-element.15), channel_id=1, source_target_pairs={{0,32},{1,33},{2,34},{3,35},{4,36},{5,37},{6,38},{7,39},{8,40},{9,... | collective-permute-start | bytes 196616 | tf_op jit(solution)/shard_map/ppermute | solution.py:319
  50.0 17.4 %collective-permute-start.7 = (bf16[64,512]{1,0:T(8,128)(2,1)S(1)}, bf16[64,512]{1,0:T(8,128)(2,1)S(1)}, u32[]{:S(2)}, u32[]{:S(2)}) collective-permute-start(bf16[64,512]{1,0:T(8,128)(2,1)S(1)} %get-tuple-element.16), channel_id=1, source_target_pairs={{0,35},{1,32},{2,33},{3,34},{4,39},{5,36},{6,37},{7,38},{8,43},{9,... | collective-permute-start | bytes 196616 | tf_op jit(solution)/shard_map/ppermute | solution.py:319
  63.6 8.9 %collective-permute-start.8 = (bf16[64,512]{1,0:T(8,128)(2,1)S(1)}, bf16[64,512]{1,0:T(8,128)(2,1)S(1)}, u32[]{:S(2)}, u32[]{:S(2)}) collective-permute-start(bf16[64,512]{1,0:T(8,128)(2,1)S(1)} %get-tuple-element.17), channel_id=1, source_target_pairs={{0,33},{1,34},{2,35},{3,32},{4,37},{5,38},{6,39},{7,36},{8,41},{9,... | collective-permute-start | bytes 196616 | tf_op jit(solution)/shard_map/ppermute | solution.py:319
  65.5 10.4 %collective-permute-start.9 = (bf16[64,512]{1,0:T(8,128)(2,1)S(1)}, bf16[64,512]{1,0:T(8,128)(2,1)S(1)}, u32[]{:S(2)}, u32[]{:S(2)}) collective-permute-start(bf16[64,512]{1,0:T(8,128)(2,1)S(1)} %get-tuple-element.18), channel_id=1, source_target_pairs={{0,34},{1,35},{2,32},{3,33},{4,38},{5,39},{6,36},{7,37},{8,42},{9,... | collective-permute-start | bytes 196616 | tf_op jit(solution)/shard_map/ppermute | solution.py:319

commit v8 on v6

--- a/solution.py
+++ b/solution.py
@@ -160,20 +160,24 @@
         new_total[...] = total_ref[...]
         new_mixed[...] = mixed_ref[...]
 
-    @pl.when(block_index >= min(distances))
-    def _():
-        for turn in range(heads):
-            _, new_total[turn], new_mixed[turn] = fold(
-                (top_ref[turn], total_ref[turn], mixed_ref[turn]),
-                distances,
-                pair_refs,
-                own_ref,
-                given_ref,
-                turn,
-                tokens,
-                grouped,
-                scale,
-            )
+    levels = sorted(distances) + [lax.axis_size("blk")]
+    for level, above in zip(levels[:-1], levels[1:], strict=True):
+        taken = [which for which, d in enumerate(distances) if d <= level]
+
+        @pl.when((block_index >= level) & (block_index < above))
+        def _(taken=taken):
+            for turn in range(heads):
+                _, new_total[turn], new_mixed[turn] = fold(
+                    (top_ref[turn], total_ref[turn], mixed_ref[turn]),
+                    [distances[which] for which in taken],
+                    [pair_refs[which] for which in taken],
+                    own_ref,
+                    given_ref,
+                    turn,
+                    tokens,
+                    grouped,
+                    scale,
+                )
 
     for turn in range(heads):
         normed = (new_mixed[turn] * (1.0 / new_total[turn])).astype(jnp.bfloat16).T

time: 76 us -> 75.2 us (0.989)
  the two profiles are of different devices: /device:TPU:70 before, /device:TPU:8 now
where the time goes in v8:
time: 75.2 us; the launch traced here: 74.7 us
  starting transfers between devices  29.9 us (40%)
  blocking collectives  21.8 us (29%)
  waiting for transfers between devices  16.3 us (22%)
  Pallas kernels  6.58 us (9%)
    all_to_all x1, blocking collectives, per_device(): lax.all_to_all(prepared, 'head', split_axis=0, concat_axis=0, tiled=True)  21.8 us
    ppermute x4, starting transfers between devices, per_device(): lax.ppermute(attended[turn], ('section', 'blk', 'head'), route)  19 us
    ppermute x6, starting transfers between devices, per_device(): pairs[d] = lax.ppermute(pairs[held], 'blk', route)  10.9 us
    ppermute x6, waiting for transfers between devices, per_device(): pairs[d] = lax.ppermute(pairs[held], 'blk', route)  9.31 us
    ppermute x4, waiting for transfers between devices, per_device(): lax.ppermute(attended[turn], ('section', 'blk', 'head'), route)  6.96 us
    pallas_call x1, Pallas kernels, call_near(): pl.pallas_call(functools.partial(near_kernel, distances=distances, tokens...  2.79 us
    pallas_call x1, Pallas kernels, call_far(): pl.pallas_call(functools.partial(far_kernel, distances=distances, tokens=...  1.9 us
  transfers between devices with their start and end apart: 10, of which 5 were waited for; matrix products, arithmetic and copies ran while one was open for 0% of the time, Pallas kernels for 4%

profile of v8, /device:TPU:8, one launch (start us, length us, event | category | flops | bytes accessed | tf_op | source)
XLA Modules:
  0.0 74.7 jit_solution(3060437215492594056)
XLA Ops:
  0.0 1.1 %prepare.1 = bf16[4,200,256]{2,1,0:T(8,128)(2,1)S(1)} custom-call(bf16[64,1024]{1,0:T(8,128)(2,1)} %bitcast.4, s32[1,64]{1,0:T(1,128)} %label_ref.1, bf16[64,2048]{1,0:T(8,128)(2,1)} %bitcast.3), custom_call_target="tpu_custom_call" | custom-call | tf_op jit(solution)/shard_map/prepare/pallas_call | solution.py:270
  1.1 21.8 %all_to_all.5.given_ref = bf16[4,200,256]{2,1,0:T(8,128)(2,1)S(1)} all-to-all(bf16[4,200,256]{2,1,0:T(8,128)(2,1)S(1)} %prepare.1), channel_id=1, replica_groups=mesh['section'=32,'blk'=8,'head'=4] {'head'}, dimensions={0} | all-to-all | bytes 819200 | tf_op jit(solution)/shard_map/all_to_all | solution.py:289
  22.9 0.1 pack.1.refs_0_.own_ref
  23.0 2.5 %collective-permute-start = (bf16[264,256]{1,0:T(8,128)(2,1)S(1)}, bf16[264,256]{1,0:T(8,128)(2,1)S(1)}, u32[]{:S(2)}, u32[]{:S(2)}) collective-permute-start(bf16[264,256]{1,0:T(8,128)(2,1)S(1)} %pack.1.refs_0_.own_ref), channel_id=1, source_target_pairs={{0,8},{4,12},{8,16},{12,20},{16,24},{20,28},{1,9},{5,13},{9,17},{1... | collective-permute-start | bytes 405512 | tf_op jit(solution)/shard_map/ppermute | solution.py:303
  25.5 0.7 collective-permute-start.1
  26.2 3.1 %collective-permute-start.2 = (bf16[264,256]{1,0:T(8,128)(2,1)S(1)}, bf16[264,256]{1,0:T(8,128)(2,1)S(1)}, u32[]{:S(2)}, u32[]{:S(2)}) collective-permute-start(bf16[264,256]{1,0:T(8,128)(2,1)S(1)} %pack.1.refs_0_.own_ref), channel_id=1, source_target_pairs={{0,4},{4,8},{8,12},{12,16},{16,20},{20,24},{24,28},{1,5},{5,9},{9,... | collective-permute-start | bytes 405512 | tf_op jit(solution)/shard_map/ppermute | solution.py:303
  29.4 0.7 collective-permute-start.3
  30.0 5.5 %collective-permute-done.refs_1_ = bf16[264,256]{1,0:T(8,128)(2,1)S(1)} collective-permute-done((bf16[264,256]{1,0:T(8,128)(2,1)S(1)}, bf16[264,256]{1,0:T(8,128)(2,1)S(1)}, u32[]{:S(2)}, u32[]{:S(2)}) %collective-permute-start) | collective-permute-done | bytes 135200 | tf_op jit(solution)/shard_map/ppermute | solution.py:303
  35.6 1.9 %collective-permute-start.4 = (bf16[264,256]{1,0:T(8,128)(2,1)S(1)}, bf16[264,256]{1,0:T(8,128)(2,1)S(1)}, u32[]{:S(2)}, u32[]{:S(2)}) collective-permute-start(bf16[264,256]{1,0:T(8,128)(2,1)S(1)} %collective-permute-done.refs_1_), channel_id=1, source_target_pairs={{8,16},{12,20},{16,24},{20,28},{9,17},{13,21},{17,25},{21,29},{10,... | collective-permute-start | bytes 405512 | tf_op jit(solution)/shard_map/ppermute | solution.py:303
  37.5 2.0 %collective-permute-start.5 = (bf16[264,256]{1,0:T(8,128)(2,1)S(1)}, bf16[264,256]{1,0:T(8,128)(2,1)S(1)}, u32[]{:S(2)}, u32[]{:S(2)}) collective-permute-start(bf16[264,256]{1,0:T(8,128)(2,1)S(1)} %collective-permute-done.refs_1_), channel_id=1, source_target_pairs={{8,12},{12,16},{16,20},{20,24},{24,28},{9,13},{13,17},{17,21},{21,... | collective-permute-start | bytes 405512 | tf_op jit(solution)/shard_map/ppermute | solution.py:303
  39.5 0.0 collective-permute-done.1.refs_2_
  39.5 0.0 collective-permute-done.2.refs_3_
  39.5 2.8 %attend_near.1 = (f32[4,1,256]{2,1,0:T(1,128)S(1)}, f32[4,1,256]{2,1,0:T(1,128)S(1)}, f32[4,128,256]{2,1,0:T(8,128)S(1)}) custom-call(bf16[4,200,256]{2,1,0:T(8,128)(2,1)S(1)} %all_to_all.5.given_ref, bf16[264,256]{1,0:T(8,128)(2,1)S(1)} %pack.1.refs_0_.own_ref, bf16[264,256]{1,0:T(8,128)(2,1)S(1)} %collective-permute-done.refs_1_, ...), custom_call_target="tpu_custom_call" | custom-call | flops 536870912 | bytes 2097152 | tf_op jit(solution)/shard_map/attend_near/pallas_call | solution.py:221
  42.3 0.0 collective-permute-done.3.refs_0_
  42.3 2.3 %collective-permute-done.4.refs_1_ = bf16[264,256]{1,0:T(8,128)(2,1)S(1)} collective-permute-done((bf16[264,256]{1,0:T(8,128)(2,1)S(1)}, bf16[264,256]{1,0:T(8,128)(2,1)S(1)}, u32[]{:S(2)}, u32[]{:S(2)}) %collective-permute-start.4) | collective-permute-done | bytes 135200 | tf_op jit(solution)/shard_map/ppermute | solution.py:303
  44.7 1.4 %collective-permute-done.5.refs_2_ = bf16[264,256]{1,0:T(8,128)(2,1)S(1)} collective-permute-done((bf16[264,256]{1,0:T(8,128)(2,1)S(1)}, bf16[264,256]{1,0:T(8,128)(2,1)S(1)}, u32[]{:S(2)}, u32[]{:S(2)}) %collective-permute-start.5) | collective-permute-done | bytes 135200 | tf_op jit(solution)/shard_map/ppermute | solution.py:303
  46.1 1.9 %attend_far.1 = (bf16[64,512]{1,0:T(8,128)(2,1)S(1)}, bf16[64,512]{1,0:T(8,128)(2,1)S(1)}, bf16[64,512]{1,0:T(8,128)(2,1)S(1)}, bf16[64,512]{1,0:T(8,128)(2,1)S(1)}) custom-call(bf16[4,200,256]{2,1,0:T(8,128)(2,1)S(1)} %all_to_all.5.given_ref, bf16[264,256]{1,0:T(8,128)(2,1)S(1)} %pack.1.refs_0_.own_ref, f32[4,1,256]{2,1,0:T(1,128)S(1)} %get-tuple-element.12.top_ref, ...), custom_call_target="tpu_custom_call" | custom-call | flops 402653184 | bytes 1572864 | tf_op jit(solution)/shard_map/attend_far/pallas_call | solution.py:240
  48.0 1.9 %collective-permute-start.6 = (bf16[64,512]{1,0:T(8,128)(2,1)S(1)}, bf16[64,512]{1,0:T(8,128)(2,1)S(1)}, u32[]{:S(2)}, u32[]{:S(2)}) collective-permute-start(bf16[64,512]{1,0:T(8,128)(2,1)S(1)} %get-tuple-element.15), channel_id=1, source_target_pairs={{0,32},{1,33},{2,34},{3,35},{4,36},{5,37},{6,38},{7,39},{8,40},{9,... | collective-permute-start | bytes 196616 | tf_op jit(solution)/shard_map/ppermute | solution.py:322
  49.9 13.2 %collective-permute-start.7 = (bf16[64,512]{1,0:T(8,128)(2,1)S(1)}, bf16[64,512]{1,0:T(8,128)(2,1)S(1)}, u32[]{:S(2)}, u32[]{:S(2)}) collective-permute-start(bf16[64,512]{1,0:T(8,128)(2,1)S(1)} %get-tuple-element.16), channel_id=1, source_target_pairs={{0,35},{1,32},{2,33},{3,34},{4,39},{5,36},{6,37},{7,38},{8,43},{9,... | collective-permute-start | bytes 196616 | tf_op jit(solution)/shard_map/ppermute | solution.py:322
  63.2 1.9 %collective-permute-start.8 = (bf16[64,512]{1,0:T(8,128)(2,1)S(1)}, bf16[64,512]{1,0:T(8,128)(2,1)S(1)}, u32[]{:S(2)}, u32[]{:S(2)}) collective-permute-start(bf16[64,512]{1,0:T(8,128)(2,1)S(1)} %get-tuple-element.17), channel_id=1, source_target_pairs={{0,34},{1,35},{2,32},{3,33},{4,38},{5,39},{6,36},{7,37},{8,42},{9,... | collective-permute-start | bytes 196616 | tf_op jit(solution)/shard_map/ppermute | solution.py:322
  65.1 1.9 %collective-permute-start.9 = (bf16[64,512]{1,0:T(8,128)(2,1)S(1)}, bf16[64,512]{1,0:T(8,128)(2,1)S(1)}, u32[]{:S(2)}, u32[]{:S(2)}) collective-permute-start(bf16[64,512]{1,0:T(8,128)(2,1)S(1)} %get-tuple-element.18), channel_id=1, source_target_pairs={{0,33},{1,34},{2,35},{3,32},{4,37},{5,38},{6,39},{7,36},{8,41},{9,... | collective-permute-start | bytes 196616 | tf_op jit(solution)/shard_map/ppermute | solution.py:322
  67.0 0.0 collective-permute-done.6.refs_0_
  67.0 0.0 collective-permute-done.7.refs_1_
  67.0 5.9 %collective-permute-done.8.refs_2_ = bf16[64,512]{1,0:T(8,128)(2,1)S(1)} collective-permute-done((bf16[64,512]{1,0:T(8,128)(2,1)S(1)}, bf16[64,512]{1,0:T(8,128)(2,1)S(1)}, u32[]{:S(2)}, u32[]{:S(2)}) %collective-permute-start.8) | collective-permute-done | bytes 65568 | tf_op jit(solution)/shard_map/ppermute | solution.py:322
  73.0 1.0 %collective-permute-done.9.refs_3_ = bf16[64,512]{1,0:T(8,128)(2,1)S(1)} collective-permute-done((bf16[64,512]{1,0:T(8,128)(2,1)S(1)}, bf16[64,512]{1,0:T(8,128)(2,1)S(1)}, u32[]{:S(2)}, u32[]{:S(2)}) %collective-permute-start.9) | collective-permute-done | bytes 65568 | tf_op jit(solution)/shard_map/ppermute | solution.py:322
  74.0 0.7 assemble.1
Async XLA Ops:
  23.0 12.6 %collective-permute-start = (bf16[264,256]{1,0:T(8,128)(2,1)S(1)}, bf16[264,256]{1,0:T(8,128)(2,1)S(1)}, u32[]{:S(2)}, u32[]{:S(2)}) collective-permute-start(bf16[264,256]{1,0:T(8,128)(2,1)S(1)} %pack.1.refs_0_.own_ref), channel_id=1, source_target_pairs={{0,8},{4,12},{8,16},{12,20},{16,24},{20,28},{1,9},{5,13},{9,17},{1... | collective-permute-start | bytes 405512 | tf_op jit(solution)/shard_map/ppermute | solution.py:303
  25.5 14.0 %collective-permute-start.1 = (bf16[264,256]{1,0:T(8,128)(2,1)S(1)}, bf16[264,256]{1,0:T(8,128)(2,1)S(1)}, u32[]{:S(2)}, u32[]{:S(2)}) collective-permute-start(bf16[264,256]{1,0:T(8,128)(2,1)S(1)} %pack.1.refs_0_.own_ref), channel_id=1, source_target_pairs={{0,20},{4,24},{8,28},{1,21},{5,25},{9,29},{2,22},{6,26},{10,30},{3... | collective-permute-start | bytes 405512 | tf_op jit(solution)/shard_map/ppermute | solution.py:303
  26.2 13.3 %collective-permute-start.2 = (bf16[264,256]{1,0:T(8,128)(2,1)S(1)}, bf16[264,256]{1,0:T(8,128)(2,1)S(1)}, u32[]{:S(2)}, u32[]{:S(2)}) collective-permute-start(bf16[264,256]{1,0:T(8,128)(2,1)S(1)} %pack.1.refs_0_.own_ref), channel_id=1, source_target_pairs={{0,4},{4,8},{8,12},{12,16},{16,20},{20,24},{24,28},{1,5},{5,9},{9,... | collective-permute-start | bytes 405512 | tf_op jit(solution)/shard_map/ppermute | solution.py:303
  29.4 13.0 %collective-permute-start.3 = (bf16[264,256]{1,0:T(8,128)(2,1)S(1)}, bf16[264,256]{1,0:T(8,128)(2,1)S(1)}, u32[]{:S(2)}, u32[]{:S(2)}) collective-permute-start(bf16[264,256]{1,0:T(8,128)(2,1)S(1)} %pack.1.refs_0_.own_ref), channel_id=1, source_target_pairs={{0,24},{4,28},{1,25},{5,29},{2,26},{6,30},{3,27},{7,31},{32,56},{3... | collective-permute-start | bytes 405512 | tf_op jit(solution)/shard_map/ppermute | solution.py:303
  35.6 9.1 %collective-permute-start.4 = (bf16[264,256]{1,0:T(8,128)(2,1)S(1)}, bf16[264,256]{1,0:T(8,128)(2,1)S(1)}, u32[]{:S(2)}, u32[]{:S(2)}) collective-permute-start(bf16[264,256]{1,0:T(8,128)(2,1)S(1)} %collective-permute-done.refs_1_), channel_id=1, source_target_pairs={{8,16},{12,20},{16,24},{20,28},{9,17},{13,21},{17,25},{21,29},{10,... | collective-permute-start | bytes 405512 | tf_op jit(solution)/shard_map/ppermute | solution.py:303
  37.5 8.6 %collective-permute-start.5 = (bf16[264,256]{1,0:T(8,128)(2,1)S(1)}, bf16[264,256]{1,0:T(8,128)(2,1)S(1)}, u32[]{:S(2)}, u32[]{:S(2)}) collective-permute-start(bf16[264,256]{1,0:T(8,128)(2,1)S(1)} %collective-permute-done.refs_1_), channel_id=1, source_target_pairs={{8,12},{12,16},{16,20},{20,24},{24,28},{9,13},{13,17},{17,21},{21,... | collective-permute-start | bytes 405512 | tf_op jit(solution)/shard_map/ppermute | solution.py:303
  48.0 19.0 %collective-permute-start.6 = (bf16[64,512]{1,0:T(8,128)(2,1)S(1)}, bf16[64,512]{1,0:T(8,128)(2,1)S(1)}, u32[]{:S(2)}, u32[]{:S(2)}) collective-permute-start(bf16[64,512]{1,0:T(8,128)(2,1)S(1)} %get-tuple-element.15), channel_id=1, source_target_pairs={{0,32},{1,33},{2,34},{3,35},{4,36},{5,37},{6,38},{7,39},{8,40},{9,... | collective-permute-start | bytes 196616 | tf_op jit(solution)/shard_map/ppermute | solution.py:322
  49.9 17.1 %collective-permute-start.7 = (bf16[64,512]{1,0:T(8,128)(2,1)S(1)}, bf16[64,512]{1,0:T(8,128)(2,1)S(1)}, u32[]{:S(2)}, u32[]{:S(2)}) collective-permute-start(bf16[64,512]{1,0:T(8,128)(2,1)S(1)} %get-tuple-element.16), channel_id=1, source_target_pairs={{0,35},{1,32},{2,33},{3,34},{4,39},{5,36},{6,37},{7,38},{8,43},{9,... | collective-permute-start | bytes 196616 | tf_op jit(solution)/shard_map/ppermute | solution.py:322
  63.2 9.8 %collective-permute-start.8 = (bf16[64,512]{1,0:T(8,128)(2,1)S(1)}, bf16[64,512]{1,0:T(8,128)(2,1)S(1)}, u32[]{:S(2)}, u32[]{:S(2)}) collective-permute-start(bf16[64,512]{1,0:T(8,128)(2,1)S(1)} %get-tuple-element.17), channel_id=1, source_target_pairs={{0,34},{1,35},{2,32},{3,33},{4,38},{5,39},{6,36},{7,37},{8,42},{9,... | collective-permute-start | bytes 196616 | tf_op jit(solution)/shard_map/ppermute | solution.py:322
  65.1 8.9 %collective-permute-start.9 = (bf16[64,512]{1,0:T(8,128)(2,1)S(1)}, bf16[64,512]{1,0:T(8,128)(2,1)S(1)}, u32[]{:S(2)}, u32[]{:S(2)}) collective-permute-start(bf16[64,512]{1,0:T(8,128)(2,1)S(1)} %get-tuple-element.18), channel_id=1, source_target_pairs={{0,33},{1,34},{2,35},{3,32},{4,37},{5,38},{6,39},{7,36},{8,41},{9,... | collective-permute-start | bytes 196616 | tf_op jit(solution)/shard_map/ppermute | solution.py:322

commit v9 on v8

--- a/solution.py
+++ b/solution.py
@@ -140,10 +140,25 @@
 def near_kernel(given_ref, *refs, distances, tokens, grouped, scale):
     pair_refs = refs[: len(distances)]
     top_ref, total_ref, mixed_ref = refs[len(distances) :]
-    for turn in range(given_ref.shape[0]):
-        top_ref[turn], total_ref[turn], mixed_ref[turn] = fold(
-            None, distances, pair_refs, pair_refs[0], given_ref, turn, tokens, grouped, scale
-        )
+    block_index = lax.axis_index("blk")
+    levels = sorted(distances) + [lax.axis_size("blk")]
+    for level, above in zip(levels[:-1], levels[1:], strict=True):
+        taken = [which for which, d in enumerate(distances) if d <= level]
+
+        @pl.when((block_index >= level) & (block_index < above))
+        def _(taken=taken):
+            for turn in range(given_ref.shape[0]):
+                top_ref[turn], total_ref[turn], mixed_ref[turn] = fold(
+                    None,
+                    [distances[which] for which in taken],
+                    [pair_refs[which] for which in taken],
+                    pair_refs[0],
+                    given_ref,
+                    turn,
+                    tokens,
+                    grouped,
+                    scale,
+                )
 
 
 def far_kernel(

time: 75.2 us -> 75.2 us (level)
  transfers between devices with their start and end apart: 10 -> 10, of which waited for: 5 -> 5; matrix products, arithmetic and copies ran while one was open for 0% -> 0% of each run, Pallas kernels for 4% -> 3%
where the time goes in v9:
time: 75.2 us; the launch traced here: 74.7 us
  starting transfers between devices  29.9 us (40%)
  blocking collectives  21.8 us (29%)
  waiting for transfers between devices  16.6 us (22%)
  Pallas kernels  6.26 us (8%)
    all_to_all x1, blocking collectives, per_device(): lax.all_to_all(prepared, 'head', split_axis=0, concat_axis=0, tiled=True)  21.8 us
    ppermute x4, starting transfers between devices, per_device(): lax.ppermute(attended[turn], ('section', 'blk', 'head'), route)  19 us
    ppermute x6, starting transfers between devices, per_device(): pairs[d] = lax.ppermute(pairs[held], 'blk', route)  10.9 us
    ppermute x6, waiting for transfers between devices, per_device(): pairs[d] = lax.ppermute(pairs[held], 'blk', route)  9.64 us
    ppermute x4, waiting for transfers between devices, per_device(): lax.ppermute(attended[turn], ('section', 'blk', 'head'), route)  6.96 us
    pallas_call x1, Pallas kernels, call_near(): pl.pallas_call(functools.partial(near_kernel, distances=distances, tokens...  2.46 us
    pallas_call x1, Pallas kernels, call_far(): pl.pallas_call(functools.partial(far_kernel, distances=distances, tokens=...  1.9 us
  transfers between devices with their start and end apart: 10, of which 5 were waited for; matrix products, arithmetic and copies ran while one was open for 0% of the time, Pallas kernels for 3%

profile of v9, /device:TPU:8, one launch (start us, length us, event | category | flops | bytes accessed | tf_op | source)
XLA Modules:
  0.0 74.7 jit_solution(10864539793755477649)
XLA Ops:
  0.0 1.1 %prepare.1 = bf16[4,200,256]{2,1,0:T(8,128)(2,1)S(1)} custom-call(bf16[64,1024]{1,0:T(8,128)(2,1)} %bitcast.4, s32[1,64]{1,0:T(1,128)} %label_ref.1, bf16[64,2048]{1,0:T(8,128)(2,1)} %bitcast.3), custom_call_target="tpu_custom_call" | custom-call | tf_op jit(solution)/shard_map/prepare/pallas_call | solution.py:285
  1.1 21.8 %all_to_all.5.given_ref = bf16[4,200,256]{2,1,0:T(8,128)(2,1)S(1)} all-to-all(bf16[4,200,256]{2,1,0:T(8,128)(2,1)S(1)} %prepare.1), channel_id=1, replica_groups=mesh['section'=32,'blk'=8,'head'=4] {'head'}, dimensions={0} | all-to-all | bytes 819200 | tf_op jit(solution)/shard_map/all_to_all | solution.py:304
  22.9 0.1 pack.1.refs_0_.own_ref
  23.0 2.5 %collective-permute-start = (bf16[264,256]{1,0:T(8,128)(2,1)S(1)}, bf16[264,256]{1,0:T(8,128)(2,1)S(1)}, u32[]{:S(2)}, u32[]{:S(2)}) collective-permute-start(bf16[264,256]{1,0:T(8,128)(2,1)S(1)} %pack.1.refs_0_.own_ref), channel_id=1, source_target_pairs={{0,8},{4,12},{8,16},{12,20},{16,24},{20,28},{1,9},{5,13},{9,17},{1... | collective-permute-start | bytes 405512 | tf_op jit(solution)/shard_map/ppermute | solution.py:318
  25.5 0.7 collective-permute-start.1
  26.2 3.1 %collective-permute-start.2 = (bf16[264,256]{1,0:T(8,128)(2,1)S(1)}, bf16[264,256]{1,0:T(8,128)(2,1)S(1)}, u32[]{:S(2)}, u32[]{:S(2)}) collective-permute-start(bf16[264,256]{1,0:T(8,128)(2,1)S(1)} %pack.1.refs_0_.own_ref), channel_id=1, source_target_pairs={{0,4},{4,8},{8,12},{12,16},{16,20},{20,24},{24,28},{1,5},{5,9},{9,... | collective-permute-start | bytes 405512 | tf_op jit(solution)/shard_map/ppermute | solution.py:318
  29.4 0.7 collective-permute-start.3
  30.0 5.5 %collective-permute-done.refs_1_ = bf16[264,256]{1,0:T(8,128)(2,1)S(1)} collective-permute-done((bf16[264,256]{1,0:T(8,128)(2,1)S(1)}, bf16[264,256]{1,0:T(8,128)(2,1)S(1)}, u32[]{:S(2)}, u32[]{:S(2)}) %collective-permute-start) | collective-permute-done | bytes 135200 | tf_op jit(solution)/shard_map/ppermute | solution.py:318
  35.6 1.9 %collective-permute-start.4 = (bf16[264,256]{1,0:T(8,128)(2,1)S(1)}, bf16[264,256]{1,0:T(8,128)(2,1)S(1)}, u32[]{:S(2)}, u32[]{:S(2)}) collective-permute-start(bf16[264,256]{1,0:T(8,128)(2,1)S(1)} %collective-permute-done.refs_1_), channel_id=1, source_target_pairs={{8,16},{12,20},{16,24},{20,28},{9,17},{13,21},{17,25},{21,29},{10,... | collective-permute-start | bytes 405512 | tf_op jit(solution)/shard_map/ppermute | solution.py:318
  37.5 2.0 %collective-permute-start.5 = (bf16[264,256]{1,0:T(8,128)(2,1)S(1)}, bf16[264,256]{1,0:T(8,128)(2,1)S(1)}, u32[]{:S(2)}, u32[]{:S(2)}) collective-permute-start(bf16[264,256]{1,0:T(8,128)(2,1)S(1)} %collective-permute-done.refs_1_), channel_id=1, source_target_pairs={{8,12},{12,16},{16,20},{20,24},{24,28},{9,13},{13,17},{17,21},{21,... | collective-permute-start | bytes 405512 | tf_op jit(solution)/shard_map/ppermute | solution.py:318
  39.5 0.0 collective-permute-done.1.refs_2_
  39.5 0.0 collective-permute-done.2.refs_3_
  39.5 2.5 %attend_near.1 = (f32[4,1,256]{2,1,0:T(1,128)S(1)}, f32[4,1,256]{2,1,0:T(1,128)S(1)}, f32[4,128,256]{2,1,0:T(8,128)S(1)}) custom-call(bf16[4,200,256]{2,1,0:T(8,128)(2,1)S(1)} %all_to_all.5.given_ref, bf16[264,256]{1,0:T(8,128)(2,1)S(1)} %pack.1.refs_0_.own_ref, bf16[264,256]{1,0:T(8,128)(2,1)S(1)} %collective-permute-done.refs_1_, ...), custom_call_target="tpu_custom_call" | custom-call | flops 536870912 | bytes 2097152 | tf_op jit(solution)/shard_map/attend_near/pallas_call | solution.py:236
  42.0 0.0 collective-permute-done.3.refs_0_
  42.0 2.7 %collective-permute-done.4.refs_1_ = bf16[264,256]{1,0:T(8,128)(2,1)S(1)} collective-permute-done((bf16[264,256]{1,0:T(8,128)(2,1)S(1)}, bf16[264,256]{1,0:T(8,128)(2,1)S(1)}, u32[]{:S(2)}, u32[]{:S(2)}) %collective-permute-start.4) | collective-permute-done | bytes 135200 | tf_op jit(solution)/shard_map/ppermute | solution.py:318
  44.7 1.4 %collective-permute-done.5.refs_2_ = bf16[264,256]{1,0:T(8,128)(2,1)S(1)} collective-permute-done((bf16[264,256]{1,0:T(8,128)(2,1)S(1)}, bf16[264,256]{1,0:T(8,128)(2,1)S(1)}, u32[]{:S(2)}, u32[]{:S(2)}) %collective-permute-start.5) | collective-permute-done | bytes 135200 | tf_op jit(solution)/shard_map/ppermute | solution.py:318
  46.1 1.9 %attend_far.1 = (bf16[64,512]{1,0:T(8,128)(2,1)S(1)}, bf16[64,512]{1,0:T(8,128)(2,1)S(1)}, bf16[64,512]{1,0:T(8,128)(2,1)S(1)}, bf16[64,512]{1,0:T(8,128)(2,1)S(1)}) custom-call(bf16[4,200,256]{2,1,0:T(8,128)(2,1)S(1)} %all_to_all.5.given_ref, bf16[264,256]{1,0:T(8,128)(2,1)S(1)} %pack.1.refs_0_.own_ref, f32[4,1,256]{2,1,0:T(1,128)S(1)} %get-tuple-element.12.top_ref, ...), custom_call_target="tpu_custom_call" | custom-call | flops 402653184 | bytes 1572864 | tf_op jit(solution)/shard_map/attend_far/pallas_call | solution.py:255
  48.0 1.9 %collective-permute-start.6 = (bf16[64,512]{1,0:T(8,128)(2,1)S(1)}, bf16[64,512]{1,0:T(8,128)(2,1)S(1)}, u32[]{:S(2)}, u32[]{:S(2)}) collective-permute-start(bf16[64,512]{1,0:T(8,128)(2,1)S(1)} %get-tuple-element.15), channel_id=1, source_target_pairs={{0,32},{1,33},{2,34},{3,35},{4,36},{5,37},{6,38},{7,39},{8,40},{9,... | collective-permute-start | bytes 196616 | tf_op jit(solution)/shard_map/ppermute | solution.py:337
  49.9 13.2 %collective-permute-start.7 = (bf16[64,512]{1,0:T(8,128)(2,1)S(1)}, bf16[64,512]{1,0:T(8,128)(2,1)S(1)}, u32[]{:S(2)}, u32[]{:S(2)}) collective-permute-start(bf16[64,512]{1,0:T(8,128)(2,1)S(1)} %get-tuple-element.16), channel_id=1, source_target_pairs={{0,35},{1,32},{2,33},{3,34},{4,39},{5,36},{6,37},{7,38},{8,43},{9,... | collective-permute-start | bytes 196616 | tf_op jit(solution)/shard_map/ppermute | solution.py:337
  63.2 1.9 %collective-permute-start.8 = (bf16[64,512]{1,0:T(8,128)(2,1)S(1)}, bf16[64,512]{1,0:T(8,128)(2,1)S(1)}, u32[]{:S(2)}, u32[]{:S(2)}) collective-permute-start(bf16[64,512]{1,0:T(8,128)(2,1)S(1)} %get-tuple-element.17), channel_id=1, source_target_pairs={{0,34},{1,35},{2,32},{3,33},{4,38},{5,39},{6,36},{7,37},{8,42},{9,... | collective-permute-start | bytes 196616 | tf_op jit(solution)/shard_map/ppermute | solution.py:337
  65.1 1.9 %collective-permute-start.9 = (bf16[64,512]{1,0:T(8,128)(2,1)S(1)}, bf16[64,512]{1,0:T(8,128)(2,1)S(1)}, u32[]{:S(2)}, u32[]{:S(2)}) collective-permute-start(bf16[64,512]{1,0:T(8,128)(2,1)S(1)} %get-tuple-element.18), channel_id=1, source_target_pairs={{0,33},{1,34},{2,35},{3,32},{4,37},{5,38},{6,39},{7,36},{8,41},{9,... | collective-permute-start | bytes 196616 | tf_op jit(solution)/shard_map/ppermute | solution.py:337
  67.0 0.0 collective-permute-done.6.refs_0_
  67.0 0.0 collective-permute-done.7.refs_1_
  67.0 5.9 %collective-permute-done.8.refs_2_ = bf16[64,512]{1,0:T(8,128)(2,1)S(1)} collective-permute-done((bf16[64,512]{1,0:T(8,128)(2,1)S(1)}, bf16[64,512]{1,0:T(8,128)(2,1)S(1)}, u32[]{:S(2)}, u32[]{:S(2)}) %collective-permute-start.8) | collective-permute-done | bytes 65568 | tf_op jit(solution)/shard_map/ppermute | solution.py:337
  73.0 1.0 %collective-permute-done.9.refs_3_ = bf16[64,512]{1,0:T(8,128)(2,1)S(1)} collective-permute-done((bf16[64,512]{1,0:T(8,128)(2,1)S(1)}, bf16[64,512]{1,0:T(8,128)(2,1)S(1)}, u32[]{:S(2)}, u32[]{:S(2)}) %collective-permute-start.9) | collective-permute-done | bytes 65568 | tf_op jit(solution)/shard_map/ppermute | solution.py:337
  74.0 0.7 assemble.1
Async XLA Ops:
  23.0 12.6 %collective-permute-start = (bf16[264,256]{1,0:T(8,128)(2,1)S(1)}, bf16[264,256]{1,0:T(8,128)(2,1)S(1)}, u32[]{:S(2)}, u32[]{:S(2)}) collective-permute-start(bf16[264,256]{1,0:T(8,128)(2,1)S(1)} %pack.1.refs_0_.own_ref), channel_id=1, source_target_pairs={{0,8},{4,12},{8,16},{12,20},{16,24},{20,28},{1,9},{5,13},{9,17},{1... | collective-permute-start | bytes 405512 | tf_op jit(solution)/shard_map/ppermute | solution.py:318
  25.5 14.0 %collective-permute-start.1 = (bf16[264,256]{1,0:T(8,128)(2,1)S(1)}, bf16[264,256]{1,0:T(8,128)(2,1)S(1)}, u32[]{:S(2)}, u32[]{:S(2)}) collective-permute-start(bf16[264,256]{1,0:T(8,128)(2,1)S(1)} %pack.1.refs_0_.own_ref), channel_id=1, source_target_pairs={{0,20},{4,24},{8,28},{1,21},{5,25},{9,29},{2,22},{6,26},{10,30},{3... | collective-permute-start | bytes 405512 | tf_op jit(solution)/shard_map/ppermute | solution.py:318
  26.2 13.3 %collective-permute-start.2 = (bf16[264,256]{1,0:T(8,128)(2,1)S(1)}, bf16[264,256]{1,0:T(8,128)(2,1)S(1)}, u32[]{:S(2)}, u32[]{:S(2)}) collective-permute-start(bf16[264,256]{1,0:T(8,128)(2,1)S(1)} %pack.1.refs_0_.own_ref), channel_id=1, source_target_pairs={{0,4},{4,8},{8,12},{12,16},{16,20},{20,24},{24,28},{1,5},{5,9},{9,... | collective-permute-start | bytes 405512 | tf_op jit(solution)/shard_map/ppermute | solution.py:318
  29.4 12.6 %collective-permute-start.3 = (bf16[264,256]{1,0:T(8,128)(2,1)S(1)}, bf16[264,256]{1,0:T(8,128)(2,1)S(1)}, u32[]{:S(2)}, u32[]{:S(2)}) collective-permute-start(bf16[264,256]{1,0:T(8,128)(2,1)S(1)} %pack.1.refs_0_.own_ref), channel_id=1, source_target_pairs={{0,24},{4,28},{1,25},{5,29},{2,26},{6,30},{3,27},{7,31},{32,56},{3... | collective-permute-start | bytes 405512 | tf_op jit(solution)/shard_map/ppermute | solution.py:318
  35.6 9.1 %collective-permute-start.4 = (bf16[264,256]{1,0:T(8,128)(2,1)S(1)}, bf16[264,256]{1,0:T(8,128)(2,1)S(1)}, u32[]{:S(2)}, u32[]{:S(2)}) collective-permute-start(bf16[264,256]{1,0:T(8,128)(2,1)S(1)} %collective-permute-done.refs_1_), channel_id=1, source_target_pairs={{8,16},{12,20},{16,24},{20,28},{9,17},{13,21},{17,25},{21,29},{10,... | collective-permute-start | bytes 405512 | tf_op jit(solution)/shard_map/ppermute | solution.py:318
  37.5 8.6 %collective-permute-start.5 = (bf16[264,256]{1,0:T(8,128)(2,1)S(1)}, bf16[264,256]{1,0:T(8,128)(2,1)S(1)}, u32[]{:S(2)}, u32[]{:S(2)}) collective-permute-start(bf16[264,256]{1,0:T(8,128)(2,1)S(1)} %collective-permute-done.refs_1_), channel_id=1, source_target_pairs={{8,12},{12,16},{16,20},{20,24},{24,28},{9,13},{13,17},{17,21},{21,... | collective-permute-start | bytes 405512 | tf_op jit(solution)/shard_map/ppermute | solution.py:318
  48.0 19.0 %collective-permute-start.6 = (bf16[64,512]{1,0:T(8,128)(2,1)S(1)}, bf16[64,512]{1,0:T(8,128)(2,1)S(1)}, u32[]{:S(2)}, u32[]{:S(2)}) collective-permute-start(bf16[64,512]{1,0:T(8,128)(2,1)S(1)} %get-tuple-element.15), channel_id=1, source_target_pairs={{0,32},{1,33},{2,34},{3,35},{4,36},{5,37},{6,38},{7,39},{8,40},{9,... | collective-permute-start | bytes 196616 | tf_op jit(solution)/shard_map/ppermute | solution.py:337
  49.9 17.1 %collective-permute-start.7 = (bf16[64,512]{1,0:T(8,128)(2,1)S(1)}, bf16[64,512]{1,0:T(8,128)(2,1)S(1)}, u32[]{:S(2)}, u32[]{:S(2)}) collective-permute-start(bf16[64,512]{1,0:T(8,128)(2,1)S(1)} %get-tuple-element.16), channel_id=1, source_target_pairs={{0,35},{1,32},{2,33},{3,34},{4,39},{5,36},{6,37},{7,38},{8,43},{9,... | collective-permute-start | bytes 196616 | tf_op jit(solution)/shard_map/ppermute | solution.py:337
  63.2 9.8 %collective-permute-start.8 = (bf16[64,512]{1,0:T(8,128)(2,1)S(1)}, bf16[64,512]{1,0:T(8,128)(2,1)S(1)}, u32[]{:S(2)}, u32[]{:S(2)}) collective-permute-start(bf16[64,512]{1,0:T(8,128)(2,1)S(1)} %get-tuple-element.17), channel_id=1, source_target_pairs={{0,34},{1,35},{2,32},{3,33},{4,38},{5,39},{6,36},{7,37},{8,42},{9,... | collective-permute-start | bytes 196616 | tf_op jit(solution)/shard_map/ppermute | solution.py:337
  65.1 8.9 %collective-permute-start.9 = (bf16[64,512]{1,0:T(8,128)(2,1)S(1)}, bf16[64,512]{1,0:T(8,128)(2,1)S(1)}, u32[]{:S(2)}, u32[]{:S(2)}) collective-permute-start(bf16[64,512]{1,0:T(8,128)(2,1)S(1)} %get-tuple-element.18), channel_id=1, source_target_pairs={{0,33},{1,34},{2,35},{3,32},{4,37},{5,38},{6,39},{7,36},{8,41},{9,... | collective-permute-start | bytes 196616 | tf_op jit(solution)/shard_map/ppermute | solution.py:337
